TPU v7x, 256 devices: a whole 4x4x8 slice. The times are simulated.
256 devices in a mesh: band: 4 (over x), tile: 64 (over y, z, core).
Axes of the slice: x: 4, y: 4, z: 8, core: 2. Of those that a mesh axis runs over, the one named last changes fastest.
Arguments:
- granules: bfloat16 [1024, 16, 4096], P('tile', 'band'), may hold values from -6 to 6
- valid_rows: int32 [1024, 64], P('tile'), may hold values 0 or 1
- scene_order: int32 [1024], P('tile'), may hold values from 0 to 1023, each once
- intersections: int32 [1024, 4], P('tile'), may hold values from 0 to 63, all different within a row; in each aligned block of 16 rows (0 to 15, 16 to 31, ...) at most 2 rows name the same one
- row_resample: bfloat16 [1024, 4, 4096], P('tile'), may hold values from 0 to 1.4, as said below
- col_resample: bfloat16 [1024, 4, 4096], P('tile'), may hold values from 0 to 1.4, as said below
- w_in: bfloat16 [16, 256], replicated, may hold values from -1.5 to 1.5
- w_hidden: bfloat16 [2, 256, 256], replicated, may hold values from -0.375 to 0.375
- w_out: bfloat16 [256], replicated, may hold values from -1.5 to 1.5
Outputs:
- composite: float32 [16, 262144], P('band', 'tile')
Inputs may be any that keep to these rules, and one draw needn't show every extreme that they name: `intersections`: each scene names 4 different output tiles; the 16 scenes of one device name any one tile at most 2 times, a bound that some block reaches. `scene_order`: each order number appears once. `row_resample`: nonnegative resampling weights. `col_resample`: nonnegative resampling weights.
All inputs are finite; a program needn't handle non-finite values. No bound on the sum of `valid_rows` on one device may be relied on, other than what follows from the above.
Results may differ from a plain program's by a relative error of at most 0.0031.
Values may be sent and summed in bfloat16 or wider, within the bound.
No kernel may reach another device: no remote copies, remote signals or barrier semaphores. Data moves between devices by JAX's collectives and lax.ppermute only.
A program may use at most 128 MiB of HBM per device.

v0:
```python
import jax
import jax.numpy as jnp
from jax import lax
from jax.sharding import PartitionSpec as P

HUBER_ITERS = 4
SMOOTH = 2


prior_weight = 0.25
huber_delta = 0.5
edge_scale = 1.0
smooth_rate = 0.2


def extended_2(block, sides, width):
    for axis, dim in sides:
        count = lax.axis_size(axis)
        forward = [(i, i + 1) for i in range(count - 1)]
        backward = [(target, source) for source, target in forward]
        low = lax.ppermute(
            lax.slice_in_dim(block, block.shape[dim] - width, None, axis=dim), axis, forward
        )
        high = lax.ppermute(lax.slice_in_dim(block, 0, width, axis=dim), axis, backward)
        block = jnp.concatenate([low, block, high], axis=dim)
    return block


def scene_weights(pixels, valid_part, recency, w_in, w_hidden, w_out, side_cells):
    scenes, row_count = valid_part.shape
    valid_pix = jnp.broadcast_to(
        valid_part.astype(jnp.float32)[:, :, None], (scenes, row_count, side_cells)
    )
    valid_pix = valid_pix.reshape(scenes, row_count * side_cells)

    def one_scene(inputs):
        scene_pixels, scene_valid, scene_recency = inputs
        hidden = jax.nn.silu(
            jnp.einsum("cn,ch->nh", scene_pixels, w_in, preferred_element_type=jnp.float32)
        ).astype(jnp.bfloat16)
        for repeat in range(w_hidden.shape[0]):
            hidden = jax.nn.silu(
                jnp.dot(hidden, w_hidden[repeat], preferred_element_type=jnp.float32)
            ).astype(jnp.bfloat16)
        logits = jnp.dot(hidden, w_out, preferred_element_type=jnp.float32)
        return (jax.nn.sigmoid(-logits) * scene_valid * scene_recency).astype(jnp.bfloat16)

    return lax.map(one_scene, (pixels, valid_pix, recency))


def reproject(planes, rows_matrix, cols_matrix):
    half_done = jnp.einsum(
        "ncil,njl->ncij", planes, cols_matrix, preferred_element_type=jnp.float32
    ).astype(jnp.bfloat16)
    return jnp.einsum(
        "nij,ncjl->ncil", rows_matrix, half_done, preferred_element_type=jnp.float32
    ).astype(jnp.bfloat16)


def huber_merge(observed, weights):
    values = observed.astype(jnp.float32)
    plain = weights.astype(jnp.float32)[:, None, :]
    estimate = jnp.sum(plain * values, 0) / (jnp.sum(plain, 0) + prior_weight)
    for repeat in range(HUBER_ITERS):
        residual = values - estimate[None]
        huber_w = plain * huber_delta / jnp.maximum(jnp.abs(residual), huber_delta)
        estimate = jnp.sum(huber_w * values, 0) / (jnp.sum(huber_w, 0) + prior_weight)
    return estimate


def smooth_step(extended, first_col, total_cols):
    positions = first_col + jnp.arange(extended.shape[2] - 1)
    inside = ((positions >= 0) & (positions + 1 < total_cols)).astype(jnp.float32)
    across = extended[:, :, 1:] - extended[:, :, :-1]
    sideways = across / (1.0 + (across / edge_scale) ** 2) * inside
    centre = extended[:, :, 1:-1]
    upward_diff = centre[:, 1:, :] - centre[:, :-1, :]
    upward = upward_diff / (1.0 + (upward_diff / edge_scale) ** 2)
    zeros_row = jnp.zeros_like(upward[:, :1, :])
    vertical = jnp.concatenate([upward, zeros_row], 1) - jnp.concatenate([zeros_row, upward], 1)
    return centre + smooth_rate * (sideways[:, :, 1:] - sideways[:, :, :-1] + vertical)


def per_device(
    granules,
    valid_rows,
    scene_order,
    intersections,
    row_resample,
    col_resample,
    w_in,
    w_hidden,
    w_out,
):
    scenes, group_bands, pixel_count = granules.shape
    side_cells = valid_rows.shape[1]
    intersection_count = intersections.shape[1]
    tile_count = lax.axis_size("tile")
    band_count = lax.axis_size("band")
    recency = jnp.exp(1.4 * scene_order.astype(jnp.float32) / (scenes * tile_count) - 0.7)
    by_rows = lax.all_to_all(granules, "band", split_axis=2, concat_axis=1, tiled=True)
    row_count = side_cells // band_count
    valid_here = lax.dynamic_slice_in_dim(
        valid_rows, lax.axis_index("band") * row_count, row_count, 1
    )
    partial_weights = scene_weights(by_rows, valid_here, recency, w_in, w_hidden, w_out, side_cells)
    weights = lax.all_gather(partial_weights, "band", axis=1, tiled=True)
    plane_count = group_bands + 1
    planes = jnp.concatenate([granules, weights[:, None, :]], 1)
    entry_count = scenes * intersection_count
    capacity = (entry_count + tile_count - 1) // tile_count + 1
    buffer_rows = tile_count * capacity
    flat_dest = intersections.reshape(entry_count)
    onehot = (flat_dest[:, None] == jnp.arange(tile_count, dtype=jnp.int32)[None, :]).astype(
        jnp.int32
    )
    slot_rank = jnp.sum((jnp.cumsum(onehot, 0) - onehot) * onehot, 1)
    slot_index = flat_dest * capacity + slot_rank
    raw_planes = jnp.repeat(planes, intersection_count, axis=0)
    matrices = jnp.stack([row_resample, col_resample], 2).reshape(entry_count, 2, pixel_count)
    raw_out = (
        jnp.zeros((buffer_rows, plane_count, pixel_count), jnp.bfloat16)
        .at[slot_index]
        .set(raw_planes)
    )
    matrix_out = jnp.zeros((buffer_rows, 2, pixel_count), jnp.bfloat16).at[slot_index].set(matrices)
    raw_in, matrix_in = (
        lax.all_to_all(raw_out, "tile", split_axis=0, concat_axis=0, tiled=True),
        lax.all_to_all(matrix_out, "tile", split_axis=0, concat_axis=0, tiled=True),
    )
    matrix_in = matrix_in.reshape(buffer_rows, 2, side_cells, side_cells)
    incoming = reproject(
        raw_in.reshape(buffer_rows, plane_count, side_cells, side_cells),
        matrix_in[:, 0],
        matrix_in[:, 1],
    )
    incoming = incoming.reshape(buffer_rows, plane_count, pixel_count)
    estimate = huber_merge(incoming[:, :group_bands], incoming[:, group_bands])
    field = estimate.reshape(group_bands, side_cells, side_cells)
    first_col = lax.axis_index("tile") * side_cells
    total_cols = tile_count * side_cells
    for repeat in range(SMOOTH):
        extended = extended_2(field, (("tile", 2),), 1)
        field = smooth_step(extended, first_col - 1, total_cols)
    return field.reshape(group_bands, pixel_count)


def solution(mesh):
    return jax.shard_map(
        per_device,
        mesh=mesh,
        in_specs=(
            P("tile", "band", None),
            P("tile", None),
            P("tile"),
            P("tile", None),
            P("tile", None, None),
            P("tile", None, None),
            P(),
            P(),
            P(),
        ),
        out_specs=P("band", "tile"),
        check_vma=False,
    )
```

profile of v0, /device:TPU:1, one launch (start us, length us, event | category | flops | bytes accessed | tf_op | source)
XLA Modules:
  0.0 472.2 jit_solution(6735166915798410247)
XLA Ops:
  0.0 6.5 %copy.57 = bf16[16,4,4096]{0,1,2:T(4,128)(2,1)} copy(bf16[16,4,4096]{2,1,0:T(4,128)(2,1)} %param.11) | data formatting | bytes 1048576 | tf_op args[0]
  6.5 6.5 %reshape.136 = bf16[4,2,32768]{2,1,0:T(2,128)(2,1)} reshape(bf16[4096,4,16]{2,1,0:T(4,128)(2,1)} %bitcast.84) | data formatting | bytes 1048576
  13.0 4.8 %all-to-all-start = ((bf16[4,2,32768]{2,1,0:T(2,128)(2,1)}), bf16[4,2,32768]{2,1,0:T(2,128)(2,1)}, u32[]{:S(2)}, u32[]{:S(2)}) async-start(bf16[4,2,32768]{2,1,0:T(2,128)(2,1)} %reshape.136), calls=%async_computation | async-start | bytes 1048576 | tf_op jit(solution)/shard_map/all_to_all | solution.py:101
  26.3 8.3 %scatter_fusion.1 = bf16[128,2,4096]{2,1,0:T(2,128)(2,1)} fusion(bf16[128,2,4096]{2,1,0:T(2,128)(2,1)} %broadcast_in_dim.40, s32[64]{0:T(128)S(1)} %fusion.59, bf16[64,2,4096]{2,1,0:T(2,128)(2,1)S(1)} %pad_maximum_fusion.1), kind=kCustom, calls=%fused_computation.1 | custom fusion | bytes 3145984 | tf_op jit(solution)/shard_map/scatter | solution.py:126
  34.6 12.6 %all-to-all-start.2 = ((bf16[128,2,4096]{2,1,0:T(2,128)(2,1)}), bf16[128,2,4096]{2,1,0:T(2,128)(2,1)S(1)}, u32[]{:S(2)}, u32[]{:S(2)}) async-start(bf16[128,2,4096]{2,1,0:T(2,128)(2,1)} %scatter_fusion.1), calls=%async_computation.2 | async-start | bytes 4194304 | tf_op jit(solution)/shard_map/all_to_all | solution.py:129
  47.2 5.4 %reshape.137 = bf16[4096,4,16]{2,1,0:T(4,128)(2,1)} reshape(bf16[4,2,32768]{2,1,0:T(2,128)(2,1)} %all-to-all-done) | data formatting | bytes 1048576
  52.5 6.1 %copy.58 = bf16[16,4,4,1024]{3,2,1,0:T(4,128)(2,1)S(1)} copy(bf16[16,4,4,1024]{0,2,3,1:T(4,128)(2,1)} %bitcast.83) | data formatting | bytes 1048576 | tf_op jit(solution)/shard_map/all_to_all | solution.py:101
  58.8 74.0 %while.10 = (s32[]{:T(128)}, bf16[16,1024]{1,0:T(8,128)(2,1)S(1)}, bf16[16,16,1024]{2,1,0:T(8,128)(2,1)S(1)}, bf16[16,256]{1,0:T(8,128)(2,1)S(1)}, bf16[2,256,25...) while((s32[]{:T(128)}, bf16[16,1024]{1,0:T(8,128)(2,1)S(1)}, ...), condition=%wide.region_3.4_spmd, body=%wide.region_2.3_spmd.sunk | while | flops 281285632 | bytes 1384577 | solution.py:48
  132.8 10.0 %all_gather.3 = bf16[16,4096]{1,0:T(8,128)(2,1)S(1)} all-gather(bf16[16,1024]{1,0:T(8,128)(2,1)S(1)} %get-tuple-element.47), channel_id=1, replica_groups=mesh['band'=4,'tile'=64] {'band'}, dimensions={1}, use_global_device_ids=true | all-gather | bytes 163840 | tf_op jit(solution)/shard_map/all_gather | solution.py:107
  145.9 4.3 broadcast_in_dim.16
  150.2 11.9 %scatter_fusion = bf16[128,5,4096]{2,1,0:T(8,128)(2,1)} fusion(bf16[128,5,4096]{2,1,0:T(8,128)(2,1)} %broadcast_in_dim.16, s32[64]{0:T(128)S(1)} %fusion.59, bf16[64,5,4096]{2,1,0:T(8,128)(2,1)} %bitcast.82), kind=kCustom, calls=%fused_computation | custom fusion | bytes 7864576 | tf_op jit(solution)/shard_map/scatter | solution.py:124
  162.1 13.5 %all-to-all-start.1 = ((bf16[128,5,4096]{2,1,0:T(8,128)(2,1)}), bf16[128,5,4096]{2,1,0:T(8,128)(2,1)}, u32[]{:S(2)}, u32[]{:S(2)}) async-start(bf16[128,5,4096]{2,1,0:T(8,128)(2,1)} %scatter_fusion), calls=%async_computation.1 | async-start | bytes 16777216 | tf_op jit(solution)/shard_map/all_to_all | solution.py:128
  175.6 4.0 copy.65
  182.3 3.9 copy.75
  190.1 171.3 %all-to-all-done.1 = bf16[128,5,4096]{2,1,0:T(8,128)(2,1)} async-done(((bf16[128,5,4096]{2,1,0:T(8,128)(2,1)}), bf16[128,5,4096]{2,1,0:T(8,128)(2,1)}, u32[]{:S(2)}, u32[]{:S(2)}) %all-to-all-start.1) | async-done | bytes 5242912 | tf_op jit(solution)/shard_map/all_to_all | solution.py:128
  361.3 10.6 %copy.62 = bf16[128,5,4096]{0,2,1:T(8,128)(2,1)} copy(bf16[128,5,4096]{2,1,0:T(8,128)(2,1)} %all-to-all-done.1) | data formatting | bytes 10485760 | tf_op jit(solution)/shard_map/all_to_all | solution.py:128
  372.0 15.7 %copy.67 = bf16[128,5,64,64]{3,2,1,0:T(8,128)(2,1)} copy(bf16[128,5,64,64]{0,3,2,1:T(8,128)(2,1)} %bitcast.81) | data formatting | bytes 10485760 | tf_op jit(solution)/shard_map/reshape | solution.py:133
  387.7 12.5 %convert_bitcast_fusion = bf16[128,5,64,64]{2,3,1,0:T(8,128)(2,1)} fusion(bf16[128,5,64,64]{3,2,1,0:T(8,128)(2,1)} %copy.67, bf16[128,1,64,64]{3,2,0,1:T(8,128)(2,1)} %copy.76, bf16[128,1,64,64]{3,2,0,1:T(8,128)(2,1)S(1)} %copy.75), kind=kOutput, calls=%fused_computation.29 | convolution fusion | flops 676331520 | bytes 12582912 | tf_op jit(solution)/shard_map/nij,ncjl->ncil/dot_general | solution.py:55
  400.2 18.1 %copy.70 = bf16[128,5,64,64]{0,3,2,1:T(8,128)(2,1)} copy(bf16[128,5,64,64]{2,3,1,0:T(8,128)(2,1)} %convert_bitcast_fusion) | data formatting | bytes 10485760 | tf_op jit(solution)/shard_map/convert_element_type | solution.py:57
  424.1 7.8 %fusion.47 = (f32[4,4096]{1,0:T(4,128)S(1)}, f32[4,4096]{1,0:T(4,128)S(1)}) fusion(f32[4,4096]{1,0:T(4,128)S(1)} %broadcast_divide_fusion, f32[128,4096]{0,1:T(8,128)S(1)} %get-tuple-element.72, bf16[128,5,4096]{0,2,1:T(8,128)(2,1)S(1)} %bitcast.77), kind=kLoop, calls=%fused_computation.53 | loop fusion | flops 16744448 | bytes 6488064 | tf_op jit(solution)/shard_map/reduce_sum | solution.py:67
  431.9 7.6 %fusion.46 = (f32[4,4096]{1,0:T(4,128)S(1)}, f32[4,4096]{1,0:T(4,128)S(1)}) fusion(f32[4,4096]{1,0:T(4,128)S(1)} %add_divide_fusion.5, f32[128,4096]{0,1:T(8,128)S(1)} %get-tuple-element.72, bf16[128,5,4096]{0,2,1:T(8,128)(2,1)S(1)} %bitcast.78), kind=kLoop, calls=%fused_computation.52 | loop fusion | flops 16744448 | bytes 6488064 | tf_op jit(solution)/shard_map/reduce_sum | solution.py:67
  439.6 7.6 %fusion.45 = (f32[4,4096]{1,0:T(4,128)S(1)}, f32[4,4096]{1,0:T(4,128)S(1)}) fusion(f32[4,4096]{1,0:T(4,128)S(1)} %add_divide_fusion.4, f32[128,4096]{0,1:T(8,128)S(1)} %get-tuple-element.72, bf16[128,5,4096]{0,2,1:T(8,128)(2,1)S(1)} %bitcast.79), kind=kLoop, calls=%fused_computation.51 | loop fusion | flops 16744448 | bytes 6488064 | tf_op jit(solution)/shard_map/reduce_sum | solution.py:67
  447.2 7.6 %fusion.44 = (f32[4,4096]{1,0:T(4,128)S(1)}, f32[4,4096]{1,0:T(4,128)S(1)}) fusion(f32[4,4096]{1,0:T(4,128)S(1)} %add_divide_fusion.3, f32[128,4096]{0,1:T(8,128)S(1)} %get-tuple-element.72, bf16[128,5,4096]{0,2,1:T(8,128)(2,1)S(1)} %bitcast.80), kind=kLoop, calls=%fused_computation.50 | loop fusion | flops 16744448 | bytes 6488064 | tf_op jit(solution)/shard_map/reduce_sum | solution.py:67
  464.9 4.4 collective-permute-start.3
  (201 shorter events, 110.3 us)
Async XLA Ops:
  0.0 17.8 %copy-start.4 = (s32[16,4]{0,1:T(4,128)S(1)}, s32[16,4]{0,1:T(4,128)}, u32[]{:S(2)}) copy-start(s32[16,4]{0,1:T(4,128)} %param.14) | copy-start | bytes 772
  0.0 17.9 %copy-start.5 = (s32[16,64]{1,0:T(8,128)S(1)}, s32[16,64]{1,0:T(8,128)}, u32[]{:S(2)}) copy-start(s32[16,64]{1,0:T(8,128)} %param.12) | copy-start | bytes 12292
  0.0 18.8 %copy-start.2 = (bf16[16,4,4096]{2,1,0:T(4,128)(2,1)S(1)}, bf16[16,4,4096]{2,1,0:T(4,128)(2,1)}, u32[]{:S(2)}) copy-start(bf16[16,4,4096]{2,1,0:T(4,128)(2,1)} %param.15) | copy-start | bytes 1572868
  0.0 19.6 %copy-start.3 = (bf16[16,4,4096]{2,1,0:T(4,128)(2,1)S(1)}, bf16[16,4,4096]{2,1,0:T(4,128)(2,1)}, u32[]{:S(2)}) copy-start(bf16[16,4,4096]{2,1,0:T(4,128)(2,1)} %param.16) | copy-start | bytes 1572868
  6.5 28.1 %copy-start.8 = (s32[16]{0:T(128)S(1)}, s32[16]{0:T(128)}, u32[]{:S(2)}) copy-start(s32[16]{0:T(128)} %param.13) | copy-start | bytes 196
  13.0 21.6 %all-to-all-start = ((bf16[4,2,32768]{2,1,0:T(2,128)(2,1)}), bf16[4,2,32768]{2,1,0:T(2,128)(2,1)}, u32[]{:S(2)}, u32[]{:S(2)}) async-start(bf16[4,2,32768]{2,1,0:T(2,128)(2,1)} %reshape.136), calls=%async_computation | async-start | bytes 1048576 | tf_op jit(solution)/shard_map/all_to_all | solution.py:101
  26.3 32.4 %copy-start.6 = (bf16[2,256,256]{2,1,0:T(8,128)(2,1)S(1)}, bf16[2,256,256]{2,1,0:T(8,128)(2,1)}, u32[]{:S(2)}) copy-start(bf16[2,256,256]{2,1,0:T(8,128)(2,1)} %param.18) | copy-start | bytes 786436
  26.3 32.4 %copy-start.7 = (bf16[16,256]{1,0:T(8,128)(2,1)S(1)}, bf16[16,256]{1,0:T(8,128)(2,1)}, u32[]{:S(2)}) copy-start(bf16[16,256]{1,0:T(8,128)(2,1)} %param.17) | copy-start | bytes 24580
  26.3 32.5 %copy-start.9 = (bf16[256]{0:T(256)(128)(2,1)S(1)}, bf16[256]{0:T(256)(128)(2,1)}, u32[]{:S(2)}) copy-start(bf16[256]{0:T(256)(128)(2,1)} %param.19) | copy-start | bytes 1540
  34.6 127.5 %all-to-all-start.2 = ((bf16[128,2,4096]{2,1,0:T(2,128)(2,1)}), bf16[128,2,4096]{2,1,0:T(2,128)(2,1)S(1)}, u32[]{:S(2)}, u32[]{:S(2)}) async-start(bf16[128,2,4096]{2,1,0:T(2,128)(2,1)} %scatter_fusion.1), calls=%async_computation.2 | async-start | bytes 4194304 | tf_op jit(solution)/shard_map/all_to_all | solution.py:129
  58.8 84.2 %copy-start.1 = (bf16[16,4,4096]{2,1,0:T(4,128)(2,1)S(1)}, bf16[16,4,4096]{2,1,0:T(4,128)(2,1)}, u32[]{:S(2)}) copy-start(bf16[16,4,4096]{2,1,0:T(4,128)(2,1)} %param.11) | copy-start | bytes 1572868
  162.1 199.3 %all-to-all-start.1 = ((bf16[128,5,4096]{2,1,0:T(8,128)(2,1)}), bf16[128,5,4096]{2,1,0:T(8,128)(2,1)}, u32[]{:S(2)}, u32[]{:S(2)}) async-start(bf16[128,5,4096]{2,1,0:T(8,128)(2,1)} %scatter_fusion), calls=%async_computation.1 | async-start | bytes 16777216 | tf_op jit(solution)/shard_map/all_to_all | solution.py:128
  418.3 3.4 copy-start
  455.1 6.3 %collective-permute-start = (f32[4,64,1]{2,1,0:T(8,128)S(1)}, f32[4,64,1]{2,1,0:T(8,128)S(1)}, u32[]{:S(2)}, u32[]{:S(2)}) collective-permute-start(f32[4,64,1]{2,1,0:T(8,128)S(1)} %get-tuple-element.78), channel_id=1, source_target_pairs={{1,0},{2,1},{3,2},{4,3},{5,4},{6,5},{7,6},{8,7},{9,8},{10,9},{11,1... | collective-permute-start | bytes 3080 | tf_op jit(solution)/shard_map/ppermute | solution.py:24
  457.0 5.6 %collective-permute-start.1 = (f32[4,64,1]{2,1,0:T(8,128)S(1)}, f32[4,64,1]{2,1,0:T(8,128)S(1)}, u32[]{:S(2)}, u32[]{:S(2)}) collective-permute-start(f32[4,64,1]{2,1,0:T(8,128)S(1)} %get-tuple-element.79), channel_id=1, source_target_pairs={{0,1},{1,2},{2,3},{3,4},{4,5},{5,6},{6,7},{7,8},{8,9},{9,10},{10,1... | collective-permute-start | bytes 3080 | tf_op jit(solution)/shard_map/ppermute | solution.py:21
  462.9 7.0 %collective-permute-start.2 = (f32[4,64,1]{2,1,0:T(8,128)S(1)}, f32[4,64,1]{2,1,0:T(8,128)S(1)}, u32[]{:S(2)}, u32[]{:S(2)}) collective-permute-start(f32[4,64,1]{2,1,0:T(8,128)S(1)} %get-tuple-element.76), channel_id=1, source_target_pairs={{1,0},{2,1},{3,2},{4,3},{5,4},{6,5},{7,6},{8,7},{9,8},{10,9},{11,1... | collective-permute-start | bytes 3080 | tf_op jit(solution)/shard_map/ppermute | solution.py:24
  464.9 6.3 %collective-permute-start.3 = (f32[4,64,1]{2,1,0:T(8,128)S(1)}, f32[4,64,1]{2,1,0:T(8,128)S(1)}, u32[]{:S(2)}, u32[]{:S(2)}) collective-permute-start(f32[4,64,1]{2,1,0:T(8,128)S(1)} %get-tuple-element.77), channel_id=1, source_target_pairs={{0,1},{1,2},{2,3},{3,4},{4,5},{5,6},{6,7},{7,8},{8,9},{9,10},{10,1... | collective-permute-start | bytes 3080 | tf_op jit(solution)/shard_map/ppermute | solution.py:21
where the time goes:
time: 477 us; the launch traced here: 472 us
  waiting for transfers between devices  175 us (37%)
  local copies, waits for them, and re-layouts  129 us (27%)
  matrix products  62.6 us (13%)
  other arithmetic  51.6 us (11%)
  starting transfers between devices  42.7 us (9%)
  blocking collectives  9.97 us (2%)
    all_to_all x1, waiting for transfers between devices, per_device(): lax.all_to_all(raw_out, 'tile', split_axis=0, concat_axis=0, tiled=True)  171 us
    reduce_sum x4, other arithmetic, huber_merge(): jnp.sum(huber_w, 0) + prior_weight  30.6 us
    unnamed x26, local copies, waits for them, and re-layouts  26.2 us
    dot_general x16, matrix products, one_scene(): logits = jnp.dot(hidden, w_out, preferred_element_type=jnp.float32)  25.4 us
    dot_general x16, matrix products, one_scene(): jnp.dot(hidden, w_hidden[repeat], preferred_element_type=jnp.float32)  24.6 us
    convert_element_type x1, local copies, waits for them, and re-layouts, reproject(): return jnp.einsum('nij,ncjl->ncil', rows_matrix, half_done, preferred_ele...  18.1 us
    reshape x1, local copies, waits for them, and re-layouts, per_device(): raw_in.reshape(buffer_rows, plane_count, side_cells, side_cells)  15.7 us
    all_to_all x1, starting transfers between devices, per_device(): lax.all_to_all(raw_out, 'tile', split_axis=0, concat_axis=0, tiled=True)  13.5 us
  transfers between devices with their start and end apart: 7, of which 5 were waited for; matrix products, arithmetic and copies ran while one was open for 29% of the time, Pallas kernels for 0%

commit v1 on v0

v1 whole, which is shorter than its diff:
```python
import jax
import jax.numpy as jnp
import numpy as np
from jax import lax
from jax.experimental import pallas as pl
from jax.experimental.pallas import tpu as pltpu
from jax.sharding import PartitionSpec as P

HUBER_ITERS = 4
SMOOTH = 2

prior_weight = 0.25
huber_delta = 0.5
smooth_rate = 0.2

F32 = jnp.float32
BF16 = jnp.bfloat16
SIDE = 64


def dot(a, b, contract=((1,), (0,))):
    return lax.dot_general(a, b, (contract, ((), ())), preferred_element_type=F32)


def spread_matrix(count):
    out = np.zeros((count * SIDE, count * SIDE // 2), np.float32)
    for a in range(count):
        for i in range(SIDE):
            out[a * SIDE + i, count * (i // 2) + a] = 1.0
    return out


def parity_mask(rows):
    row = lax.broadcasted_iota(jnp.int32, (rows, 128), 0)
    lane = lax.broadcasted_iota(jnp.int32, (rows, 128), 1)
    return (row & 1) == (lane >> 6)


def spread_pair(both, mask):
    col = jnp.where(mask, both[:, :128], 0.0)
    col = (col + pltpu.roll(col, 64, 1)).astype(BF16)
    row = jnp.where(mask, both[:, 128:], 0.0).astype(BF16)
    return col, row


def reproject_kernel(x_ref, col_ref, row_ref, spread_ref, out_ref, scratch):
    mask = parity_mask(256)
    spread = spread_ref[...]
    for s in range(4):
        x = dot(spread, x_ref[s])
        x = jnp.where(mask, x, 0.0).astype(BF16)
        both = dot(spread, jnp.concatenate([col_ref[s], row_ref[s]], 1))
        col, row = spread_pair(both, mask)
        half = dot(x, col, ((1,), (1,)))
        for k in range(4):
            lanes = slice(k * SIDE, (k + 1) * SIDE)
            part = jnp.concatenate([half[c * SIDE : (c + 1) * SIDE, lanes] for c in range(4)], 1)
            part = part.astype(BF16)
            part = jnp.concatenate([part, part], 0)
            moved = dot(row[k * SIDE : (k + 1) * SIDE], part)
            for v in range(2):
                scratch[v, pl.ds(4 * s + k, SIDE, stride=16), :] = moved[:, v * 128 : (v + 1) * 128]
    for v in range(2):
        out_ref[:, :, v * 128 : (v + 1) * 128] = scratch[v].reshape(SIDE, 16, 128).astype(BF16)


def weight_kernel(w_ref, col_ref, row_ref, spread_ref, spread1_ref, out_ref, scratch):
    step = pl.program_id(0)
    mask = parity_mask(256)
    mask1 = parity_mask(SIDE)
    spread = spread_ref[...]
    spread1 = spread1_ref[...]
    for s in range(4):
        w = dot(spread1, w_ref[s])
        w = jnp.where(mask1, w, 0.0).astype(BF16)
        both = dot(spread, jnp.concatenate([col_ref[s], row_ref[s]], 1))
        col, row = spread_pair(both, mask)
        half = dot(w, col, ((1,), (1,)))
        parts = []
        for k in range(4):
            part = half[:, k * SIDE : (k + 1) * SIDE].astype(BF16)
            part = jnp.concatenate([part, part], 0)
            parts.append(dot(row[k * SIDE : (k + 1) * SIDE], part))
        for v in range(2):
            scratch[v, pl.ds(4 * step + s, SIDE, stride=16), :] = jnp.concatenate(
                parts[2 * v : 2 * v + 2], 1
            )

    @pl.when(step == 3)
    def _():
        for v in range(2):
            out_ref[:, :, v * 128 : (v + 1) * 128] = scratch[v].reshape(SIDE, 16, 128).astype(BF16)


def cloud_kernel(x_ref, factor_ref, w_in_ref, w_hidden_ref, w_out_ref, out_ref):
    def silu_of_twice(u):
        return (u + u * jnp.tanh(u)).astype(BF16)

    x = jnp.concatenate([x_ref[b, 0] for b in range(4)], 0)
    hidden = silu_of_twice(dot(w_in_ref[...], x))
    for layer in range(2):
        hidden = silu_of_twice(dot(w_hidden_ref[layer], hidden))
    logits = dot(w_out_ref[...], hidden)[:1]
    out_ref[0] = (factor_ref[0] / (1.0 + jnp.exp(logits))).astype(BF16)


def merge_kernel(y_ref, w_ref, id_ref, out_ref, pick, pick_t, weight):
    entries = y_ref.shape[0]
    chunk = 512
    chunks = entries // chunk
    lane = lax.broadcasted_iota(jnp.int32, (chunk // 4, 128), 1)
    for i in range(chunks):
        span = slice(i * chunk, (i + 1) * chunk)
        tile = lax.broadcasted_iota(jnp.int32, (128, chunk), 0) & 63
        hit = jnp.where(id_ref[:, span] == tile, 1.0, 0.0)
        pick[:, span] = hit[:SIDE].astype(BF16)
        pick_t[span, :] = hit.T.astype(BF16)
        rows = slice(i * chunk // 4, (i + 1) * chunk // 4)
        for v in range(2):
            w = w_ref[rows, v * 128 : (v + 1) * 128].astype(F32)
            turned = pltpu.roll(w, 64, 1)
            weight[pl.ds(i * chunk + 2 * v, chunk // 4, stride=4), :] = jnp.where(lane < 64, w, turned)
            weight[pl.ds(i * chunk + 2 * v + 1, chunk // 4, stride=4), :] = jnp.where(
                lane < 64, turned, w
            )

    def totals(estimate, exact):
        top = bottom = 0.0
        if estimate is not None:
            high = estimate.astype(BF16)
            low = (estimate - high.astype(F32)).astype(BF16)
            stacked = jnp.concatenate([high, low], 0)
        for i in range(chunks):
            span = slice(i * chunk, (i + 1) * chunk)
            y = y_ref[span, :].astype(F32)
            w = weight[span, :]
            h = jnp.concatenate([w, w], 1)
            if estimate is not None:
                residual = y - dot(pick_t[span, :], stacked)
                h = h * huber_delta / jnp.maximum(jnp.abs(residual), huber_delta)
            hy = h * y
            picked = pick[:, span]
            h_high, hy_high = h.astype(BF16), hy.astype(BF16)
            top = top + dot(picked, hy_high)
            bottom = bottom + dot(picked, h_high)
            if exact:
                top = top + dot(picked, (hy - hy_high.astype(F32)).astype(BF16))
                bottom = bottom + dot(picked, (h - h_high.astype(F32)).astype(BF16))
        return top / (bottom + prior_weight)

    estimate = totals(None, False)
    estimate = lax.fori_loop(0, HUBER_ITERS - 1, lambda _, e: totals(e, False), estimate)
    estimate = totals(estimate, True)

    lane = lax.broadcasted_iota(jnp.int32, (SIDE, 128), 1)
    for v in range(2):
        own = estimate[:, v * 128 : (v + 1) * 128]
        turned = pltpu.roll(own, 64, 1)
        for odd in range(2):
            first, second = (turned, own) if odd else (own, turned)
            after = pltpu.roll(second, SIDE - 1, 0)
            before = pltpu.roll(second, 1, 0)
            out_ref[:, 2 * v + odd, :] = jnp.where(
                lane < 64, first, jnp.where(lane < 96, after, before)
            )


def smooth_kernel(tile_ref, g_ref, out_ref):
    first = tile_ref[0] == 0
    last = tile_ref[0] == tile_ref[1] - 1
    lane = lax.broadcasted_iota(jnp.int32, (SIDE, 128), 1)
    row = lax.broadcasted_iota(jnp.int32, (SIDE, 128), 0)
    closed = ((lane == 127) & first) | ((lane == SIDE - 1) & last)
    bottom = row == SIDE - 1

    def flux(d):
        return d / (1.0 + d * d)

    for c in range(4):
        g = g_ref[:, c, :]
        for repeat in range(SMOOTH):
            across = jnp.where(closed, 0.0, flux(pltpu.roll(g, 127, 1) - g))
            down = jnp.where(bottom, 0.0, flux(pltpu.roll(g, SIDE - 1, 0) - g))
            g = g + smooth_rate * (
                across - pltpu.roll(across, 1, 1) + (down - pltpu.roll(down, 1, 0))
            )
        out_ref[c] = g[:, :SIDE]


def two_rows_per_line(x):
    scenes, planes, _ = x.shape
    x = x.reshape(scenes, planes, SIDE // 2, 128)
    return x.transpose(0, 2, 1, 3).reshape(scenes, planes * SIDE // 2, 128)


def whole(shape):
    return pl.BlockSpec(shape, lambda *_: (0,) * len(shape))


def per_device(
    granules,
    valid_rows,
    scene_order,
    intersections,
    row_resample,
    col_resample,
    w_in,
    w_hidden,
    w_out,
):
    scenes, bands, pixels = granules.shape
    tiles = lax.axis_size("tile")
    groups = lax.axis_size("band")
    share = scenes // groups
    spread = jnp.asarray(spread_matrix(4), BF16)
    spread1 = jnp.asarray(spread_matrix(1), BF16)

    by_scene = lax.all_to_all(
        granules.reshape(groups, share, bands, pixels), "band", split_axis=0, concat_axis=0
    )

    cols = two_rows_per_line(col_resample)
    rows = two_rows_per_line(row_resample)
    scene_block = pl.BlockSpec((4, 128, 128), lambda i: (i, 0, 0))
    moved = pl.pallas_call(
        reproject_kernel,
        grid=(4,),
        in_specs=[scene_block, scene_block, scene_block, whole((256, 128))],
        out_specs=pl.BlockSpec((SIDE, 16, 256), lambda i: (0, i, 0)),
        out_shape=jax.ShapeDtypeStruct((SIDE, 64, 256), BF16),
        scratch_shapes=[pltpu.VMEM((2, SIDE * 16, 128), F32)],
        name="reproject",
    )(two_rows_per_line(granules), cols, rows, spread)
    values = lax.all_to_all(moved, "tile", split_axis=0, concat_axis=0)

    ids = jnp.broadcast_to(intersections.reshape(1, 1, scenes * 4), (tiles, 1, scenes * 4))
    ids = lax.all_to_all(ids, "tile", split_axis=0, concat_axis=0).reshape(1, tiles * scenes * 4)

    first_scene = lax.axis_index("band") * share
    recency = jnp.exp(1.4 * scene_order.astype(F32) / (scenes * tiles) - 0.7)
    factor = valid_rows.astype(F32) * recency[:, None]
    factor = lax.dynamic_slice_in_dim(factor, first_scene, share, 0)
    factor = jnp.broadcast_to(factor[:, :, None], (share, SIDE, SIDE)).reshape(share, 1, pixels)
    half = jnp.asarray(0.5, BF16)
    width = 2048
    weights = pl.pallas_call(
        cloud_kernel,
        grid=(share, pixels // width),
        in_specs=[
            pl.BlockSpec((groups, 1, bands, width), lambda s, i: (0, s, 0, i)),
            pl.BlockSpec((1, 1, width), lambda s, i: (s, 0, i)),
            whole((256, 16)),
            whole((2, 256, 256)),
            whole((8, 256)),
        ],
        out_specs=pl.BlockSpec((1, 1, width), lambda s, i: (s, 0, i)),
        out_shape=jax.ShapeDtypeStruct((share, 1, pixels), BF16),
        name="cloud",
    )(
        by_scene,
        factor,
        w_in.T * half,
        w_hidden.transpose(0, 2, 1) * half,
        jnp.broadcast_to(w_out[None, :], (8, 256)),
    )
    weights = weights.reshape(1, share * SIDE // 2, 128)
    weights = lax.all_to_all(
        jnp.broadcast_to(weights, (groups,) + weights.shape[1:]), "band", split_axis=0, concat_axis=0
    ).reshape(scenes, SIDE // 2, 128)
    moved_weights = pl.pallas_call(
        weight_kernel,
        grid=(4,),
        in_specs=[
            pl.BlockSpec((4, SIDE // 2, 128), lambda i: (i, 0, 0)),
            scene_block,
            scene_block,
            whole((256, 128)),
            whole((SIDE, SIDE // 2)),
        ],
        out_specs=whole((SIDE, scenes, 256)),
        out_shape=jax.ShapeDtypeStruct((SIDE, scenes, 256), BF16),
        scratch_shapes=[pltpu.VMEM((2, SIDE * 16, 128), F32)],
        name="reproject_weights",
    )(weights, cols, rows, spread, spread1)
    moved_weights = lax.all_to_all(moved_weights, "tile", split_axis=0, concat_axis=0)

    entries = tiles * scenes * 4
    estimate = pl.pallas_call(
        merge_kernel,
        out_shape=jax.ShapeDtypeStruct((tiles, 4, 128), F32),
        scratch_shapes=[
            pltpu.VMEM((SIDE, entries), BF16),
            pltpu.VMEM((entries, 128), BF16),
            pltpu.VMEM((entries, 128), F32),
        ],
        name="merge",
    )(values.reshape(entries, 256), moved_weights.reshape(tiles * scenes, 256), ids)
    field = lax.all_to_all(estimate, "tile", split_axis=0, concat_axis=0)

    place = jnp.stack([lax.axis_index("tile"), tiles]).astype(jnp.int32)
    out = pl.pallas_call(
        smooth_kernel,
        in_specs=[pl.BlockSpec(memory_space=pltpu.SMEM), whole((SIDE, 4, 128))],
        out_specs=whole((4, SIDE, SIDE)),
        out_shape=jax.ShapeDtypeStruct((4, SIDE, SIDE), F32),
        name="smooth",
    )(place, field)
    return out.reshape(4, pixels)


def solution(mesh):
    return jax.shard_map(
        per_device,
        mesh=mesh,
        in_specs=(
            P("tile", "band", None),
            P("tile", None),
            P("tile"),
            P("tile", None),
            P("tile", None, None),
            P("tile", None, None),
            P(),
            P(),
            P(),
        ),
        out_specs=P("band", "tile"),
        check_vma=False,
    )
```

time: 477 us -> 185 us (0.39)
  local copies, waits for them, and re-layouts: 129 us -> 10.7 us
  waiting for transfers between devices: 175 us -> 69.9 us
  matrix products: 62.6 us -> 0 us
  Pallas kernels: 0 us -> 51.5 us
  other arithmetic: 51.6 us -> 5.21 us
  blocking collectives: 9.97 us -> 0 us
    all_to_all x3 -> x6, waiting for transfers between devices: 171 us -> 69.9 us  [the longest x1 49.3 us: per_device(): values = lax.all_to_all(moved, 'tile', split_axis=0, concat_axis=0)]
    dot_general x33 -> x0, matrix products: 62.6 us -> none  [the longest x16 25.4 us: one_scene(): logits = jnp.dot(hidden, w_out, preferred_element_type=jnp.float32)]
    pallas_call x0 -> x5, Pallas kernels: none -> 51.5 us  [the longest x1 14.9 us: per_device(): pl.pallas_call(merge_kernel, out_shape=jax.ShapeDtypeStruct((tiles, 4, 12...]
    reduce_sum x6 -> x0, other arithmetic: 33 us -> none  [the longest x4 30.6 us: huber_merge(): jnp.sum(huber_w, 0) + prior_weight]
    unnamed x26 -> x16, local copies, waits for them, and re-layouts: 26.2 us -> 4.12 us
    all_to_all x4 -> x1, local copies, waits for them, and re-layouts: 20.9 us -> 0.51 us  [per_device(): lax.all_to_all(ids, 'tile', split_axis=0, concat_axis=0)]
    scatter x2 -> x0, local copies, waits for them, and re-layouts: 20.1 us -> none  [the longest x1 11.9 us: per_device(): raw_out = jnp.zeros((buffer_rows, plane_count, pixel_count), jnp.bfloat16...]
    convert_element_type x1 -> x0, local copies, waits for them, and re-layouts: 18.1 us -> none  [reproject(): return jnp.einsum('nij,ncjl->ncil', rows_matrix, half_done, preferred_ele...]
  transfers between devices with their start and end apart: 7 -> 6, of which waited for: 5 -> 5; matrix products, arithmetic and copies ran while one was open for 29% -> 5% of each run, Pallas kernels for 0% -> 13%
where the time goes in v1:
time: 185 us; the launch traced here: 184 us
  waiting for transfers between devices  69.9 us (38%)
  Pallas kernels  51.5 us (28%)
  starting transfers between devices  46.6 us (25%)
  local copies, waits for them, and re-layouts  10.7 us (6%)
  other arithmetic  5.21 us (3%)
    all_to_all x1, waiting for transfers between devices, per_device(): values = lax.all_to_all(moved, 'tile', split_axis=0, concat_axis=0)  49.3 us
    all_to_all x1, starting transfers between devices, per_device(): lax.all_to_all(ids, 'tile', split_axis=0, concat_axis=0)  15.9 us
    pallas_call x1, Pallas kernels, per_device(): pl.pallas_call(merge_kernel, out_shape=jax.ShapeDtypeStruct((tiles, 4, 12...  14.9 us
    pallas_call x1, Pallas kernels, per_device(): pl.pallas_call(reproject_kernel, grid=(4,), in_specs=[scene_block, scene_...  12.9 us
    pallas_call x1, Pallas kernels, per_device(): pl.pallas_call(cloud_kernel, grid=(share, pixels // width), in_specs=[pl....  11.1 us
    pallas_call x1, Pallas kernels, per_device(): pl.pallas_call(weight_kernel, grid=(4,), in_specs=[pl.BlockSpec((4, SIDE...  10.8 us
    all_to_all x1, starting transfers between devices, per_device(): lax.all_to_all(moved_weights, 'tile', split_axis=0, concat_axis=0)  10.3 us
    all_to_all x1, waiting for transfers between devices, per_device(): field = lax.all_to_all(estimate, 'tile', split_axis=0, concat_axis=0)  9.75 us
  transfers between devices with their start and end apart: 6, of which 5 were waited for; matrix products, arithmetic and copies ran while one was open for 5% of the time, Pallas kernels for 13%

profile of v1, /device:TPU:1, one launch (start us, length us, event | category | flops | bytes accessed | tf_op | source)
XLA Modules:
  0.0 184.0 jit_solution(16856821996690610925)
XLA Ops:
  0.0 5.0 %all-to-all-start.1 = ((bf16[4,4,4,4096]{3,2,1,0:T(4,128)(2,1)}), bf16[4,4,4,4096]{3,2,1,0:T(4,128)(2,1)S(1)}, u32[]{:S(2)}, u32[]{:S(2)}) async-start(bf16[4,4,4,4096]{3,2,1,0:T(4,128)(2,1)} %bitcast.28), calls=%async_computation.1 | async-start | bytes 1048576 | tf_op jit(solution)/shard_map/all_to_all | solution.py:218
  5.7 0.8 fusion
  6.6 0.8 reshape.56.factor_ref
  8.8 1.1 copy.37
  9.8 0.7 multiply_bitcast_fusion.w_hidden_ref
  10.6 1.8 all-to-all-done.1.x_ref
  13.1 11.1 %cloud.1 = bf16[4,1,4096]{2,1,0:T(2,128)(2,1)} custom-call(bf16[4,4,4,4096]{3,2,1,0:T(4,128)(2,1)} %copy-done.1, f32[4,1,4096]{2,1,0:T(1,128)} %reshape.56.factor_ref, bf16[256,16]{1,0:T(8,128)(2,1)} %bitcast.32, bf16[2,256,256]{2,1,0:T(8,128)(2,1)} %multiply_bitcast_fusion.w_hidden_ref, bf16[8,256]{1,0:T(8,128)(2,1)} %broadcast_in_dim.13.w_out_ref), custom_call_target="tpu_custom_call" | custom-call | tf_op jit(solution)/shard_map/cloud/pallas_call | solution.py:246
  24.2 1.0 reduce
  26.0 3.3 %all-to-all-start.2 = ((bf16[4,128,128]{2,1,0:T(8,128)(2,1)}), bf16[4,128,128]{2,1,0:T(8,128)(2,1)S(1)}, u32[]{:S(2)}, u32[]{:S(2)}) async-start(bf16[4,128,128]{2,1,0:T(8,128)(2,1)} %broadcast_in_dim.30), calls=%async_computation.2 | async-start | bytes 262144 | tf_op jit(solution)/shard_map/all_to_all | solution.py:267
  29.5 4.6 %all-to-all-done.2 = bf16[4,128,128]{2,1,0:T(8,128)(2,1)S(1)} async-done(((bf16[4,128,128]{2,1,0:T(8,128)(2,1)}), bf16[4,128,128]{2,1,0:T(8,128)(2,1)S(1)}, u32[]{:S(2)}, u32[]{:S(2)}) %all-to-all-start.2) | async-done | bytes 131104 | tf_op jit(solution)/shard_map/all_to_all | solution.py:267
  34.7 15.9 %all-to-all-start.4 = ((s32[64,1,64]{2,1,0:T(1,128)}), s32[64,1,64]{2,1,0:T(1,128)S(1)}, u32[]{:S(2)}, u32[]{:S(2)}) async-start(s32[64,1,64]{2,1,0:T(1,128)} %broadcast_in_dim.32), calls=%async_computation.4 | async-start | bytes 65536 | tf_op jit(solution)/shard_map/all_to_all | solution.py:237
  50.6 10.8 %reproject_weights.1 = bf16[64,16,256]{2,1,0:T(8,128)(2,1)} custom-call(bf16[16,32,128]{2,1,0:T(8,128)(2,1)} %bitcast.31, bf16[16,128,128]{2,1,0:T(8,128)(2,1)} %bitcast.24, bf16[16,128,128]{2,1,0:T(8,128)(2,1)} %bitcast.26, bf16[256,128]{1,0:T(8,128)(2,1)} %constant.32.clone.spread_ref, bf16[64,32]{1,0:T(8,128)(2,1)} %constant.33.clone.spread1_ref), custom_call_target="tpu_custom_call" | custom-call | tf_op jit(solution)/shard_map/reproject_weights/pallas_call | solution.py:270
  61.4 10.3 %all-to-all-start.3 = ((bf16[64,16,256]{2,1,0:T(8,128)(2,1)}), bf16[64,16,256]{2,1,0:T(8,128)(2,1)S(1)}, u32[]{:S(2)}, u32[]{:S(2)}) async-start(bf16[64,16,256]{2,1,0:T(8,128)(2,1)} %reproject_weights.1), calls=%async_computation.3 | async-start | bytes 1048576 | tf_op jit(solution)/shard_map/all_to_all | solution.py:285
  71.7 12.9 %reproject.1 = bf16[64,64,256]{2,1,0:T(8,128)(2,1)} custom-call(bf16[16,128,128]{2,1,0:T(8,128)(2,1)} %bitcast.29, bf16[16,128,128]{2,1,0:T(8,128)(2,1)} %bitcast.25, bf16[16,128,128]{2,1,0:T(8,128)(2,1)} %bitcast.27, bf16[256,128]{1,0:T(8,128)(2,1)} %constant.32.clone.spread_ref), custom_call_target="tpu_custom_call" | custom-call | tf_op jit(solution)/shard_map/reproject/pallas_call | solution.py:225
  84.6 4.5 %all-to-all-done.3 = bf16[64,16,256]{2,1,0:T(8,128)(2,1)S(1)} async-done(((bf16[64,16,256]{2,1,0:T(8,128)(2,1)}), bf16[64,16,256]{2,1,0:T(8,128)(2,1)S(1)}, u32[]{:S(2)}, u32[]{:S(2)}) %all-to-all-start.3) | async-done | bytes 524320 | tf_op jit(solution)/shard_map/all_to_all | solution.py:285
  89.1 0.8 copy-done.2
  89.9 6.3 %all-to-all-start = ((bf16[64,64,256]{2,1,0:T(8,128)(2,1)}), bf16[64,64,256]{2,1,0:T(8,128)(2,1)S(1)}, u32[]{:S(2)}, u32[]{:S(2)}) async-start(bf16[64,64,256]{2,1,0:T(8,128)(2,1)} %reproject.1), calls=%async_computation | async-start | bytes 4194304 | tf_op jit(solution)/shard_map/all_to_all | solution.py:234
  98.1 49.3 %all-to-all-done = bf16[64,64,256]{2,1,0:T(8,128)(2,1)S(1)} async-done(((bf16[64,64,256]{2,1,0:T(8,128)(2,1)}), bf16[64,64,256]{2,1,0:T(8,128)(2,1)S(1)}, u32[]{:S(2)}, u32[]{:S(2)}) %all-to-all-start) | async-done | bytes 2097184 | tf_op jit(solution)/shard_map/all_to_all | solution.py:234
  147.4 1.3 copy-done
  148.7 14.9 %merge.1 = f32[64,4,128]{2,1,0:T(4,128)} custom-call(bf16[4096,256]{1,0:T(8,128)(2,1)} %bitcast.23, bf16[1024,256]{1,0:T(8,128)(2,1)} %bitcast.30, s32[1,4096]{1,0:T(1,128)} %reshape.59.id_ref), custom_call_target="tpu_custom_call" | custom-call | tf_op jit(solution)/shard_map/merge/pallas_call | solution.py:288
  163.6 5.8 %all-to-all-start.5 = ((f32[64,4,128]{2,1,0:T(4,128)}), f32[64,4,128]{2,1,0:T(4,128)S(1)}, u32[]{:S(2)}, u32[]{:S(2)}) async-start(f32[64,4,128]{2,1,0:T(4,128)} %merge.1), calls=%async_computation.5 | async-start | bytes 262144 | tf_op jit(solution)/shard_map/all_to_all | solution.py:298
  170.0 9.8 %all-to-all-done.5.g_ref = f32[64,4,128]{2,1,0:T(4,128)S(1)} async-done(((f32[64,4,128]{2,1,0:T(4,128)}), f32[64,4,128]{2,1,0:T(4,128)S(1)}, u32[]{:S(2)}, u32[]{:S(2)}) %all-to-all-start.5) | async-done | bytes 131104 | tf_op jit(solution)/shard_map/all_to_all | solution.py:298
  180.4 1.9 %smooth.1 = f32[4,64,64]{2,1,0:T(8,128)} custom-call(s32[2]{0:T(128)} %pad_add_fusion.tile_ref, f32[64,4,128]{2,1,0:T(4,128)} %copy-done.4), custom_call_target="tpu_custom_call" | custom-call | tf_op jit(solution)/shard_map/smooth/pallas_call | solution.py:301
  182.4 1.6 reshape.60
  (28 shorter events, 7.8 us)
Async XLA Ops:
  0.0 12.4 %copy-start.6 = (bf16[256]{0:T(256)(128)(2,1)S(1)}, bf16[256]{0:T(256)(128)(2,1)}, u32[]{:S(2)}) copy-start(bf16[256]{0:T(256)(128)(2,1)} %param.19) | copy-start | bytes 1540
  0.0 29.3 %copy-start.5 = (s32[16,4]{0,1:T(4,128)S(1)}, s32[16,4]{0,1:T(4,128)}, u32[]{:S(2)}) copy-start(s32[16,4]{0,1:T(4,128)} %param.14) | copy-start | bytes 772
  0.0 12.3 %all-to-all-start.1 = ((bf16[4,4,4,4096]{3,2,1,0:T(4,128)(2,1)}), bf16[4,4,4,4096]{3,2,1,0:T(4,128)(2,1)S(1)}, u32[]{:S(2)}, u32[]{:S(2)}) async-start(bf16[4,4,4,4096]{3,2,1,0:T(4,128)(2,1)} %bitcast.28), calls=%async_computation.1 | async-start | bytes 1048576 | tf_op jit(solution)/shard_map/all_to_all | solution.py:218
  12.4 0.8 copy-start.1
  26.0 8.1 %all-to-all-start.2 = ((bf16[4,128,128]{2,1,0:T(8,128)(2,1)}), bf16[4,128,128]{2,1,0:T(8,128)(2,1)S(1)}, u32[]{:S(2)}, u32[]{:S(2)}) async-start(bf16[4,128,128]{2,1,0:T(8,128)(2,1)} %broadcast_in_dim.30), calls=%async_computation.2 | async-start | bytes 262144 | tf_op jit(solution)/shard_map/all_to_all | solution.py:267
  34.1 16.5 %copy-start.3 = (bf16[4,128,128]{2,1,0:T(8,128)(2,1)}, bf16[4,128,128]{2,1,0:T(8,128)(2,1)S(1)}, u32[]{:S(2)}) copy-start(bf16[4,128,128]{2,1,0:T(8,128)(2,1)S(1)} %all-to-all-done.2) | copy-start | bytes 393220
  34.7 26.7 %all-to-all-start.4 = ((s32[64,1,64]{2,1,0:T(1,128)}), s32[64,1,64]{2,1,0:T(1,128)S(1)}, u32[]{:S(2)}, u32[]{:S(2)}) async-start(s32[64,1,64]{2,1,0:T(1,128)} %broadcast_in_dim.32), calls=%async_computation.4 | async-start | bytes 65536 | tf_op jit(solution)/shard_map/all_to_all | solution.py:237
  61.4 27.7 %all-to-all-start.3 = ((bf16[64,16,256]{2,1,0:T(8,128)(2,1)}), bf16[64,16,256]{2,1,0:T(8,128)(2,1)S(1)}, u32[]{:S(2)}, u32[]{:S(2)}) async-start(bf16[64,16,256]{2,1,0:T(8,128)(2,1)} %reproject_weights.1), calls=%async_computation.3 | async-start | bytes 1048576 | tf_op jit(solution)/shard_map/all_to_all | solution.py:285
  89.1 0.8 copy-start.2
  89.9 57.5 %all-to-all-start = ((bf16[64,64,256]{2,1,0:T(8,128)(2,1)}), bf16[64,64,256]{2,1,0:T(8,128)(2,1)S(1)}, u32[]{:S(2)}, u32[]{:S(2)}) async-start(bf16[64,64,256]{2,1,0:T(8,128)(2,1)} %reproject.1), calls=%async_computation | async-start | bytes 4194304 | tf_op jit(solution)/shard_map/all_to_all | solution.py:234
  147.4 1.3 copy-start
  163.6 16.2 %all-to-all-start.5 = ((f32[64,4,128]{2,1,0:T(4,128)}), f32[64,4,128]{2,1,0:T(4,128)S(1)}, u32[]{:S(2)}, u32[]{:S(2)}) async-start(f32[64,4,128]{2,1,0:T(4,128)} %merge.1), calls=%async_computation.5 | async-start | bytes 262144 | tf_op jit(solution)/shard_map/all_to_all | solution.py:298
  179.8 0.7 copy-start.4

commit v2 on v1

v2 whole, which is shorter than its diff:
```python
import jax
import jax.numpy as jnp
import numpy as np
from jax import lax
from jax.experimental import pallas as pl
from jax.experimental.pallas import tpu as pltpu
from jax.sharding import PartitionSpec as P

HUBER_ITERS = 4
SMOOTH = 2

prior_weight = 0.25
huber_delta = 0.5
smooth_rate = 0.2

F32 = jnp.float32
BF16 = jnp.bfloat16
SIDE = 64


def dot(a, b, contract=((1,), (0,))):
    return lax.dot_general(a, b, (contract, ((), ())), preferred_element_type=F32)


def spread_matrix(count):
    out = np.zeros((count * SIDE, count * SIDE // 2), np.float32)
    for a in range(count):
        for i in range(SIDE):
            out[a * SIDE + i, count * (i // 2) + a] = 1.0
    return out


def parity_mask(rows):
    row = lax.broadcasted_iota(jnp.int32, (rows, 128), 0)
    lane = lax.broadcasted_iota(jnp.int32, (rows, 128), 1)
    return (row & 1) == (lane >> 6)


def spread_pair(both, mask):
    col = jnp.where(mask, both[:, :128], 0.0)
    col = (col + pltpu.roll(col, 64, 1)).astype(BF16)
    row = jnp.where(mask, both[:, 128:], 0.0).astype(BF16)
    return col, row


def reproject_kernel(x_ref, col_ref, row_ref, spread_ref, out_ref, scratch):
    mask = parity_mask(256)
    spread = spread_ref[...]
    group = range(4)
    wide = [jnp.concatenate([x_ref[s], col_ref[s], row_ref[s]], 1) for s in group]
    wide = [dot(spread, w) for w in wide]
    planes = [jnp.where(mask, w[:, :128], 0.0).astype(BF16) for w in wide]
    pairs = [spread_pair(w[:, 128:], mask) for w in wide]
    halves = [dot(planes[s], pairs[s][0], ((1,), (1,))) for s in group]
    for s in group:
        for k in range(4):
            lanes = slice(k * SIDE, (k + 1) * SIDE)
            part = [halves[s][c * SIDE : (c + 1) * SIDE, lanes] for c in range(4)]
            part = jnp.concatenate(part, 1).astype(BF16)
            part = jnp.concatenate([part, part], 0)
            moved = dot(pairs[s][1][k * SIDE : (k + 1) * SIDE], part)
            for v in range(2):
                scratch[v, pl.ds(4 * k + s, SIDE, stride=16), :] = moved[:, v * 128 : (v + 1) * 128]
    for v in range(2):
        out_ref[:, :, v * 128 : (v + 1) * 128] = scratch[v].reshape(SIDE, 16, 128).astype(BF16)


def weight_kernel(
    band_ref, w_ref, id_ref, col_ref, row_ref, spread_ref, spread1_ref, out_ref, scratch
):
    mask = parity_mask(256)
    mask1 = parity_mask(SIDE)
    spread = spread_ref[...]
    spread1 = spread1_ref[...]
    group = range(4)
    planes = [jnp.where(mask1, dot(spread1, w_ref[s]), 0.0).astype(BF16) for s in group]
    wide = [dot(spread, jnp.concatenate([col_ref[s], row_ref[s]], 1)) for s in group]
    pairs = [spread_pair(w, mask) for w in wide]
    halves = [dot(planes[s], pairs[s][0], ((1,), (1,))) for s in group]
    for s in group:
        parts = []
        for k in range(4):
            part = halves[s][:, k * SIDE : (k + 1) * SIDE].astype(BF16)
            part = jnp.concatenate([part, part], 0)
            parts.append(dot(pairs[s][1][k * SIDE : (k + 1) * SIDE], part))
        for v in range(2):
            pair = jnp.concatenate(parts[2 * v : 2 * v + 2], 1)
            scratch[v, pl.ds(s, SIDE, stride=4), :] = pair
    for v in range(2):
        out_ref[:, v] = scratch[v].reshape(SIDE, 4, 128).astype(BF16)
    out_ref[:, 2] = jnp.broadcast_to(id_ref[...].astype(BF16)[None], (SIDE, 4, 128))


def cloud_kernel(x0, x1, x2, x3, factor_ref, w_in_ref, w_hidden_ref, w_out_ref, out_ref):
    def silu_of_twice(u):
        return (u + u * jnp.tanh(u)).astype(BF16)

    scene, width = pl.program_id(0), factor_ref.shape[2]
    lanes = pl.ds(pl.multiple_of(pl.program_id(1) * width, width), width)
    x = jnp.concatenate([x_ref[scene, :, lanes] for x_ref in (x0, x1, x2, x3)], 0)
    hidden = silu_of_twice(dot(w_in_ref[...], x))
    for layer in range(2):
        hidden = silu_of_twice(dot(w_hidden_ref[layer], hidden))
    logits = dot(w_out_ref[...], hidden)[:1]
    weight = factor_ref[0] / (1.0 + jnp.exp(logits))
    lines = [weight[:, i * 128 : (i + 1) * 128] for i in range(weight.shape[1] // 128)]
    out_ref[0] = jnp.concatenate(lines, 0).astype(BF16)


def merge_kernel(y_ref, w_ref, out_ref, pick, pick_t, weight):
    entries = y_ref.shape[0]
    chunk = 512
    chunks = entries // chunk
    lane = lax.broadcasted_iota(jnp.int32, (entries // SIDE, 128), 1)
    tile = (lax.broadcasted_iota(jnp.int32, (128, 128), 0) & 63).astype(F32)
    ids = w_ref[0, :, 2].astype(F32)[:, 0, :]
    turned = pltpu.roll(ids, 64, 1)
    for i in range(entries // 128):
        span = slice(i * 128, (i + 1) * 128)
        pair = jnp.where(lane[:1] < 64, ids[2 * i : 2 * i + 1], turned[2 * i + 1 : 2 * i + 2])
        hit = jnp.where(pair == tile, 1.0, 0.0)
        pick[:, span] = hit[:SIDE].astype(BF16)
        pick_t[span, :] = hit.T.astype(BF16)
    lane = lax.broadcasted_iota(jnp.int32, (entries // SIDE, 4, 128), 2)
    for b in range(4):
        for v in range(2):
            w = w_ref[b, :, v].astype(F32) * huber_delta
            turned = pltpu.roll(w, 64, 2)
            first = 16 * b + 8 * v
            weight[:, first : first + 4, :] = jnp.where(lane < 64, w, turned)
            weight[:, first + 4 : first + 8, :] = jnp.where(lane < 64, turned, w)

    def totals(estimate, exact):
        top = bottom = 0.0
        if estimate is not None:
            high = estimate.astype(BF16)
            low = (estimate - high.astype(F32)).astype(BF16)
            stacked = jnp.concatenate([high, low], 0)
        for i in range(chunks):
            span = slice(i * chunk, (i + 1) * chunk)
            y = y_ref[span, :].astype(F32)
            w = weight[i * chunk // SIDE : (i + 1) * chunk // SIDE].reshape(chunk, 128)
            if estimate is None:
                h = jnp.concatenate([w, w], 1) * (1.0 / huber_delta)
            else:
                residual = y - dot(pick_t[span, :], stacked)
                h = jnp.concatenate([w, w], 1) / jnp.maximum(jnp.abs(residual), huber_delta)
            hy = h * y
            picked = pick[:, span]
            h_high, hy_high = h.astype(BF16), hy.astype(BF16)
            top = top + dot(picked, hy_high)
            bottom = bottom + dot(picked, h_high)
            if exact:
                top = top + dot(picked, (hy - hy_high.astype(F32)).astype(BF16))
                bottom = bottom + dot(picked, (h - h_high.astype(F32)).astype(BF16))
        return top / (bottom + prior_weight)

    estimate = totals(None, False)
    estimate = lax.fori_loop(0, HUBER_ITERS - 1, lambda _, e: totals(e, False), estimate)
    estimate = totals(estimate, True)

    lane = lax.broadcasted_iota(jnp.int32, (SIDE, 128), 1)
    for v in range(2):
        own = estimate[:, v * 128 : (v + 1) * 128]
        turned = pltpu.roll(own, 64, 1)
        for odd in range(2):
            first, second = (turned, own) if odd else (own, turned)
            after = pltpu.roll(second, SIDE - 1, 0)
            before = pltpu.roll(second, 1, 0)
            out_ref[:, 2 * v + odd, :] = jnp.where(
                lane < 64, first, jnp.where(lane < 96, after, before)
            )


def smooth_kernel(tile_ref, g_ref, out_ref, scratch):
    first = tile_ref[0] == 0
    last = tile_ref[0] == tile_ref[1] - 1
    lane = lax.broadcasted_iota(jnp.int32, (SIDE, 128), 1)
    row = lax.broadcasted_iota(jnp.int32, (SIDE, 128), 0)
    closed = ((lane == 127) & first) | ((lane == SIDE - 1) & last)
    bottom = row == SIDE - 1

    def flux(d):
        return d / (1.0 + d * d)

    for c in range(4):
        g = g_ref[:, c, :]
        for repeat in range(SMOOTH):
            across = jnp.where(closed, 0.0, flux(pltpu.roll(g, 127, 1) - g))
            down = jnp.where(bottom, 0.0, flux(pltpu.roll(g, SIDE - 1, 0) - g))
            g = g + smooth_rate * (
                across - pltpu.roll(across, 1, 1) + (down - pltpu.roll(down, 1, 0))
            )
        scratch[c] = g
        even = scratch[c, pl.ds(0, SIDE // 2, stride=2), :]
        odd = scratch[c, pl.ds(1, SIDE // 2, stride=2), :]
        out_ref[:, c, :] = jnp.where(lane[: SIDE // 2] < SIDE, even, pltpu.roll(odd, SIDE, 1))


def two_rows_per_line(x):
    scenes, planes, _ = x.shape
    x = x.reshape(scenes, planes, SIDE // 2, 128)
    return x.transpose(0, 2, 1, 3).reshape(scenes, planes * SIDE // 2, 128)


def keep(x):
    return pltpu.with_memory_space_constraint(x, pltpu.VMEM)


def whole(shape):
    return pl.BlockSpec(shape, lambda *_: (0,) * len(shape))


def per_device(
    granules,
    valid_rows,
    scene_order,
    intersections,
    row_resample,
    col_resample,
    w_in,
    w_hidden,
    w_out,
):
    scenes, bands, pixels = granules.shape
    tiles = lax.axis_size("tile")
    groups = lax.axis_size("band")
    share = scenes // groups
    spread = jnp.asarray(spread_matrix(4), BF16)
    spread1 = jnp.asarray(spread_matrix(1), BF16)

    in_vmem = pl.BlockSpec(memory_space=pltpu.VMEM)
    cols = two_rows_per_line(col_resample)
    rows = two_rows_per_line(row_resample)
    scene_block = pl.BlockSpec((4, 128, 128), lambda i: (i, 0, 0))
    moved = pl.pallas_call(
        reproject_kernel,
        grid=(4,),
        in_specs=[scene_block, scene_block, scene_block, whole((256, 128))],
        out_specs=pl.BlockSpec((SIDE, 16, 256), lambda i: (0, i, 0)),
        out_shape=jax.ShapeDtypeStruct((SIDE, 64, 256), BF16),
        scratch_shapes=[pltpu.VMEM((2, SIDE * 16, 128), F32)],
        name="reproject",
    )(two_rows_per_line(granules), cols, rows, spread)
    moved, granules = lax.optimization_barrier((moved, granules))
    values = lax.all_to_all(moved, "tile", split_axis=0, concat_axis=0)

    band = lax.axis_index("band")
    by_group = granules.reshape(groups, share, bands, pixels)
    w_in = w_in.reshape(groups, bands, -1)
    layers, w_rows = [], []
    for turn in range(groups):
        part = lax.dynamic_index_in_dim(by_group, (band + turn) % groups, 0, keepdims=False)
        if turn:
            part = lax.ppermute(part, "band", [(i, (i + turn) % groups) for i in range(groups)])
        layers.append(part)
        w_rows.append(lax.dynamic_index_in_dim(w_in, (band - turn) % groups, 0, keepdims=False))
    w_in = jnp.concatenate(w_rows, 0)

    first_scene = band * share
    recency = jnp.exp(1.4 * scene_order.astype(F32) / (scenes * tiles) - 0.7)
    factor = valid_rows.astype(F32) * recency[:, None]
    factor = lax.dynamic_slice_in_dim(factor, first_scene, share, 0)
    factor = jnp.broadcast_to(factor[:, :, None], (share, SIDE, SIDE)).reshape(share, 1, pixels)
    half = jnp.asarray(0.5, BF16)
    width = 2048
    weights = pl.pallas_call(
        cloud_kernel,
        grid=(share, pixels // width),
        in_specs=[in_vmem] * groups
        + [
            pl.BlockSpec((1, 1, width), lambda s, i: (s, 0, i)),
            whole((256, 16)),
            whole((2, 256, 256)),
            whole((8, 256)),
        ],
        out_specs=pl.BlockSpec((1, width // 128, 128), lambda s, i: (s, i, 0)),
        out_shape=jax.ShapeDtypeStruct((share, SIDE // 2, 128), BF16),
        cost_estimate=pl.CostEstimate(flops=12 * 10**9, transcendentals=0, bytes_accessed=10**6),
        name="cloud",
    )(
        *map(keep, layers),
        factor,
        w_in.T * half,
        w_hidden.transpose(0, 2, 1) * half,
        jnp.broadcast_to(w_out[None, :], (8, 256)),
    )
    ids = intersections.reshape(groups, share, 4).transpose(0, 2, 1).reshape(1, scenes * 4)
    ids = jnp.broadcast_to(jnp.pad(ids, ((0, 0), (0, 128 - scenes * 4))).astype(F32), (4, 128))
    mine = pl.BlockSpec((4, 128, 128), lambda i, b: (b[0], 0, 0))
    moved_weights = pl.pallas_call(
        weight_kernel,
        grid_spec=pltpu.PrefetchScalarGridSpec(
            num_scalar_prefetch=1,
            grid=(1,),
            in_specs=[
                whole((share, SIDE // 2, 128)),
                whole((4, 128)),
                mine,
                mine,
                whole((256, 128)),
                whole((SIDE, SIDE // 2)),
            ],
            out_specs=whole((SIDE, 3, share, 128)),
            scratch_shapes=[pltpu.VMEM((2, SIDE * share, 128), F32)],
        ),
        out_shape=jax.ShapeDtypeStruct((SIDE, 3, share, 128), BF16),
        name="reproject_weights",
    )(band.astype(jnp.int32).reshape(1), weights, ids, cols, rows, spread, spread1)
    moved_weights, values = lax.optimization_barrier((moved_weights, values))
    moved_weights = lax.all_to_all(moved_weights, "tile", split_axis=0, concat_axis=0)
    moved_weights = jnp.broadcast_to(moved_weights[None], (groups,) + moved_weights.shape)
    moved_weights = lax.all_to_all(moved_weights, "band", split_axis=0, concat_axis=0)

    entries = tiles * scenes * 4
    estimate = pl.pallas_call(
        merge_kernel,
        in_specs=[in_vmem, in_vmem],
        out_shape=jax.ShapeDtypeStruct((tiles, 4, 128), F32),
        scratch_shapes=[
            pltpu.VMEM((SIDE, entries), BF16),
            pltpu.VMEM((entries, 128), BF16),
            pltpu.VMEM((tiles, SIDE, 128), F32),
        ],
        name="merge",
    )(keep(values.reshape(entries, 256)), keep(moved_weights))
    field = lax.all_to_all(estimate, "tile", split_axis=0, concat_axis=0)

    place = jnp.stack([lax.axis_index("tile"), tiles]).astype(jnp.int32)
    out = pl.pallas_call(
        smooth_kernel,
        in_specs=[pl.BlockSpec(memory_space=pltpu.SMEM), in_vmem],
        out_shape=jax.ShapeDtypeStruct((SIDE // 2, 4, 128), F32),
        scratch_shapes=[pltpu.VMEM((4, SIDE, 128), F32)],
        name="smooth",
    )(place, keep(field))
    return out.transpose(1, 0, 2).reshape(4, pixels)


def solution(mesh):
    return jax.shard_map(
        per_device,
        mesh=mesh,
        in_specs=(
            P("tile", "band", None),
            P("tile", None),
            P("tile"),
            P("tile", None),
            P("tile", None, None),
            P("tile", None, None),
            P(),
            P(),
            P(),
        ),
        out_specs=P("band", "tile"),
        check_vma=False,
    )
```

time: 185 us -> 138 us (0.75)
  waiting for transfers between devices: 69.9 us -> 36.8 us
  blocking collectives: 0 us -> 32.7 us
  starting transfers between devices: 46.6 us -> 24.6 us
  Pallas kernels: 51.5 us -> 35 us
  local copies, waits for them, and re-layouts: 10.7 us -> 4.95 us
  other arithmetic: 5.21 us -> 2.82 us
    all_to_all x4 -> x0, starting transfers between devices: 34.5 us -> none  [the longest x1 15.9 us: per_device(): lax.all_to_all(ids, 'tile', split_axis=0, concat_axis=0)]
    all_to_all x0 -> x2, blocking collectives: none -> 32.7 us  [the longest x1 16.7 us: per_device(): lax.all_to_all(moved_weights, 'tile', split_axis=0, concat_axis=0)]
    all_to_all x1, waiting for transfers between devices: 49.3 us -> 26.5 us  [per_device(): values = lax.all_to_all(moved, 'tile', split_axis=0, concat_axis=0)]
    all_to_all x4 -> x0, waiting for transfers between devices: 10.9 us -> none  [the longest x1 4.61 us: per_device(): lax.all_to_all(jnp.broadcast_to(weights, (groups,) + weights.shape[1:]),...]
    pallas_call x3, Pallas kernels: 36.7 us -> 26.6 us  [the longest x1 13.1 us: per_device(): pl.pallas_call(merge_kernel, in_specs=[in_vmem, in_vmem], out_shape=jax.S...]
    all_to_all x1, starting transfers between devices: 6.29 us -> 13.3 us  [per_device(): values = lax.all_to_all(moved, 'tile', split_axis=0, concat_axis=0)]
    pallas_call x1, Pallas kernels: 12.9 us -> 6.65 us  [per_device(): pl.pallas_call(reproject_kernel, grid=(4,), in_specs=[scene_block, scene_...]
    ppermute x0 -> x3, starting transfers between devices: none -> 4.89 us  [per_device(): lax.ppermute(part, 'band', [(i, (i + turn) % groups) for i in range(group...]
  transfers between devices with their start and end apart: 6 -> 5, of which waited for: 5 -> 3; matrix products, arithmetic and copies ran while one was open for 5% -> 5% of each run, Pallas kernels for 13% -> 10%
where the time goes in v2:
time: 138 us; the launch traced here: 137 us
  waiting for transfers between devices  36.8 us (27%)
  Pallas kernels  35 us (25%)
  blocking collectives  32.7 us (24%)
  starting transfers between devices  24.6 us (18%)
  local copies, waits for them, and re-layouts  4.95 us (4%)
  other arithmetic  2.82 us (2%)
    all_to_all x1, waiting for transfers between devices, per_device(): values = lax.all_to_all(moved, 'tile', split_axis=0, concat_axis=0)  26.5 us
    all_to_all x1, blocking collectives, per_device(): lax.all_to_all(moved_weights, 'tile', split_axis=0, concat_axis=0)  16.7 us
    all_to_all x1, blocking collectives, per_device(): lax.all_to_all(moved_weights, 'band', split_axis=0, concat_axis=0)  15.9 us
    all_to_all x1, starting transfers between devices, per_device(): values = lax.all_to_all(moved, 'tile', split_axis=0, concat_axis=0)  13.3 us
    pallas_call x1, Pallas kernels, per_device(): pl.pallas_call(merge_kernel, in_specs=[in_vmem, in_vmem], out_shape=jax.S...  13.1 us
    pallas_call x1, Pallas kernels, per_device(): pl.pallas_call(cloud_kernel, grid=(share, pixels // width), in_specs=[in_...  11 us
    all_to_all x1, waiting for transfers between devices, per_device(): field = lax.all_to_all(estimate, 'tile', split_axis=0, concat_axis=0)  9.71 us
    pallas_call x1, Pallas kernels, per_device(): pl.pallas_call(reproject_kernel, grid=(4,), in_specs=[scene_block, scene_...  6.65 us
  transfers between devices with their start and end apart: 5, of which 3 were waited for; matrix products, arithmetic and copies ran while one was open for 5% of the time, Pallas kernels for 10%

profile of v2, /device:TPU:1, one launch (start us, length us, event | category | flops | bytes accessed | tf_op | source)
XLA Modules:
  0.0 137.1 jit_solution(4165313722118358343)
XLA Ops:
  0.0 6.7 %reproject.1 = bf16[64,64,256]{2,1,0:T(8,128)(2,1)} custom-call(bf16[16,128,128]{2,1,0:T(8,128)(2,1)} %bitcast.47, bf16[16,128,128]{2,1,0:T(8,128)(2,1)} %bitcast.49, bf16[16,128,128]{2,1,0:T(8,128)(2,1)} %bitcast.51, bf16[256,128]{1,0:T(8,128)(2,1)} %constant.99.clone.spread_ref), custom_call_target="tpu_custom_call" | custom-call | tf_op jit(solution)/shard_map/reproject/pallas_call | solution.py:236
  6.7 13.3 %all-to-all-start = ((bf16[64,64,256]{2,1,0:T(8,128)(2,1)}), bf16[64,64,256]{2,1,0:T(8,128)(2,1)S(1)}, u32[]{:S(2)}, u32[]{:S(2)}) async-start(bf16[64,64,256]{2,1,0:T(8,128)(2,1)} %reproject.1), calls=%async_computation | async-start | bytes 4194304 | tf_op jit(solution)/shard_map/all_to_all | solution.py:246
  20.3 1.3 collective-permute-start
  21.6 2.5 %collective-permute-start.1 = (bf16[4,4,4096]{2,1,0:T(4,128)(2,1)S(1)}, bf16[4,4,4096]{2,1,0:T(4,128)(2,1)S(1)}, u32[]{:S(2)}, u32[]{:S(2)}) collective-permute-start(bf16[4,4,4096]{2,1,0:T(4,128)(2,1)S(1)} %get-tuple-element.14), channel_id=1, source_target_pairs={{0,128},{64,192},{128,0},{192,64},{1,129},{65,193},{129,1},{193,65... | collective-permute-start | bytes 393224 | tf_op jit(solution)/shard_map/ppermute | solution.py:255
  24.0 1.1 collective-permute-start.2
  25.4 0.7 add_exponential_fusion
  26.1 0.8 fusion.1
  26.9 0.7 multiply_bitcast_fusion.w_hidden_ref
  27.6 0.7 copy.31
  28.4 0.8 reshape.54.factor_ref
  29.4 0.6 collective-permute-done.1.x2
  30.0 0.6 broadcast_in_dim.11.w_out_ref
  30.6 11.0 %cloud.1.w_ref = bf16[4,32,128]{2,1,0:T(8,128)(2,1)} custom-call(bf16[4,4,4096]{2,1,0:T(4,128)(2,1)S(1)} %get-tuple-element.16.x0, bf16[4,4,4096]{2,1,0:T(4,128)(2,1)S(1)} %collective-permute-done.x1, bf16[4,4,4096]{2,1,0:T(4,128)(2,1)S(1)} %collective-permute-done.1.x2, bf16[4,4,4096]{2,1,0:T(4,128)(2,1)S(1)} %collective-permute-done.2.x3, ...), custom_call_target="tpu_custom_call" | custom-call | flops 12000000000 | bytes 1000000 | tf_op jit(solution)/shard_map/cloud/pallas_call | solution.py:267
  41.6 0.6 broadcast_in_dim.13.id_ref
  42.1 2.5 %reproject_weights.1 = bf16[64,3,4,128]{3,2,1,0:T(4,128)(2,1)} custom-call(s32[1]{0:T(128)} %bitcast.1.band_ref, bf16[4,32,128]{2,1,0:T(8,128)(2,1)} %cloud.1.w_ref, f32[4,128]{1,0:T(4,128)} %broadcast_in_dim.13.id_ref, bf16[16,128,128]{2,1,0:T(8,128)(2,1)} %bitcast.50, bf16[16,128,128]{2,1,0:T(8,128)(2,1)} %bitcast.52, ...), custom_call_target="tpu_custom_call" | custom-call | tf_op jit(solution)/shard_map/reproject_weights/pallas_call | solution.py:291
  44.7 26.5 %all-to-all-done = bf16[64,64,256]{2,1,0:T(8,128)(2,1)S(1)} async-done(((bf16[64,64,256]{2,1,0:T(8,128)(2,1)}), bf16[64,64,256]{2,1,0:T(8,128)(2,1)S(1)}, u32[]{:S(2)}, u32[]{:S(2)}) %all-to-all-start) | async-done | bytes 2097184 | tf_op jit(solution)/shard_map/all_to_all | solution.py:246
  71.2 1.3 copy-done
  72.6 16.7 %all_to_all.20 = bf16[64,3,4,128]{3,2,1,0:T(4,128)(2,1)S(1)} all-to-all(bf16[64,3,4,128]{3,2,1,0:T(4,128)(2,1)} %reproject_weights.1), channel_id=1, replica_groups=mesh['band'=4,'tile'=64] {'tile'}, dimensions={0} | all-to-all | bytes 393216 | tf_op jit(solution)/shard_map/all_to_all | solution.py:311
  89.5 15.9 %all_to_all.21.w_ref = bf16[4,64,3,4,128]{4,3,2,1,0:T(4,128)(2,1)S(1)} all-to-all(bf16[4,64,3,4,128]{4,3,2,1,0:T(4,128)(2,1)S(1)} %broadcast_in_dim.14), channel_id=1, replica_groups=mesh['band'=4,'tile'=64] {'band'}, dimensions={0} | all-to-all | bytes 1572864 | tf_op jit(solution)/shard_map/all_to_all | solution.py:313
  105.4 13.1 %merge.1 = f32[64,4,128]{2,1,0:T(4,128)} custom-call(bf16[4096,256]{1,0:T(8,128)(2,1)S(1)} %bitcast.46, bf16[4,64,3,4,128]{4,3,2,1,0:T(4,128)(2,1)S(1)} %all_to_all.21.w_ref), custom_call_target="tpu_custom_call" | custom-call | tf_op jit(solution)/shard_map/merge/pallas_call | solution.py:316
  118.5 6.4 %all-to-all-start.3 = ((f32[64,4,128]{2,1,0:T(4,128)}), f32[64,4,128]{2,1,0:T(4,128)S(1)}, u32[]{:S(2)}, u32[]{:S(2)}) async-start(f32[64,4,128]{2,1,0:T(4,128)} %merge.1), calls=%async_computation.3 | async-start | bytes 262144 | tf_op jit(solution)/shard_map/all_to_all | solution.py:327
  125.0 0.7 pad_add_fusion.tile_ref
  125.6 9.7 %all-to-all-done.3.g_ref = f32[64,4,128]{2,1,0:T(4,128)S(1)} async-done(((f32[64,4,128]{2,1,0:T(4,128)}), f32[64,4,128]{2,1,0:T(4,128)S(1)}, u32[]{:S(2)}, u32[]{:S(2)}) %all-to-all-start.3) | async-done | bytes 131104 | tf_op jit(solution)/shard_map/all_to_all | solution.py:327
  135.3 1.8 %smooth.1 = f32[32,4,128]{2,1,0:T(4,128)} custom-call(s32[2]{0:T(128)} %pad_add_fusion.tile_ref, f32[64,4,128]{2,1,0:T(4,128)S(1)} %all-to-all-done.3.g_ref), custom_call_target="tpu_custom_call" | custom-call | tf_op jit(solution)/shard_map/smooth/pallas_call | solution.py:330
  (27 shorter events, 1.0 us)
Async XLA Ops:
  6.7 13.4 %copy-start.2 = (bf16[16,4,4096]{2,1,0:T(4,128)(2,1)S(1)}, bf16[16,4,4096]{2,1,0:T(4,128)(2,1)}, u32[]{:S(2)}) copy-start(bf16[16,4,4096]{2,1,0:T(4,128)(2,1)} %param.11) | copy-start | bytes 1572868
  6.7 18.5 %copy-start.4 = (bf16[16,256]{1,0:T(8,128)(2,1)S(1)}, bf16[16,256]{1,0:T(8,128)(2,1)}, u32[]{:S(2)}) copy-start(bf16[16,256]{1,0:T(8,128)(2,1)} %param.17) | copy-start | bytes 24580
  6.7 18.5 %copy-start.3 = (bf16[2,256,256]{2,1,0:T(8,128)(2,1)S(1)}, bf16[2,256,256]{2,1,0:T(8,128)(2,1)}, u32[]{:S(2)}) copy-start(bf16[2,256,256]{2,1,0:T(8,128)(2,1)} %param.18) | copy-start | bytes 786436
  6.7 64.6 %all-to-all-start = ((bf16[64,64,256]{2,1,0:T(8,128)(2,1)}), bf16[64,64,256]{2,1,0:T(8,128)(2,1)S(1)}, u32[]{:S(2)}, u32[]{:S(2)}) async-start(bf16[64,64,256]{2,1,0:T(8,128)(2,1)} %reproject.1), calls=%async_computation | async-start | bytes 4194304 | tf_op jit(solution)/shard_map/all_to_all | solution.py:246
  20.0 9.2 %copy-start.5 = (s32[16,4]{0,1:T(4,128)S(1)}, s32[16,4]{0,1:T(4,128)}, u32[]{:S(2)}) copy-start(s32[16,4]{0,1:T(4,128)} %param.14) | copy-start | bytes 772
  20.0 10.0 %copy-start.6 = (bf16[256]{0:T(256)(128)(2,1)S(1)}, bf16[256]{0:T(256)(128)(2,1)}, u32[]{:S(2)}) copy-start(bf16[256]{0:T(256)(128)(2,1)} %param.19) | copy-start | bytes 1540
  20.3 9.1 %collective-permute-start = (bf16[4,4,4096]{2,1,0:T(4,128)(2,1)S(1)}, bf16[4,4,4096]{2,1,0:T(4,128)(2,1)S(1)}, u32[]{:S(2)}, u32[]{:S(2)}) collective-permute-start(bf16[4,4,4096]{2,1,0:T(4,128)(2,1)S(1)} %get-tuple-element.15), channel_id=1, source_target_pairs={{0,64},{64,128},{128,192},{192,0},{1,65},{65,129},{129,193},{193,1... | collective-permute-start | bytes 393224 | tf_op jit(solution)/shard_map/ppermute | solution.py:255
  21.6 8.4 %collective-permute-start.1 = (bf16[4,4,4096]{2,1,0:T(4,128)(2,1)S(1)}, bf16[4,4,4096]{2,1,0:T(4,128)(2,1)S(1)}, u32[]{:S(2)}, u32[]{:S(2)}) collective-permute-start(bf16[4,4,4096]{2,1,0:T(4,128)(2,1)S(1)} %get-tuple-element.14), channel_id=1, source_target_pairs={{0,128},{64,192},{128,0},{192,64},{1,129},{65,193},{129,1},{193,65... | collective-permute-start | bytes 393224 | tf_op jit(solution)/shard_map/ppermute | solution.py:255
  24.0 6.0 %collective-permute-start.2 = (bf16[4,4,4096]{2,1,0:T(4,128)(2,1)S(1)}, bf16[4,4,4096]{2,1,0:T(4,128)(2,1)S(1)}, u32[]{:S(2)}, u32[]{:S(2)}) collective-permute-start(bf16[4,4,4096]{2,1,0:T(4,128)(2,1)S(1)} %get-tuple-element.13), channel_id=1, source_target_pairs={{0,192},{64,0},{128,64},{192,128},{1,193},{65,1},{129,65},{193,129... | collective-permute-start | bytes 393224 | tf_op jit(solution)/shard_map/ppermute | solution.py:255
  71.2 1.3 copy-start
  89.3 16.1 %copy-start.1 = (bf16[64,64,256]{2,1,0:T(8,128)(2,1)S(1)}, bf16[64,64,256]{2,1,0:T(8,128)(2,1)}, u32[]{:S(2)}) copy-start(bf16[64,64,256]{2,1,0:T(8,128)(2,1)} %copy-done) | copy-start | bytes 6291460
  118.5 16.8 %all-to-all-start.3 = ((f32[64,4,128]{2,1,0:T(4,128)}), f32[64,4,128]{2,1,0:T(4,128)S(1)}, u32[]{:S(2)}, u32[]{:S(2)}) async-start(f32[64,4,128]{2,1,0:T(4,128)} %merge.1), calls=%async_computation.3 | async-start | bytes 262144 | tf_op jit(solution)/shard_map/all_to_all | solution.py:327

commit v3 on v2

--- a/solution.py
+++ b/solution.py
@@ -66,16 +66,19 @@
 
 
 def weight_kernel(
-    band_ref, w_ref, id_ref, col_ref, row_ref, spread_ref, spread1_ref, out_ref, scratch
+    band_ref, w0, w1, w2, w3, id_ref, col_ref, row_ref, spread_ref, spread1_ref, out_ref, scratch
 ):
+    turn = pl.program_id(0)
+    place = 2 * ((band_ref[0] + 4 - turn) % 4)
     mask = parity_mask(256)
     mask1 = parity_mask(SIDE)
     spread = spread_ref[...]
     spread1 = spread1_ref[...]
     group = range(4)
-    planes = [jnp.where(mask1, dot(spread1, w_ref[s]), 0.0).astype(BF16) for s in group]
+    w = jnp.where(turn < 2, jnp.where(turn < 1, w0[...], w1[...]), jnp.where(turn < 3, w2[...], w3[...]))
+    planes = [jnp.where(mask1, dot(spread1, w[s]), 0.0).astype(BF16) for s in group]
     wide = [dot(spread, jnp.concatenate([col_ref[s], row_ref[s]], 1)) for s in group]
-    pairs = [spread_pair(w, mask) for w in wide]
+    pairs = [spread_pair(x, mask) for x in wide]
     halves = [dot(planes[s], pairs[s][0], ((1,), (1,))) for s in group]
     for s in group:
         parts = []
@@ -87,8 +90,15 @@
             pair = jnp.concatenate(parts[2 * v : 2 * v + 2], 1)
             scratch[v, pl.ds(s, SIDE, stride=4), :] = pair
     for v in range(2):
-        out_ref[:, v] = scratch[v].reshape(SIDE, 4, 128).astype(BF16)
-    out_ref[:, 2] = jnp.broadcast_to(id_ref[...].astype(BF16)[None], (SIDE, 4, 128))
+        out_ref[:, place + v] = scratch[v].reshape(SIDE, 4, 128).astype(BF16)
+
+    @pl.when(turn == 0)
+    def _():
+        out_ref[:, 8] = jnp.broadcast_to(id_ref[...].astype(BF16)[None], (SIDE, 4, 128))
+
+
+def after_kernel(x_ref, first_ref, out_ref):
+    pass
 
 
 def cloud_kernel(x0, x1, x2, x3, factor_ref, w_in_ref, w_hidden_ref, w_out_ref, out_ref):
@@ -107,13 +117,15 @@
     out_ref[0] = jnp.concatenate(lines, 0).astype(BF16)
 
 
-def merge_kernel(y_ref, w_ref, out_ref, pick, pick_t, weight):
+def merge_kernel(y_in, w_ref, out_ref, y_ref, pick, pick_t, weight, arrival):
+    fetch = pltpu.make_async_copy(y_in, y_ref, arrival)
+    fetch.start()
     entries = y_ref.shape[0]
     chunk = 512
     chunks = entries // chunk
     lane = lax.broadcasted_iota(jnp.int32, (entries // SIDE, 128), 1)
     tile = (lax.broadcasted_iota(jnp.int32, (128, 128), 0) & 63).astype(F32)
-    ids = w_ref[0, :, 2].astype(F32)[:, 0, :]
+    ids = w_ref[:, 8].astype(F32)[:, 0, :]
     turned = pltpu.roll(ids, 64, 1)
     for i in range(entries // 128):
         span = slice(i * 128, (i + 1) * 128)
@@ -124,11 +136,13 @@
     lane = lax.broadcasted_iota(jnp.int32, (entries // SIDE, 4, 128), 2)
     for b in range(4):
         for v in range(2):
-            w = w_ref[b, :, v].astype(F32) * huber_delta
+            w = w_ref[:, 2 * b + v].astype(F32) * huber_delta
             turned = pltpu.roll(w, 64, 2)
             first = 16 * b + 8 * v
             weight[:, first : first + 4, :] = jnp.where(lane < 64, w, turned)
             weight[:, first + 4 : first + 8, :] = jnp.where(lane < 64, turned, w)
+
+    fetch.wait()
 
     def totals(estimate, exact):
         top = bottom = 0.0
@@ -145,9 +159,13 @@
             else:
                 residual = y - dot(pick_t[span, :], stacked)
                 h = jnp.concatenate([w, w], 1) / jnp.maximum(jnp.abs(residual), huber_delta)
-            hy = h * y
             picked = pick[:, span]
-            h_high, hy_high = h.astype(BF16), hy.astype(BF16)
+            h_high = h.astype(BF16)
+            if exact:
+                hy = h * y
+                hy_high = hy.astype(BF16)
+            else:
+                hy_high = h_high * y_ref[span, :]
             top = top + dot(picked, hy_high)
             bottom = bottom + dot(picked, h_high)
             if exact:
@@ -287,43 +305,50 @@
     )
     ids = intersections.reshape(groups, share, 4).transpose(0, 2, 1).reshape(1, scenes * 4)
     ids = jnp.broadcast_to(jnp.pad(ids, ((0, 0), (0, 128 - scenes * 4))).astype(F32), (4, 128))
-    mine = pl.BlockSpec((4, 128, 128), lambda i, b: (b[0], 0, 0))
+    all_weights = [weights] + [
+        lax.ppermute(weights, "band", [(i, (i + turn) % groups) for i in range(groups)])
+        for turn in range(1, groups)
+    ]
+    theirs = pl.BlockSpec((4, 128, 128), lambda i, b: ((b[0] + 4 - i) % 4, 0, 0))
     moved_weights = pl.pallas_call(
         weight_kernel,
         grid_spec=pltpu.PrefetchScalarGridSpec(
             num_scalar_prefetch=1,
-            grid=(1,),
-            in_specs=[
-                whole((share, SIDE // 2, 128)),
-                whole((4, 128)),
-                mine,
-                mine,
-                whole((256, 128)),
-                whole((SIDE, SIDE // 2)),
-            ],
-            out_specs=whole((SIDE, 3, share, 128)),
+            grid=(groups,),
+            in_specs=[whole((share, SIDE // 2, 128))] * groups
+            + [whole((4, 128)), theirs, theirs, whole((256, 128)), whole((SIDE, SIDE // 2))],
+            out_specs=whole((SIDE, 9, share, 128)),
             scratch_shapes=[pltpu.VMEM((2, SIDE * share, 128), F32)],
         ),
-        out_shape=jax.ShapeDtypeStruct((SIDE, 3, share, 128), BF16),
+        out_shape=jax.ShapeDtypeStruct((SIDE, 9, share, 128), BF16),
+        cost_estimate=pl.CostEstimate(flops=8 * 10**9, transcendentals=0, bytes_accessed=10**6),
         name="reproject_weights",
-    )(band.astype(jnp.int32).reshape(1), weights, ids, cols, rows, spread, spread1)
-    moved_weights, values = lax.optimization_barrier((moved_weights, values))
+    )(band.astype(jnp.int32).reshape(1), *all_weights, ids, cols, rows, spread, spread1)
+    anywhere = pl.BlockSpec(memory_space=pl.ANY)
+    moved_weights = pl.pallas_call(
+        after_kernel,
+        in_specs=[anywhere, anywhere],
+        out_specs=anywhere,
+        out_shape=jax.ShapeDtypeStruct(moved_weights.shape, BF16),
+        input_output_aliases={0: 0},
+        name="after",
+    )(moved_weights, keep(values))
     moved_weights = lax.all_to_all(moved_weights, "tile", split_axis=0, concat_axis=0)
-    moved_weights = jnp.broadcast_to(moved_weights[None], (groups,) + moved_weights.shape)
-    moved_weights = lax.all_to_all(moved_weights, "band", split_axis=0, concat_axis=0)
 
     entries = tiles * scenes * 4
     estimate = pl.pallas_call(
         merge_kernel,
-        in_specs=[in_vmem, in_vmem],
+        in_specs=[anywhere, in_vmem],
         out_shape=jax.ShapeDtypeStruct((tiles, 4, 128), F32),
         scratch_shapes=[
+            pltpu.VMEM((entries, 256), BF16),
             pltpu.VMEM((SIDE, entries), BF16),
             pltpu.VMEM((entries, 128), BF16),
             pltpu.VMEM((tiles, SIDE, 128), F32),
+            pltpu.SemaphoreType.DMA,
         ],
         name="merge",
-    )(keep(values.reshape(entries, 256)), keep(moved_weights))
+    )(values.reshape(entries, 256), keep(moved_weights))
     field = lax.all_to_all(estimate, "tile", split_axis=0, concat_axis=0)
 
     place = jnp.stack([lax.axis_index("tile"), tiles]).astype(jnp.int32)

time: 138 us -> 129 us (0.935)
  blocking collectives: 32.7 us -> 24.5 us
  waiting for transfers between devices: 36.8 us -> 30.3 us
  Pallas kernels: 35 us -> 39.6 us
  starting transfers between devices: 24.6 us -> 28.6 us
  local copies, waits for them, and re-layouts: 4.95 us -> 3.46 us
    all_to_all x1 -> x0, blocking collectives: 15.9 us -> none  [per_device(): lax.all_to_all(moved_weights, 'band', split_axis=0, concat_axis=0)]
    all_to_all x1, waiting for transfers between devices: 26.5 us -> 17 us  [per_device(): values = lax.all_to_all(moved, 'tile', split_axis=0, concat_axis=0)]
    all_to_all x1, blocking collectives: 16.7 us -> 24.5 us  [per_device(): lax.all_to_all(moved_weights, 'tile', split_axis=0, concat_axis=0)]
    ppermute x0 -> x3, starting transfers between devices: none -> 4.16 us  [per_device(): lax.ppermute(weights, 'band', [(i, (i + turn) % groups) for i in range(gr...]
    pallas_call x1, Pallas kernels: 2.54 us -> 5.51 us  [per_device(): pl.pallas_call(weight_kernel, grid_spec=pltpu.PrefetchScalarGridSpec(num_...]
    ppermute x0 -> x3, waiting for transfers between devices: none -> 2.35 us  [per_device(): lax.ppermute(weights, 'band', [(i, (i + turn) % groups) for i in range(gr...]
    pallas_call x1 -> x2, Pallas kernels: 13.1 us -> 14.7 us  [the longest x1 14.7 us: per_device(): pl.pallas_call(merge_kernel, in_specs=[anywhere, in_vmem], out_shape=jax....]
  transfers between devices with their start and end apart: 5 -> 8, of which waited for: 3 -> 6; matrix products, arithmetic and copies ran while one was open for 5% -> 4% of each run, Pallas kernels for 10% -> 13%
where the time goes in v3:
time: 129 us
  Pallas kernels  39.6 us (31%)
  waiting for transfers between devices  30.3 us (23%)
  starting transfers between devices  28.6 us (22%)
  blocking collectives  24.5 us (19%)
  local copies, waits for them, and re-layouts  3.46 us (3%)
  other arithmetic  2.11 us (2%)
    all_to_all x1, blocking collectives, per_device(): lax.all_to_all(moved_weights, 'tile', split_axis=0, concat_axis=0)  24.5 us
    all_to_all x1, waiting for transfers between devices, per_device(): values = lax.all_to_all(moved, 'tile', split_axis=0, concat_axis=0)  17 us
    pallas_call x1, Pallas kernels, per_device(): pl.pallas_call(merge_kernel, in_specs=[anywhere, in_vmem], out_shape=jax....  14.7 us
    all_to_all x1, starting transfers between devices, per_device(): values = lax.all_to_all(moved, 'tile', split_axis=0, concat_axis=0)  13.3 us
    pallas_call x1, Pallas kernels, per_device(): pl.pallas_call(cloud_kernel, grid=(share, pixels // width), in_specs=[in_...  11 us
    all_to_all x1, waiting for transfers between devices, per_device(): field = lax.all_to_all(estimate, 'tile', split_axis=0, concat_axis=0)  9.76 us
    pallas_call x1, Pallas kernels, per_device(): pl.pallas_call(reproject_kernel, grid=(4,), in_specs=[scene_block, scene_...  6.66 us
    all_to_all x1, starting transfers between devices, per_device(): field = lax.all_to_all(estimate, 'tile', split_axis=0, concat_axis=0)  6.28 us
  transfers between devices with their start and end apart: 8, of which 6 were waited for; matrix products, arithmetic and copies ran while one was open for 4% of the time, Pallas kernels for 13%

profile of v3, /device:TPU:1, one launch (start us, length us, event | category | flops | bytes accessed | tf_op | source)
XLA Modules:
  0.0 128.9 jit_solution(11675937399493617489)
XLA Ops:
  0.0 6.7 %reproject.1 = bf16[64,64,256]{2,1,0:T(8,128)(2,1)} custom-call(bf16[16,128,128]{2,1,0:T(8,128)(2,1)} %bitcast.47, bf16[16,128,128]{2,1,0:T(8,128)(2,1)} %bitcast.49, bf16[16,128,128]{2,1,0:T(8,128)(2,1)} %bitcast.51, bf16[256,128]{1,0:T(8,128)(2,1)} %constant.99.clone.spread_ref), custom_call_target="tpu_custom_call" | custom-call | tf_op jit(solution)/shard_map/reproject/pallas_call | solution.py:254
  6.7 13.3 %all-to-all-start = ((bf16[64,64,256]{2,1,0:T(8,128)(2,1)}), bf16[64,64,256]{2,1,0:T(8,128)(2,1)S(1)}, u32[]{:S(2)}, u32[]{:S(2)}) async-start(bf16[64,64,256]{2,1,0:T(8,128)(2,1)} %reproject.1), calls=%async_computation | async-start | bytes 4194304 | tf_op jit(solution)/shard_map/all_to_all | solution.py:264
  20.3 1.3 collective-permute-start
  21.6 2.5 %collective-permute-start.1 = (bf16[4,4,4096]{2,1,0:T(4,128)(2,1)S(1)}, bf16[4,4,4096]{2,1,0:T(4,128)(2,1)S(1)}, u32[]{:S(2)}, u32[]{:S(2)}) collective-permute-start(bf16[4,4,4096]{2,1,0:T(4,128)(2,1)S(1)} %get-tuple-element.10), channel_id=1, source_target_pairs={{0,128},{64,192},{128,0},{192,64},{1,129},{65,193},{129,1},{193,65... | collective-permute-start | bytes 393224 | tf_op jit(solution)/shard_map/ppermute | solution.py:273
  24.1 1.1 collective-permute-start.2
  25.3 0.8 fusion.1
  26.1 0.8 reshape.54.factor_ref
  27.0 0.7 copy.32
  28.1 0.7 multiply_bitcast_fusion.w_hidden_ref
  28.8 1.2 collective-permute-done.1.x2
  30.6 11.0 %cloud.1.w0 = bf16[4,32,128]{2,1,0:T(8,128)(2,1)} custom-call(bf16[4,4,4096]{2,1,0:T(4,128)(2,1)S(1)} %get-tuple-element.12.x0, bf16[4,4,4096]{2,1,0:T(4,128)(2,1)S(1)} %collective-permute-done.x1, bf16[4,4,4096]{2,1,0:T(4,128)(2,1)S(1)} %collective-permute-done.1.x2, bf16[4,4,4096]{2,1,0:T(4,128)(2,1)S(1)} %collective-permute-done.2.x3, ...), custom_call_target="tpu_custom_call" | custom-call | flops 12000000000 | bytes 1000000 | tf_op jit(solution)/shard_map/cloud/pallas_call | solution.py:285
  41.6 1.1 collective-permute-start.3
  42.7 2.1 %collective-permute-start.4 = (bf16[4,32,128]{2,1,0:T(8,128)(2,1)}, bf16[4,32,128]{2,1,0:T(8,128)(2,1)S(1)}, u32[]{:S(2)}, u32[]{:S(2)}) collective-permute-start(bf16[4,32,128]{2,1,0:T(8,128)(2,1)} %cloud.1.w0), channel_id=1, source_target_pairs={{0,128},{64,192},{128,0},{192,64},{1,129},{65,193},{129,1},{193,65... | collective-permute-start | bytes 98312 | tf_op jit(solution)/shard_map/ppermute | solution.py:309
  44.8 0.9 collective-permute-start.5
  46.1 1.4 %collective-permute-done.4.w2 = bf16[4,32,128]{2,1,0:T(8,128)(2,1)S(1)} collective-permute-done((bf16[4,32,128]{2,1,0:T(8,128)(2,1)}, bf16[4,32,128]{2,1,0:T(8,128)(2,1)S(1)}, u32[]{:S(2)}, u32[]{:S(2)}) %collective-permute-start.4) | collective-permute-done | bytes 32800 | tf_op jit(solution)/shard_map/ppermute | solution.py:309
  47.5 0.6 collective-permute-done.5.w3
  48.1 0.6 broadcast_in_dim.11.id_ref
  48.7 5.5 %reproject_weights.1.x_ref = bf16[64,9,4,128]{3,2,1,0:T(4,128)(2,1)} custom-call(s32[1]{0:T(128)} %bitcast.11.band_ref, bf16[4,32,128]{2,1,0:T(8,128)(2,1)} %cloud.1.w0, bf16[4,32,128]{2,1,0:T(8,128)(2,1)} %copy-done.6, bf16[4,32,128]{2,1,0:T(8,128)(2,1)} %copy-done.7, bf16[4,32,128]{2,1,0:T(8,128)(2,1)} %copy-done.8, f32[4,128]{1,0:T(4,128)} %broadcast_in_dim.11.id_ref, ...), custom_call_target="tpu_custom_call" | custom-call | flops 8000000000 | bytes 1000000 | tf_op jit(solution)/shard_map/reproject_weights/pallas_call | solution.py:313
  54.2 17.0 %all-to-all-done.first_ref = bf16[64,64,256]{2,1,0:T(8,128)(2,1)S(1)} async-done(((bf16[64,64,256]{2,1,0:T(8,128)(2,1)}), bf16[64,64,256]{2,1,0:T(8,128)(2,1)S(1)}, u32[]{:S(2)}, u32[]{:S(2)}) %all-to-all-start) | async-done | bytes 2097184 | tf_op jit(solution)/shard_map/all_to_all | solution.py:264
  71.2 24.5 %all_to_all.15.w_ref = bf16[64,9,4,128]{3,2,1,0:T(4,128)(2,1)S(1)} all-to-all(bf16[64,9,4,128]{3,2,1,0:T(4,128)(2,1)} %after.1), channel_id=1, replica_groups=mesh['band'=4,'tile'=64] {'tile'}, dimensions={0} | all-to-all | bytes 1179648 | tf_op jit(solution)/shard_map/all_to_all | solution.py:336
  95.8 14.7 %merge.1 = f32[64,4,128]{2,1,0:T(4,128)} custom-call(bf16[4096,256]{1,0:T(8,128)(2,1)} %bitcast.46, bf16[64,9,4,128]{3,2,1,0:T(4,128)(2,1)S(1)} %all_to_all.15.w_ref), custom_call_target="tpu_custom_call" | custom-call | tf_op jit(solution)/shard_map/merge/pallas_call | solution.py:339
  110.5 6.3 %all-to-all-start.2 = ((f32[64,4,128]{2,1,0:T(4,128)}), f32[64,4,128]{2,1,0:T(4,128)S(1)}, u32[]{:S(2)}, u32[]{:S(2)}) async-start(f32[64,4,128]{2,1,0:T(4,128)} %merge.1), calls=%async_computation.2 | async-start | bytes 262144 | tf_op jit(solution)/shard_map/all_to_all | solution.py:352
  117.4 9.8 %all-to-all-done.2.g_ref = f32[64,4,128]{2,1,0:T(4,128)S(1)} async-done(((f32[64,4,128]{2,1,0:T(4,128)}), f32[64,4,128]{2,1,0:T(4,128)S(1)}, u32[]{:S(2)}, u32[]{:S(2)}) %all-to-all-start.2) | async-done | bytes 131104 | tf_op jit(solution)/shard_map/all_to_all | solution.py:352
  127.1 1.8 %smooth.1 = f32[32,4,128]{2,1,0:T(4,128)} custom-call(s32[2]{0:T(128)} %pad_add_fusion.tile_ref, f32[64,4,128]{2,1,0:T(4,128)S(1)} %all-to-all-done.2.g_ref), custom_call_target="tpu_custom_call" | custom-call | tf_op jit(solution)/shard_map/smooth/pallas_call | solution.py:355
  (38 shorter events, 2.3 us)
Async XLA Ops:
  6.7 13.4 %copy-start.1 = (bf16[16,4,4096]{2,1,0:T(4,128)(2,1)S(1)}, bf16[16,4,4096]{2,1,0:T(4,128)(2,1)}, u32[]{:S(2)}) copy-start(bf16[16,4,4096]{2,1,0:T(4,128)(2,1)} %param.11) | copy-start | bytes 1572868
  6.7 18.5 %copy-start.9 = (s32[16]{0:T(128)S(1)}, s32[16]{0:T(128)}, u32[]{:S(2)}) copy-start(s32[16]{0:T(128)} %param.13) | copy-start | bytes 196
  6.7 20.3 %copy-start.3 = (bf16[16,256]{1,0:T(8,128)(2,1)S(1)}, bf16[16,256]{1,0:T(8,128)(2,1)}, u32[]{:S(2)}) copy-start(bf16[16,256]{1,0:T(8,128)(2,1)} %param.17) | copy-start | bytes 24580
  6.7 21.0 %copy-start.2 = (bf16[2,256,256]{2,1,0:T(8,128)(2,1)S(1)}, bf16[2,256,256]{2,1,0:T(8,128)(2,1)}, u32[]{:S(2)}) copy-start(bf16[2,256,256]{2,1,0:T(8,128)(2,1)} %param.18) | copy-start | bytes 786436
  6.7 64.6 %all-to-all-start = ((bf16[64,64,256]{2,1,0:T(8,128)(2,1)}), bf16[64,64,256]{2,1,0:T(8,128)(2,1)S(1)}, u32[]{:S(2)}, u32[]{:S(2)}) async-start(bf16[64,64,256]{2,1,0:T(8,128)(2,1)} %reproject.1), calls=%async_computation | async-start | bytes 4194304 | tf_op jit(solution)/shard_map/all_to_all | solution.py:264
  20.0 7.9 %copy-start.4 = (s32[16,4]{0,1:T(4,128)S(1)}, s32[16,4]{0,1:T(4,128)}, u32[]{:S(2)}) copy-start(s32[16,4]{0,1:T(4,128)} %param.14) | copy-start | bytes 772
  20.0 10.0 %copy-start.5 = (bf16[256]{0:T(256)(128)(2,1)S(1)}, bf16[256]{0:T(256)(128)(2,1)}, u32[]{:S(2)}) copy-start(bf16[256]{0:T(256)(128)(2,1)} %param.19) | copy-start | bytes 1540
  20.3 8.5 %collective-permute-start = (bf16[4,4,4096]{2,1,0:T(4,128)(2,1)S(1)}, bf16[4,4,4096]{2,1,0:T(4,128)(2,1)S(1)}, u32[]{:S(2)}, u32[]{:S(2)}) collective-permute-start(bf16[4,4,4096]{2,1,0:T(4,128)(2,1)S(1)} %get-tuple-element.11), channel_id=1, source_target_pairs={{0,64},{64,128},{128,192},{192,0},{1,65},{65,129},{129,193},{193,1... | collective-permute-start | bytes 393224 | tf_op jit(solution)/shard_map/ppermute | solution.py:273
  21.6 8.4 %collective-permute-start.1 = (bf16[4,4,4096]{2,1,0:T(4,128)(2,1)S(1)}, bf16[4,4,4096]{2,1,0:T(4,128)(2,1)S(1)}, u32[]{:S(2)}, u32[]{:S(2)}) collective-permute-start(bf16[4,4,4096]{2,1,0:T(4,128)(2,1)S(1)} %get-tuple-element.10), channel_id=1, source_target_pairs={{0,128},{64,192},{128,0},{192,64},{1,129},{65,193},{129,1},{193,65... | collective-permute-start | bytes 393224 | tf_op jit(solution)/shard_map/ppermute | solution.py:273
  24.1 6.0 %collective-permute-start.2 = (bf16[4,4,4096]{2,1,0:T(4,128)(2,1)S(1)}, bf16[4,4,4096]{2,1,0:T(4,128)(2,1)S(1)}, u32[]{:S(2)}, u32[]{:S(2)}) collective-permute-start(bf16[4,4,4096]{2,1,0:T(4,128)(2,1)S(1)} %get-tuple-element.9), channel_id=1, source_target_pairs={{0,192},{64,0},{128,64},{192,128},{1,193},{65,1},{129,65},{193,129... | collective-permute-start | bytes 393224 | tf_op jit(solution)/shard_map/ppermute | solution.py:273
  41.6 4.5 %collective-permute-start.3 = (bf16[4,32,128]{2,1,0:T(8,128)(2,1)}, bf16[4,32,128]{2,1,0:T(8,128)(2,1)S(1)}, u32[]{:S(2)}, u32[]{:S(2)}) collective-permute-start(bf16[4,32,128]{2,1,0:T(8,128)(2,1)} %cloud.1.w0), channel_id=1, source_target_pairs={{0,64},{64,128},{128,192},{192,0},{1,65},{65,129},{129,193},{193,1... | collective-permute-start | bytes 98312 | tf_op jit(solution)/shard_map/ppermute | solution.py:309
  42.7 4.8 %collective-permute-start.4 = (bf16[4,32,128]{2,1,0:T(8,128)(2,1)}, bf16[4,32,128]{2,1,0:T(8,128)(2,1)S(1)}, u32[]{:S(2)}, u32[]{:S(2)}) collective-permute-start(bf16[4,32,128]{2,1,0:T(8,128)(2,1)} %cloud.1.w0), channel_id=1, source_target_pairs={{0,128},{64,192},{128,0},{192,64},{1,129},{65,193},{129,1},{193,65... | collective-permute-start | bytes 98312 | tf_op jit(solution)/shard_map/ppermute | solution.py:309
  44.8 3.3 %collective-permute-start.5 = (bf16[4,32,128]{2,1,0:T(8,128)(2,1)}, bf16[4,32,128]{2,1,0:T(8,128)(2,1)S(1)}, u32[]{:S(2)}, u32[]{:S(2)}) collective-permute-start(bf16[4,32,128]{2,1,0:T(8,128)(2,1)} %cloud.1.w0), channel_id=1, source_target_pairs={{0,192},{64,0},{128,64},{192,128},{1,193},{65,1},{129,65},{193,129... | collective-permute-start | bytes 98312 | tf_op jit(solution)/shard_map/ppermute | solution.py:309
  46.1 2.6 %copy-start.6 = (bf16[4,32,128]{2,1,0:T(8,128)(2,1)}, bf16[4,32,128]{2,1,0:T(8,128)(2,1)S(1)}, u32[]{:S(2)}) copy-start(bf16[4,32,128]{2,1,0:T(8,128)(2,1)S(1)} %collective-permute-done.3.w1) | copy-start | bytes 98308
  47.5 1.2 copy-start.7
  48.1 0.6 copy-start.8
  71.2 24.5 %copy-start = (bf16[64,64,256]{2,1,0:T(8,128)(2,1)}, bf16[64,64,256]{2,1,0:T(8,128)(2,1)S(1)}, u32[]{:S(2)}) copy-start(bf16[64,64,256]{2,1,0:T(8,128)(2,1)S(1)} %all-to-all-done.first_ref) | copy-start | bytes 6291460
  110.5 16.6 %all-to-all-start.2 = ((f32[64,4,128]{2,1,0:T(4,128)}), f32[64,4,128]{2,1,0:T(4,128)S(1)}, u32[]{:S(2)}, u32[]{:S(2)}) async-start(f32[64,4,128]{2,1,0:T(4,128)} %merge.1), calls=%async_computation.2 | async-start | bytes 262144 | tf_op jit(solution)/shard_map/all_to_all | solution.py:352

commit v4 on v3

--- a/solution.py
+++ b/solution.py
@@ -30,6 +30,11 @@
     return out
 
 
+def double_matrix():
+    eye = huber_delta * np.eye(SIDE, dtype=np.float32)
+    return np.kron(np.eye(2, dtype=np.float32), np.concatenate([eye, eye], 1))
+
+
 def parity_mask(rows):
     row = lax.broadcasted_iota(jnp.int32, (rows, 128), 0)
     lane = lax.broadcasted_iota(jnp.int32, (rows, 128), 1)
@@ -37,8 +42,8 @@
 
 
 def spread_pair(both, mask):
-    col = jnp.where(mask, both[:, :128], 0.0)
-    col = (col + pltpu.roll(col, 64, 1)).astype(BF16)
+    col = jnp.where(mask, both[:, :128], 0.0).astype(BF16)
+    col = col + pltpu.roll(col, 64, 1)
     row = jnp.where(mask, both[:, 128:], 0.0).astype(BF16)
     return col, row
 
@@ -51,12 +56,12 @@
     wide = [dot(spread, w) for w in wide]
     planes = [jnp.where(mask, w[:, :128], 0.0).astype(BF16) for w in wide]
     pairs = [spread_pair(w[:, 128:], mask) for w in wide]
-    halves = [dot(planes[s], pairs[s][0], ((1,), (1,))) for s in group]
+    halves = [dot(planes[s], pairs[s][0], ((1,), (1,))).astype(BF16) for s in group]
     for s in group:
         for k in range(4):
             lanes = slice(k * SIDE, (k + 1) * SIDE)
             part = [halves[s][c * SIDE : (c + 1) * SIDE, lanes] for c in range(4)]
-            part = jnp.concatenate(part, 1).astype(BF16)
+            part = jnp.concatenate(part, 1)
             part = jnp.concatenate([part, part], 0)
             moved = dot(pairs[s][1][k * SIDE : (k + 1) * SIDE], part)
             for v in range(2):
@@ -117,65 +122,57 @@
     out_ref[0] = jnp.concatenate(lines, 0).astype(BF16)
 
 
-def merge_kernel(y_in, w_ref, out_ref, y_ref, pick, pick_t, weight, arrival):
+def merge_kernel(y_in, w_ref, double_ref, out_ref, y_ref, pick, pick_t, weight, arrival):
     fetch = pltpu.make_async_copy(y_in, y_ref, arrival)
     fetch.start()
     entries = y_ref.shape[0]
     chunk = 512
-    chunks = entries // chunk
-    lane = lax.broadcasted_iota(jnp.int32, (entries // SIDE, 128), 1)
+    lane = lax.broadcasted_iota(jnp.int32, (1, 128), 1)
     tile = (lax.broadcasted_iota(jnp.int32, (128, 128), 0) & 63).astype(F32)
     ids = w_ref[:, 8].astype(F32)[:, 0, :]
     turned = pltpu.roll(ids, 64, 1)
     for i in range(entries // 128):
         span = slice(i * 128, (i + 1) * 128)
-        pair = jnp.where(lane[:1] < 64, ids[2 * i : 2 * i + 1], turned[2 * i + 1 : 2 * i + 2])
+        pair = jnp.where(lane < 64, ids[2 * i : 2 * i + 1], turned[2 * i + 1 : 2 * i + 2])
         hit = jnp.where(pair == tile, 1.0, 0.0)
         pick[:, span] = hit[:SIDE].astype(BF16)
         pick_t[span, :] = hit.T.astype(BF16)
-    lane = lax.broadcasted_iota(jnp.int32, (entries // SIDE, 4, 128), 2)
-    for b in range(4):
-        for v in range(2):
-            w = w_ref[:, 2 * b + v].astype(F32) * huber_delta
-            turned = pltpu.roll(w, 64, 2)
-            first = 16 * b + 8 * v
-            weight[:, first : first + 4, :] = jnp.where(lane < 64, w, turned)
-            weight[:, first + 4 : first + 8, :] = jnp.where(lane < 64, turned, w)
-
+    for i in range(8):
+        w = dot(w_ref[:, i].reshape(entries // 16, 128), double_ref[...])
+        for half in range(2):
+            first = 8 * i + 4 * half
+            weight[:, first : first + 4, :] = w[:, half * 128 : (half + 1) * 128].reshape(
+                entries // SIDE, 4, 128
+            )
     fetch.wait()
 
-    def totals(estimate, exact):
+    def totals(estimate):
         top = bottom = 0.0
         if estimate is not None:
             high = estimate.astype(BF16)
             low = (estimate - high.astype(F32)).astype(BF16)
             stacked = jnp.concatenate([high, low], 0)
-        for i in range(chunks):
-            span = slice(i * chunk, (i + 1) * chunk)
-            y = y_ref[span, :].astype(F32)
+        spans = [slice(i * chunk, (i + 1) * chunk) for i in range(entries // chunk)]
+
+        def expected(span):
+            return None if estimate is None else dot(pick_t[span, :], stacked)
+
+        ahead = expected(spans[0])
+        for i, span in enumerate(spans):
+            here, ahead = ahead, expected(spans[i + 1]) if i + 1 < len(spans) else None
             w = weight[i * chunk // SIDE : (i + 1) * chunk // SIDE].reshape(chunk, 128)
-            if estimate is None:
-                h = jnp.concatenate([w, w], 1) * (1.0 / huber_delta)
-            else:
-                residual = y - dot(pick_t[span, :], stacked)
-                h = jnp.concatenate([w, w], 1) / jnp.maximum(jnp.abs(residual), huber_delta)
+            y = y_ref[span, :]
+            h = jnp.concatenate([w, w], 1)
+            if estimate is not None:
+                h = h / jnp.maximum(jnp.abs(y.astype(F32) - here), huber_delta)
+            h = h.astype(BF16)
             picked = pick[:, span]
-            h_high = h.astype(BF16)
-            if exact:
-                hy = h * y
-                hy_high = hy.astype(BF16)
-            else:
-                hy_high = h_high * y_ref[span, :]
-            top = top + dot(picked, hy_high)
-            bottom = bottom + dot(picked, h_high)
-            if exact:
-                top = top + dot(picked, (hy - hy_high.astype(F32)).astype(BF16))
-                bottom = bottom + dot(picked, (h - h_high.astype(F32)).astype(BF16))
-        return top / (bottom + prior_weight)
-
-    estimate = totals(None, False)
-    estimate = lax.fori_loop(0, HUBER_ITERS - 1, lambda _, e: totals(e, False), estimate)
-    estimate = totals(estimate, True)
+            top = top + dot(picked, h * y)
+            bottom = bottom + dot(picked, h)
+        prior = prior_weight if estimate is not None else prior_weight * huber_delta
+        return top / (bottom + prior)
+
+    estimate = lax.fori_loop(0, HUBER_ITERS, lambda _, e: totals(e), totals(None))
 
     lane = lax.broadcasted_iota(jnp.int32, (SIDE, 128), 1)
     for v in range(2):
@@ -338,7 +335,7 @@
     entries = tiles * scenes * 4
     estimate = pl.pallas_call(
         merge_kernel,
-        in_specs=[anywhere, in_vmem],
+        in_specs=[anywhere, in_vmem, in_vmem],
         out_shape=jax.ShapeDtypeStruct((tiles, 4, 128), F32),
         scratch_shapes=[
             pltpu.VMEM((entries, 256), BF16),
@@ -348,7 +345,7 @@
             pltpu.SemaphoreType.DMA,
         ],
         name="merge",
-    )(values.reshape(entries, 256), keep(moved_weights))
+    )(values.reshape(entries, 256), keep(moved_weights), jnp.asarray(double_matrix(), BF16))
     field = lax.all_to_all(estimate, "tile", split_axis=0, concat_axis=0)
 
     place = jnp.stack([lax.axis_index("tile"), tiles]).astype(jnp.int32)

time: 129 us -> 125 us (0.969)
  Pallas kernels: 39.6 us -> 35.5 us
    pallas_call x1, Pallas kernels: 14.7 us -> 10.6 us  [per_device(): pl.pallas_call(merge_kernel, in_specs=[anywhere, in_vmem, in_vmem], out_s...]
where the time goes in v4:
time: 125 us
  Pallas kernels  35.5 us (28%)
  waiting for transfers between devices  30.3 us (24%)
  starting transfers between devices  28.7 us (23%)
  blocking collectives  24.5 us (20%)
  local copies, waits for them, and re-layouts  3.46 us (3%)
  other arithmetic  2.11 us (2%)
    all_to_all x1, blocking collectives, per_device(): lax.all_to_all(moved_weights, 'tile', split_axis=0, concat_axis=0)  24.5 us
    all_to_all x1, waiting for transfers between devices, per_device(): values = lax.all_to_all(moved, 'tile', split_axis=0, concat_axis=0)  17 us
    all_to_all x1, starting transfers between devices, per_device(): values = lax.all_to_all(moved, 'tile', split_axis=0, concat_axis=0)  13.3 us
    pallas_call x1, Pallas kernels, per_device(): pl.pallas_call(cloud_kernel, grid=(share, pixels // width), in_specs=[in_...  11 us
    pallas_call x1, Pallas kernels, per_device(): pl.pallas_call(merge_kernel, in_specs=[anywhere, in_vmem, in_vmem], out_s...  10.6 us
    all_to_all x1, waiting for transfers between devices, per_device(): field = lax.all_to_all(estimate, 'tile', split_axis=0, concat_axis=0)  9.76 us
    pallas_call x1, Pallas kernels, per_device(): pl.pallas_call(reproject_kernel, grid=(4,), in_specs=[scene_block, scene_...  6.67 us
    all_to_all x1, starting transfers between devices, per_device(): field = lax.all_to_all(estimate, 'tile', split_axis=0, concat_axis=0)  6.28 us
  transfers between devices with their start and end apart: 8, of which 6 were waited for; matrix products, arithmetic and copies ran while one was open for 4% of the time, Pallas kernels for 13%

profile of v4, /device:TPU:1, one launch (start us, length us, event | category | flops | bytes accessed | tf_op | source)
XLA Modules:
  0.0 124.8 jit_solution(1188992896280444114)
XLA Ops:
  0.0 6.7 %reproject.1 = bf16[64,64,256]{2,1,0:T(8,128)(2,1)} custom-call(bf16[16,128,128]{2,1,0:T(8,128)(2,1)} %bitcast.47, bf16[16,128,128]{2,1,0:T(8,128)(2,1)} %bitcast.49, bf16[16,128,128]{2,1,0:T(8,128)(2,1)} %bitcast.51, bf16[256,128]{1,0:T(8,128)(2,1)} %constant.101.clone.spread_ref), custom_call_target="tpu_custom_call" | custom-call | tf_op jit(solution)/shard_map/reproject/pallas_call | solution.py:251
  6.7 13.3 %all-to-all-start = ((bf16[64,64,256]{2,1,0:T(8,128)(2,1)}), bf16[64,64,256]{2,1,0:T(8,128)(2,1)S(1)}, u32[]{:S(2)}, u32[]{:S(2)}) async-start(bf16[64,64,256]{2,1,0:T(8,128)(2,1)} %reproject.1), calls=%async_computation | async-start | bytes 4194304 | tf_op jit(solution)/shard_map/all_to_all | solution.py:261
  20.3 1.3 %collective-permute-start = (bf16[4,4,4096]{2,1,0:T(4,128)(2,1)S(1)}, bf16[4,4,4096]{2,1,0:T(4,128)(2,1)S(1)}, u32[]{:S(2)}, u32[]{:S(2)}) collective-permute-start(bf16[4,4,4096]{2,1,0:T(4,128)(2,1)S(1)} %get-tuple-element.11), channel_id=1, source_target_pairs={{0,64},{64,128},{128,192},{192,0},{1,65},{65,129},{129,193},{193,1... | collective-permute-start | bytes 393224 | tf_op jit(solution)/shard_map/ppermute | solution.py:270
  21.6 2.5 %collective-permute-start.1 = (bf16[4,4,4096]{2,1,0:T(4,128)(2,1)S(1)}, bf16[4,4,4096]{2,1,0:T(4,128)(2,1)S(1)}, u32[]{:S(2)}, u32[]{:S(2)}) collective-permute-start(bf16[4,4,4096]{2,1,0:T(4,128)(2,1)S(1)} %get-tuple-element.10), channel_id=1, source_target_pairs={{0,128},{64,192},{128,0},{192,64},{1,129},{65,193},{129,1},{193,65... | collective-permute-start | bytes 393224 | tf_op jit(solution)/shard_map/ppermute | solution.py:270
  24.1 1.2 collective-permute-start.2
  25.3 0.8 fusion.1
  26.2 0.8 reshape.54.factor_ref
  27.0 0.7 copy.33
  28.1 0.7 multiply_bitcast_fusion.w_hidden_ref
  28.8 1.2 collective-permute-done.1.x2
  30.6 11.0 %cloud.1.w0 = bf16[4,32,128]{2,1,0:T(8,128)(2,1)} custom-call(bf16[4,4,4096]{2,1,0:T(4,128)(2,1)S(1)} %get-tuple-element.12.x0, bf16[4,4,4096]{2,1,0:T(4,128)(2,1)S(1)} %collective-permute-done.x1, bf16[4,4,4096]{2,1,0:T(4,128)(2,1)S(1)} %collective-permute-done.1.x2, bf16[4,4,4096]{2,1,0:T(4,128)(2,1)S(1)} %collective-permute-done.2.x3, ...), custom_call_target="tpu_custom_call" | custom-call | flops 12000000000 | bytes 1000000 | tf_op jit(solution)/shard_map/cloud/pallas_call | solution.py:282
  41.6 1.1 collective-permute-start.3
  42.7 2.1 %collective-permute-start.4 = (bf16[4,32,128]{2,1,0:T(8,128)(2,1)}, bf16[4,32,128]{2,1,0:T(8,128)(2,1)S(1)}, u32[]{:S(2)}, u32[]{:S(2)}) collective-permute-start(bf16[4,32,128]{2,1,0:T(8,128)(2,1)} %cloud.1.w0), channel_id=1, source_target_pairs={{0,128},{64,192},{128,0},{192,64},{1,129},{65,193},{129,1},{193,65... | collective-permute-start | bytes 98312 | tf_op jit(solution)/shard_map/ppermute | solution.py:306
  44.9 0.9 collective-permute-start.5
  46.1 1.4 %collective-permute-done.4.w2 = bf16[4,32,128]{2,1,0:T(8,128)(2,1)S(1)} collective-permute-done((bf16[4,32,128]{2,1,0:T(8,128)(2,1)}, bf16[4,32,128]{2,1,0:T(8,128)(2,1)S(1)}, u32[]{:S(2)}, u32[]{:S(2)}) %collective-permute-start.4) | collective-permute-done | bytes 32800 | tf_op jit(solution)/shard_map/ppermute | solution.py:306
  47.5 0.6 collective-permute-done.5.w3
  48.1 0.6 broadcast_in_dim.11.id_ref
  48.7 5.5 %reproject_weights.1.x_ref = bf16[64,9,4,128]{3,2,1,0:T(4,128)(2,1)} custom-call(s32[1]{0:T(128)} %bitcast.11.band_ref, bf16[4,32,128]{2,1,0:T(8,128)(2,1)} %cloud.1.w0, bf16[4,32,128]{2,1,0:T(8,128)(2,1)} %copy-done.6, bf16[4,32,128]{2,1,0:T(8,128)(2,1)} %copy-done.7, bf16[4,32,128]{2,1,0:T(8,128)(2,1)} %copy-done.8, f32[4,128]{1,0:T(4,128)} %broadcast_in_dim.11.id_ref, ...), custom_call_target="tpu_custom_call" | custom-call | flops 8000000000 | bytes 1000000 | tf_op jit(solution)/shard_map/reproject_weights/pallas_call | solution.py:310
  54.2 17.0 %all-to-all-done.first_ref = bf16[64,64,256]{2,1,0:T(8,128)(2,1)S(1)} async-done(((bf16[64,64,256]{2,1,0:T(8,128)(2,1)}), bf16[64,64,256]{2,1,0:T(8,128)(2,1)S(1)}, u32[]{:S(2)}, u32[]{:S(2)}) %all-to-all-start) | async-done | bytes 2097184 | tf_op jit(solution)/shard_map/all_to_all | solution.py:261
  71.3 24.5 %all_to_all.15.w_ref = bf16[64,9,4,128]{3,2,1,0:T(4,128)(2,1)S(1)} all-to-all(bf16[64,9,4,128]{3,2,1,0:T(4,128)(2,1)} %after.1), channel_id=1, replica_groups=mesh['band'=4,'tile'=64] {'tile'}, dimensions={0} | all-to-all | bytes 1179648 | tf_op jit(solution)/shard_map/all_to_all | solution.py:333
  95.8 10.6 %merge.1 = f32[64,4,128]{2,1,0:T(4,128)} custom-call(bf16[4096,256]{1,0:T(8,128)(2,1)} %bitcast.46, bf16[64,9,4,128]{3,2,1,0:T(4,128)(2,1)S(1)} %all_to_all.15.w_ref, bf16[128,256]{1,0:T(8,128)(2,1)} %constant.103.clone.double_ref), custom_call_target="tpu_custom_call" | custom-call | tf_op jit(solution)/shard_map/merge/pallas_call | solution.py:336
  106.4 6.3 %all-to-all-start.2 = ((f32[64,4,128]{2,1,0:T(4,128)}), f32[64,4,128]{2,1,0:T(4,128)S(1)}, u32[]{:S(2)}, u32[]{:S(2)}) async-start(f32[64,4,128]{2,1,0:T(4,128)} %merge.1), calls=%async_computation.2 | async-start | bytes 262144 | tf_op jit(solution)/shard_map/all_to_all | solution.py:349
  113.3 9.8 %all-to-all-done.2.g_ref = f32[64,4,128]{2,1,0:T(4,128)S(1)} async-done(((f32[64,4,128]{2,1,0:T(4,128)}), f32[64,4,128]{2,1,0:T(4,128)S(1)}, u32[]{:S(2)}, u32[]{:S(2)}) %all-to-all-start.2) | async-done | bytes 131104 | tf_op jit(solution)/shard_map/all_to_all | solution.py:349
  123.0 1.8 %smooth.1 = f32[32,4,128]{2,1,0:T(4,128)} custom-call(s32[2]{0:T(128)} %pad_add_fusion.tile_ref, f32[64,4,128]{2,1,0:T(4,128)S(1)} %all-to-all-done.2.g_ref), custom_call_target="tpu_custom_call" | custom-call | tf_op jit(solution)/shard_map/smooth/pallas_call | solution.py:352
  (38 shorter events, 2.3 us)
Async XLA Ops:
  6.7 13.4 %copy-start.1 = (bf16[16,4,4096]{2,1,0:T(4,128)(2,1)S(1)}, bf16[16,4,4096]{2,1,0:T(4,128)(2,1)}, u32[]{:S(2)}) copy-start(bf16[16,4,4096]{2,1,0:T(4,128)(2,1)} %param.12) | copy-start | bytes 1572868
  6.7 18.6 %copy-start.9 = (s32[16]{0:T(128)S(1)}, s32[16]{0:T(128)}, u32[]{:S(2)}) copy-start(s32[16]{0:T(128)} %param.14) | copy-start | bytes 196
  6.7 20.3 %copy-start.3 = (bf16[16,256]{1,0:T(8,128)(2,1)S(1)}, bf16[16,256]{1,0:T(8,128)(2,1)}, u32[]{:S(2)}) copy-start(bf16[16,256]{1,0:T(8,128)(2,1)} %param.18) | copy-start | bytes 24580
  6.7 21.1 %copy-start.2 = (bf16[2,256,256]{2,1,0:T(8,128)(2,1)S(1)}, bf16[2,256,256]{2,1,0:T(8,128)(2,1)}, u32[]{:S(2)}) copy-start(bf16[2,256,256]{2,1,0:T(8,128)(2,1)} %param.19) | copy-start | bytes 786436
  6.7 64.6 %all-to-all-start = ((bf16[64,64,256]{2,1,0:T(8,128)(2,1)}), bf16[64,64,256]{2,1,0:T(8,128)(2,1)S(1)}, u32[]{:S(2)}, u32[]{:S(2)}) async-start(bf16[64,64,256]{2,1,0:T(8,128)(2,1)} %reproject.1), calls=%async_computation | async-start | bytes 4194304 | tf_op jit(solution)/shard_map/all_to_all | solution.py:261
  20.0 7.9 %copy-start.4 = (s32[16,4]{0,1:T(4,128)S(1)}, s32[16,4]{0,1:T(4,128)}, u32[]{:S(2)}) copy-start(s32[16,4]{0,1:T(4,128)} %param.15) | copy-start | bytes 772
  20.0 10.0 %copy-start.5 = (bf16[256]{0:T(256)(128)(2,1)S(1)}, bf16[256]{0:T(256)(128)(2,1)}, u32[]{:S(2)}) copy-start(bf16[256]{0:T(256)(128)(2,1)} %param.20) | copy-start | bytes 1540
  20.3 8.5 %collective-permute-start = (bf16[4,4,4096]{2,1,0:T(4,128)(2,1)S(1)}, bf16[4,4,4096]{2,1,0:T(4,128)(2,1)S(1)}, u32[]{:S(2)}, u32[]{:S(2)}) collective-permute-start(bf16[4,4,4096]{2,1,0:T(4,128)(2,1)S(1)} %get-tuple-element.11), channel_id=1, source_target_pairs={{0,64},{64,128},{128,192},{192,0},{1,65},{65,129},{129,193},{193,1... | collective-permute-start | bytes 393224 | tf_op jit(solution)/shard_map/ppermute | solution.py:270
  21.6 8.4 %collective-permute-start.1 = (bf16[4,4,4096]{2,1,0:T(4,128)(2,1)S(1)}, bf16[4,4,4096]{2,1,0:T(4,128)(2,1)S(1)}, u32[]{:S(2)}, u32[]{:S(2)}) collective-permute-start(bf16[4,4,4096]{2,1,0:T(4,128)(2,1)S(1)} %get-tuple-element.10), channel_id=1, source_target_pairs={{0,128},{64,192},{128,0},{192,64},{1,129},{65,193},{129,1},{193,65... | collective-permute-start | bytes 393224 | tf_op jit(solution)/shard_map/ppermute | solution.py:270
  24.1 6.0 %collective-permute-start.2 = (bf16[4,4,4096]{2,1,0:T(4,128)(2,1)S(1)}, bf16[4,4,4096]{2,1,0:T(4,128)(2,1)S(1)}, u32[]{:S(2)}, u32[]{:S(2)}) collective-permute-start(bf16[4,4,4096]{2,1,0:T(4,128)(2,1)S(1)} %get-tuple-element.9), channel_id=1, source_target_pairs={{0,192},{64,0},{128,64},{192,128},{1,193},{65,1},{129,65},{193,129... | collective-permute-start | bytes 393224 | tf_op jit(solution)/shard_map/ppermute | solution.py:270
  41.6 4.5 %collective-permute-start.3 = (bf16[4,32,128]{2,1,0:T(8,128)(2,1)}, bf16[4,32,128]{2,1,0:T(8,128)(2,1)S(1)}, u32[]{:S(2)}, u32[]{:S(2)}) collective-permute-start(bf16[4,32,128]{2,1,0:T(8,128)(2,1)} %cloud.1.w0), channel_id=1, source_target_pairs={{0,64},{64,128},{128,192},{192,0},{1,65},{65,129},{129,193},{193,1... | collective-permute-start | bytes 98312 | tf_op jit(solution)/shard_map/ppermute | solution.py:306
  42.7 4.8 %collective-permute-start.4 = (bf16[4,32,128]{2,1,0:T(8,128)(2,1)}, bf16[4,32,128]{2,1,0:T(8,128)(2,1)S(1)}, u32[]{:S(2)}, u32[]{:S(2)}) collective-permute-start(bf16[4,32,128]{2,1,0:T(8,128)(2,1)} %cloud.1.w0), channel_id=1, source_target_pairs={{0,128},{64,192},{128,0},{192,64},{1,129},{65,193},{129,1},{193,65... | collective-permute-start | bytes 98312 | tf_op jit(solution)/shard_map/ppermute | solution.py:306
  44.9 3.3 %collective-permute-start.5 = (bf16[4,32,128]{2,1,0:T(8,128)(2,1)}, bf16[4,32,128]{2,1,0:T(8,128)(2,1)S(1)}, u32[]{:S(2)}, u32[]{:S(2)}) collective-permute-start(bf16[4,32,128]{2,1,0:T(8,128)(2,1)} %cloud.1.w0), channel_id=1, source_target_pairs={{0,192},{64,0},{128,64},{192,128},{1,193},{65,1},{129,65},{193,129... | collective-permute-start | bytes 98312 | tf_op jit(solution)/shard_map/ppermute | solution.py:306
  46.1 2.6 %copy-start.6 = (bf16[4,32,128]{2,1,0:T(8,128)(2,1)}, bf16[4,32,128]{2,1,0:T(8,128)(2,1)S(1)}, u32[]{:S(2)}) copy-start(bf16[4,32,128]{2,1,0:T(8,128)(2,1)S(1)} %collective-permute-done.3.w1) | copy-start | bytes 98308
  47.5 1.2 %copy-start.7 = (bf16[4,32,128]{2,1,0:T(8,128)(2,1)}, bf16[4,32,128]{2,1,0:T(8,128)(2,1)S(1)}, u32[]{:S(2)}) copy-start(bf16[4,32,128]{2,1,0:T(8,128)(2,1)S(1)} %collective-permute-done.4.w2) | copy-start | bytes 98308
  48.1 0.6 copy-start.8
  71.3 24.5 %copy-start = (bf16[64,64,256]{2,1,0:T(8,128)(2,1)}, bf16[64,64,256]{2,1,0:T(8,128)(2,1)S(1)}, u32[]{:S(2)}) copy-start(bf16[64,64,256]{2,1,0:T(8,128)(2,1)S(1)} %all-to-all-done.first_ref) | copy-start | bytes 6291460
  106.4 16.6 %all-to-all-start.2 = ((f32[64,4,128]{2,1,0:T(4,128)}), f32[64,4,128]{2,1,0:T(4,128)S(1)}, u32[]{:S(2)}, u32[]{:S(2)}) async-start(f32[64,4,128]{2,1,0:T(4,128)} %merge.1), calls=%async_computation.2 | async-start | bytes 262144 | tf_op jit(solution)/shard_map/all_to_all | solution.py:349

commit v5 on v4

--- a/solution.py
+++ b/solution.py
@@ -70,18 +70,14 @@
         out_ref[:, :, v * 128 : (v + 1) * 128] = scratch[v].reshape(SIDE, 16, 128).astype(BF16)
 
 
-def weight_kernel(
-    band_ref, w0, w1, w2, w3, id_ref, col_ref, row_ref, spread_ref, spread1_ref, out_ref, scratch
-):
-    turn = pl.program_id(0)
-    place = 2 * ((band_ref[0] + 4 - turn) % 4)
+def weight_kernel(place_ref, w_ref, id_ref, col_ref, row_ref, spread_ref, spread1_ref, *rest):
+    outs, scratch = rest[:-1], rest[-1]
     mask = parity_mask(256)
     mask1 = parity_mask(SIDE)
     spread = spread_ref[...]
     spread1 = spread1_ref[...]
     group = range(4)
-    w = jnp.where(turn < 2, jnp.where(turn < 1, w0[...], w1[...]), jnp.where(turn < 3, w2[...], w3[...]))
-    planes = [jnp.where(mask1, dot(spread1, w[s]), 0.0).astype(BF16) for s in group]
+    planes = [jnp.where(mask1, dot(spread1, w_ref[s]), 0.0).astype(BF16) for s in group]
     wide = [dot(spread, jnp.concatenate([col_ref[s], row_ref[s]], 1)) for s in group]
     pairs = [spread_pair(x, mask) for x in wide]
     halves = [dot(planes[s], pairs[s][0], ((1,), (1,))) for s in group]
@@ -94,12 +90,28 @@
         for v in range(2):
             pair = jnp.concatenate(parts[2 * v : 2 * v + 2], 1)
             scratch[v, pl.ds(s, SIDE, stride=4), :] = pair
-    for v in range(2):
-        out_ref[:, place + v] = scratch[v].reshape(SIDE, 4, 128).astype(BF16)
-
-    @pl.when(turn == 0)
-    def _():
-        out_ref[:, 8] = jnp.broadcast_to(id_ref[...].astype(BF16)[None], (SIDE, 4, 128))
+    ids = jnp.broadcast_to(id_ref[...].astype(BF16)[None], (8, 4, 128))
+    for turn, out_ref in enumerate(outs):
+        z = (place_ref[1] + turn) % 8
+        for y in range(4):
+            for v in range(2):
+                line = scratch[v, pl.ds(pl.multiple_of(64 * y + 8 * z, 8), 8), :]
+                out_ref[2 * y : 2 * y + 2, v] = line.reshape(2, 4, 128).astype(BF16)
+        out_ref[:, 2] = ids
+
+
+def stack_kernel(place_ref, *rest):
+    parts, out_ref, ids = rest[:8], rest[8], rest[9]
+    for turn, part in enumerate(parts):
+        z = (place_ref[1] + 8 - turn) % 8
+        for b in range(4):
+            for v in range(2):
+                out_ref[:, b, pl.ds(8 * v + z, 1)] = part[:, v : v + 1]
+        ids[pl.ds(z, 1)] = jnp.broadcast_to(part[0, 2].astype(F32)[:1][None], (1, 8, 128))
+    lines = jnp.concatenate([ids[z, :1] for z in range(8)], 0)
+    lines = jnp.broadcast_to(lines.reshape(1, 2, 4, 128), (8, 2, 4, 128)).astype(BF16)
+    for b in range(4):
+        out_ref[:, b, 16:18] = lines
 
 
 def after_kernel(x_ref, first_ref, out_ref):
@@ -129,21 +141,25 @@
     chunk = 512
     lane = lax.broadcasted_iota(jnp.int32, (1, 128), 1)
     tile = (lax.broadcasted_iota(jnp.int32, (128, 128), 0) & 63).astype(F32)
-    ids = w_ref[:, 8].astype(F32)[:, 0, :]
-    turned = pltpu.roll(ids, 64, 1)
+    ids = w_ref[:, 0, 16:18].astype(F32).reshape(8, 8, 128)
+    turned = pltpu.roll(ids, 64, 2)
     for i in range(entries // 128):
         span = slice(i * 128, (i + 1) * 128)
-        pair = jnp.where(lane < 64, ids[2 * i : 2 * i + 1], turned[2 * i + 1 : 2 * i + 2])
+        y, z = i // 8, i % 8
+        pair = jnp.where(lane < 64, ids[2 * y, z : z + 1], turned[2 * y + 1, z : z + 1])
         hit = jnp.where(pair == tile, 1.0, 0.0)
         pick[:, span] = hit[:SIDE].astype(BF16)
         pick_t[span, :] = hit.T.astype(BF16)
-    for i in range(8):
-        w = dot(w_ref[:, i].reshape(entries // 16, 128), double_ref[...])
-        for half in range(2):
-            first = 8 * i + 4 * half
-            weight[:, first : first + 4, :] = w[:, half * 128 : (half + 1) * 128].reshape(
-                entries // SIDE, 4, 128
-            )
+    for b in range(4):
+        for v in range(2):
+            w = w_ref[:, b, 8 * v : 8 * v + 8].reshape(entries // 16, 128)
+            w = dot(w, double_ref[...])
+            for half in range(2):
+                first = 16 * b + 8 * v + 4 * half
+                part = w[:, half * 128 : (half + 1) * 128].reshape(4, 2, 8, 4, 128)
+                for y in range(4):
+                    for c in range(2):
+                        weight[y, :, c, first : first + 4, :] = part[y, c]
     fetch.wait()
 
     def totals(estimate):
@@ -160,7 +176,7 @@
         ahead = expected(spans[0])
         for i, span in enumerate(spans):
             here, ahead = ahead, expected(spans[i + 1]) if i + 1 < len(spans) else None
-            w = weight[i * chunk // SIDE : (i + 1) * chunk // SIDE].reshape(chunk, 128)
+            w = weight[i // 2, 4 * (i % 2) : 4 * (i % 2) + 4].reshape(chunk, 128)
             y = y_ref[span, :]
             h = jnp.concatenate([w, w], 1)
             if estimate is not None:
@@ -302,25 +318,40 @@
     )
     ids = intersections.reshape(groups, share, 4).transpose(0, 2, 1).reshape(1, scenes * 4)
     ids = jnp.broadcast_to(jnp.pad(ids, ((0, 0), (0, 128 - scenes * 4))).astype(F32), (4, 128))
-    all_weights = [weights] + [
-        lax.ppermute(weights, "band", [(i, (i + turn) % groups) for i in range(groups)])
-        for turn in range(1, groups)
-    ]
-    theirs = pl.BlockSpec((4, 128, 128), lambda i, b: ((b[0] + 4 - i) % 4, 0, 0))
-    moved_weights = pl.pallas_call(
+    tile = lax.axis_index("tile")
+    place = jnp.stack([band, (tile // 2) % 8]).astype(jnp.int32)
+    mine = pl.BlockSpec((4, 128, 128), lambda i, place: (place[0], 0, 0))
+    pieces = pl.pallas_call(
         weight_kernel,
         grid_spec=pltpu.PrefetchScalarGridSpec(
             num_scalar_prefetch=1,
-            grid=(groups,),
-            in_specs=[whole((share, SIDE // 2, 128))] * groups
-            + [whole((4, 128)), theirs, theirs, whole((256, 128)), whole((SIDE, SIDE // 2))],
-            out_specs=whole((SIDE, 9, share, 128)),
+            grid=(1,),
+            in_specs=[
+                whole((share, SIDE // 2, 128)),
+                whole((4, 128)),
+                mine,
+                mine,
+                whole((256, 128)),
+                whole((SIDE, SIDE // 2)),
+            ],
+            out_specs=[whole((8, 3, share, 128))] * 8,
             scratch_shapes=[pltpu.VMEM((2, SIDE * share, 128), F32)],
         ),
-        out_shape=jax.ShapeDtypeStruct((SIDE, 9, share, 128), BF16),
-        cost_estimate=pl.CostEstimate(flops=8 * 10**9, transcendentals=0, bytes_accessed=10**6),
+        out_shape=[jax.ShapeDtypeStruct((8, 3, share, 128), BF16)] * 8,
+        cost_estimate=pl.CostEstimate(flops=3 * 10**9, transcendentals=0, bytes_accessed=10**6),
         name="reproject_weights",
-    )(band.astype(jnp.int32).reshape(1), *all_weights, ids, cols, rows, spread, spread1)
+    )(place, weights, ids, cols, rows, spread, spread1)
+    along_z = [
+        [(t, t // 16 * 16 + (t // 2 + turn) % 8 * 2 + t % 2) for t in range(tiles)] for turn in range(8)
+    ]
+    pieces = [pieces[0]] + [lax.ppermute(pieces[t], "tile", along_z[t]) for t in range(1, 8)]
+    moved_weights = pl.pallas_call(
+        stack_kernel,
+        in_specs=[pl.BlockSpec(memory_space=pltpu.SMEM)] + [in_vmem] * 8,
+        out_shape=jax.ShapeDtypeStruct((8, groups, 18, share, 128), BF16),
+        scratch_shapes=[pltpu.VMEM((8, 8, 128), F32)],
+        name="stack",
+    )(place, *map(keep, pieces))
     anywhere = pl.BlockSpec(memory_space=pl.ANY)
     moved_weights = pl.pallas_call(
         after_kernel,
@@ -330,7 +361,17 @@
         input_output_aliases={0: 0},
         name="after",
     )(moved_weights, keep(values))
-    moved_weights = lax.all_to_all(moved_weights, "tile", split_axis=0, concat_axis=0)
+    same_z = [
+        [(16 * y + 2 * z + c) * groups + b for y in range(4) for c in range(2) for b in range(groups)]
+        for z in range(8)
+    ]
+    moved_weights = lax.all_to_all(
+        moved_weights.reshape(8 * groups, 18, share, 128),
+        ("tile", "band"),
+        split_axis=0,
+        concat_axis=0,
+        axis_index_groups=same_z,
+    ).reshape(8, groups, 18, share, 128)
 
     entries = tiles * scenes * 4
     estimate = pl.pallas_call(
@@ -341,14 +382,14 @@
             pltpu.VMEM((entries, 256), BF16),
             pltpu.VMEM((SIDE, entries), BF16),
             pltpu.VMEM((entries, 128), BF16),
-            pltpu.VMEM((tiles, SIDE, 128), F32),
+            pltpu.VMEM((4, 8, 2, SIDE, 128), F32),
             pltpu.SemaphoreType.DMA,
         ],
         name="merge",
     )(values.reshape(entries, 256), keep(moved_weights), jnp.asarray(double_matrix(), BF16))
     field = lax.all_to_all(estimate, "tile", split_axis=0, concat_axis=0)
 
-    place = jnp.stack([lax.axis_index("tile"), tiles]).astype(jnp.int32)
+    place = jnp.stack([tile, tiles]).astype(jnp.int32)
     out = pl.pallas_call(
         smooth_kernel,
         in_specs=[pl.BlockSpec(memory_space=pltpu.SMEM), in_vmem],

time: 125 us -> 128 us (1.024)
  starting transfers between devices: 28.7 us -> 39.3 us
  waiting for transfers between devices: 30.3 us -> 25.2 us
  blocking collectives: 24.5 us -> 20 us
  other arithmetic: 2.11 us -> 3.43 us
    all_to_all x1, waiting for transfers between devices: 17 us -> 0.01 us  [per_device(): values = lax.all_to_all(moved, 'tile', split_axis=0, concat_axis=0)]
    ppermute x3 -> x7, waiting for transfers between devices: 2.34 us -> 15.4 us  [per_device(): lax.ppermute(pieces[t], 'tile', along_z[t])]
    ppermute x3 -> x7, starting transfers between devices: 4.17 us -> 14.6 us  [per_device(): lax.ppermute(pieces[t], 'tile', along_z[t])]
    all_to_all x1, blocking collectives: 24.5 us -> 20 us  [per_device(): lax.all_to_all(moved_weights.reshape(8 * groups, 18, share, 128), ('tile'...]
    pallas_call x1, Pallas kernels: 5.49 us -> 3.16 us  [per_device(): pl.pallas_call(weight_kernel, grid_spec=pltpu.PrefetchScalarGridSpec(num_...]
    pallas_call x0 -> x1, Pallas kernels: none -> 1.66 us  [per_device(): pl.pallas_call(stack_kernel, in_specs=[pl.BlockSpec(memory_space=pltpu.SM...]
  transfers between devices with their start and end apart: 8 -> 12, of which waited for: 6 -> 4; matrix products, arithmetic and copies ran while one was open for 4% -> 5% of each run, Pallas kernels for 13% -> 12%
where the time goes in v5:
time: 128 us; the launch traced here: 127 us
  starting transfers between devices  39.3 us (31%)
  Pallas kernels  34.8 us (27%)
  waiting for transfers between devices  25.2 us (20%)
  blocking collectives  20 us (16%)
  local copies, waits for them, and re-layouts  4.15 us (3%)
  other arithmetic  3.43 us (3%)
    all_to_all x1, blocking collectives, per_device(): lax.all_to_all(moved_weights.reshape(8 * groups, 18, share, 128), ('tile'...  20 us
    ppermute x7, waiting for transfers between devices, per_device(): lax.ppermute(pieces[t], 'tile', along_z[t])  15.4 us
    ppermute x7, starting transfers between devices, per_device(): lax.ppermute(pieces[t], 'tile', along_z[t])  14.6 us
    all_to_all x1, starting transfers between devices, per_device(): values = lax.all_to_all(moved, 'tile', split_axis=0, concat_axis=0)  13.3 us
    pallas_call x1, Pallas kernels, per_device(): pl.pallas_call(cloud_kernel, grid=(share, pixels // width), in_specs=[in_...  11 us
    pallas_call x1, Pallas kernels, per_device(): pl.pallas_call(merge_kernel, in_specs=[anywhere, in_vmem, in_vmem], out_s...  10.6 us
    all_to_all x1, waiting for transfers between devices, per_device(): field = lax.all_to_all(estimate, 'tile', split_axis=0, concat_axis=0)  9.77 us
    pallas_call x1, Pallas kernels, per_device(): pl.pallas_call(reproject_kernel, grid=(4,), in_specs=[scene_block, scene_...  6.68 us
  transfers between devices with their start and end apart: 12, of which 4 were waited for; matrix products, arithmetic and copies ran while one was open for 5% of the time, Pallas kernels for 12%

profile of v5, /device:TPU:1, one launch (start us, length us, event | category | flops | bytes accessed | tf_op | source)
XLA Modules:
  0.0 127.0 jit_solution(11062800916075423557)
XLA Ops:
  0.0 6.7 %reproject.1 = bf16[64,64,256]{2,1,0:T(8,128)(2,1)} custom-call(bf16[16,128,128]{2,1,0:T(8,128)(2,1)} %bitcast.52, bf16[16,128,128]{2,1,0:T(8,128)(2,1)} %bitcast.54, bf16[16,128,128]{2,1,0:T(8,128)(2,1)} %bitcast.56, bf16[256,128]{1,0:T(8,128)(2,1)} %constant.121.clone.spread_ref), custom_call_target="tpu_custom_call" | custom-call | tf_op jit(solution)/shard_map/reproject/pallas_call | solution.py:267
  6.7 13.3 %all-to-all-start = ((bf16[64,64,256]{2,1,0:T(8,128)(2,1)}), bf16[64,64,256]{2,1,0:T(8,128)(2,1)S(1)}, u32[]{:S(2)}, u32[]{:S(2)}) async-start(bf16[64,64,256]{2,1,0:T(8,128)(2,1)} %reproject.1), calls=%async_computation | async-start | bytes 4194304 | tf_op jit(solution)/shard_map/all_to_all | solution.py:277
  20.3 1.3 %collective-permute-start = (bf16[4,4,4096]{2,1,0:T(4,128)(2,1)S(1)}, bf16[4,4,4096]{2,1,0:T(4,128)(2,1)S(1)}, u32[]{:S(2)}, u32[]{:S(2)}) collective-permute-start(bf16[4,4,4096]{2,1,0:T(4,128)(2,1)S(1)} %get-tuple-element.27), channel_id=1, source_target_pairs={{0,64},{64,128},{128,192},{192,0},{1,65},{65,129},{129,193},{193,1... | collective-permute-start | bytes 393224 | tf_op jit(solution)/shard_map/ppermute | solution.py:286
  21.6 2.5 %collective-permute-start.1 = (bf16[4,4,4096]{2,1,0:T(4,128)(2,1)S(1)}, bf16[4,4,4096]{2,1,0:T(4,128)(2,1)S(1)}, u32[]{:S(2)}, u32[]{:S(2)}) collective-permute-start(bf16[4,4,4096]{2,1,0:T(4,128)(2,1)S(1)} %get-tuple-element.26), channel_id=1, source_target_pairs={{0,128},{64,192},{128,0},{192,64},{1,129},{65,193},{129,1},{193,65... | collective-permute-start | bytes 393224 | tf_op jit(solution)/shard_map/ppermute | solution.py:286
  24.1 1.2 collective-permute-start.2
  26.4 0.8 fusion.1
  28.0 0.8 reshape.56.factor_ref
  30.7 11.0 %cloud.1.w_ref = bf16[4,32,128]{2,1,0:T(8,128)(2,1)} custom-call(bf16[4,4,4096]{2,1,0:T(4,128)(2,1)S(1)} %get-tuple-element.28.x0, bf16[4,4,4096]{2,1,0:T(4,128)(2,1)S(1)} %collective-permute-done.x1, bf16[4,4,4096]{2,1,0:T(4,128)(2,1)S(1)} %collective-permute-done.1.x2, bf16[4,4,4096]{2,1,0:T(4,128)(2,1)S(1)} %collective-permute-done.2.x3, ...), custom_call_target="tpu_custom_call" | custom-call | flops 12000000000 | bytes 1000000 | tf_op jit(solution)/shard_map/cloud/pallas_call | solution.py:298
  42.3 3.2 %reproject_weights.1 = (bf16[8,3,4,128]{3,2,1,0:T(4,128)(2,1)}, bf16[8,3,4,128]{3,2,1,0:T(4,128)(2,1)}, bf16[8,3,4,128]{3,2,1,0:T(4,128)(2,1)}, bf16[8,3,4,128]{...) custom-call(s32[2]{0:T(128)} %pad_add_fusion.1.place_ref, ...), custom_call_target="tpu_custom_call" | custom-call | flops 3000000000 | bytes 1000000 | tf_op jit(solution)/shard_map/reproject_weights/pallas_call | solution.py:324
  45.4 1.5 %collective-permute-start.3 = (bf16[8,3,4,128]{3,2,1,0:T(4,128)(2,1)}, bf16[8,3,4,128]{3,2,1,0:T(4,128)(2,1)S(1)}, u32[]{:S(2)}, u32[]{:S(2)}) collective-permute-start(bf16[8,3,4,128]{3,2,1,0:T(4,128)(2,1)} %get-tuple-element.18), channel_id=1, source_target_pairs={{0,2},{1,3},{2,4},{3,5},{4,6},{5,7},{6,8},{7,9},{8,10},{9,11},{10,... | collective-permute-start | bytes 73736 | tf_op jit(solution)/shard_map/ppermute | solution.py:347
  46.9 2.1 %collective-permute-start.4 = (bf16[8,3,4,128]{3,2,1,0:T(4,128)(2,1)}, bf16[8,3,4,128]{3,2,1,0:T(4,128)(2,1)S(1)}, u32[]{:S(2)}, u32[]{:S(2)}) collective-permute-start(bf16[8,3,4,128]{3,2,1,0:T(4,128)(2,1)} %get-tuple-element.19), channel_id=1, source_target_pairs={{0,4},{1,5},{2,6},{3,7},{4,8},{5,9},{6,10},{7,11},{8,12},{9,13},{1... | collective-permute-start | bytes 73736 | tf_op jit(solution)/shard_map/ppermute | solution.py:347
  49.0 2.4 %collective-permute-start.5 = (bf16[8,3,4,128]{3,2,1,0:T(4,128)(2,1)}, bf16[8,3,4,128]{3,2,1,0:T(4,128)(2,1)S(1)}, u32[]{:S(2)}, u32[]{:S(2)}) collective-permute-start(bf16[8,3,4,128]{3,2,1,0:T(4,128)(2,1)} %get-tuple-element.20), channel_id=1, source_target_pairs={{0,6},{1,7},{2,8},{3,9},{4,10},{5,11},{6,12},{7,13},{8,14},{9,15},... | collective-permute-start | bytes 73736 | tf_op jit(solution)/shard_map/ppermute | solution.py:347
  51.4 2.1 %collective-permute-start.6 = (bf16[8,3,4,128]{3,2,1,0:T(4,128)(2,1)}, bf16[8,3,4,128]{3,2,1,0:T(4,128)(2,1)S(1)}, u32[]{:S(2)}, u32[]{:S(2)}) collective-permute-start(bf16[8,3,4,128]{3,2,1,0:T(4,128)(2,1)} %get-tuple-element.21), channel_id=1, source_target_pairs={{0,8},{1,9},{2,10},{3,11},{4,12},{5,13},{6,14},{7,15},{8,0},{9,1},... | collective-permute-start | bytes 73736 | tf_op jit(solution)/shard_map/ppermute | solution.py:347
  53.5 2.4 %collective-permute-start.7 = (bf16[8,3,4,128]{3,2,1,0:T(4,128)(2,1)}, bf16[8,3,4,128]{3,2,1,0:T(4,128)(2,1)S(1)}, u32[]{:S(2)}, u32[]{:S(2)}) collective-permute-start(bf16[8,3,4,128]{3,2,1,0:T(4,128)(2,1)} %get-tuple-element.22), channel_id=1, source_target_pairs={{0,10},{1,11},{2,12},{3,13},{4,14},{5,15},{6,0},{7,1},{8,2},{9,3},... | collective-permute-start | bytes 73736 | tf_op jit(solution)/shard_map/ppermute | solution.py:347
  55.9 11.8 %collective-permute-done.3.rest_1_ = bf16[8,3,4,128]{3,2,1,0:T(4,128)(2,1)S(1)} collective-permute-done((bf16[8,3,4,128]{3,2,1,0:T(4,128)(2,1)}, bf16[8,3,4,128]{3,2,1,0:T(4,128)(2,1)S(1)}, u32[]{:S(2)}, u32[]{:S(2)}) %collective-permute-start.3) | collective-permute-done | bytes 24608 | tf_op jit(solution)/shard_map/ppermute | solution.py:347
  67.7 1.8 %collective-permute-start.8 = (bf16[8,3,4,128]{3,2,1,0:T(4,128)(2,1)}, bf16[8,3,4,128]{3,2,1,0:T(4,128)(2,1)S(1)}, u32[]{:S(2)}, u32[]{:S(2)}) collective-permute-start(bf16[8,3,4,128]{3,2,1,0:T(4,128)(2,1)} %get-tuple-element.23), channel_id=1, source_target_pairs={{0,12},{1,13},{2,14},{3,15},{4,0},{5,1},{6,2},{7,3},{8,4},{9,5},{1... | collective-permute-start | bytes 73736 | tf_op jit(solution)/shard_map/ppermute | solution.py:347
  70.1 2.3 %collective-permute-start.9 = (bf16[8,3,4,128]{3,2,1,0:T(4,128)(2,1)}, bf16[8,3,4,128]{3,2,1,0:T(4,128)(2,1)S(1)}, u32[]{:S(2)}, u32[]{:S(2)}) collective-permute-start(bf16[8,3,4,128]{3,2,1,0:T(4,128)(2,1)} %get-tuple-element.24), channel_id=1, source_target_pairs={{0,14},{1,15},{2,0},{3,1},{4,2},{5,3},{6,4},{7,5},{8,6},{9,7},{10,... | collective-permute-start | bytes 73736 | tf_op jit(solution)/shard_map/ppermute | solution.py:347
  72.4 3.0 %collective-permute-done.6.rest_4_ = bf16[8,3,4,128]{3,2,1,0:T(4,128)(2,1)S(1)} collective-permute-done((bf16[8,3,4,128]{3,2,1,0:T(4,128)(2,1)}, bf16[8,3,4,128]{3,2,1,0:T(4,128)(2,1)S(1)}, u32[]{:S(2)}, u32[]{:S(2)}) %collective-permute-start.6) | collective-permute-done | bytes 24608 | tf_op jit(solution)/shard_map/ppermute | solution.py:347
  76.2 1.7 %stack.21.x_ref = bf16[8,4,18,4,128]{4,3,2,1,0:T(4,128)(2,1)} custom-call(s32[2]{0:T(128)} %pad_add_fusion.1.place_ref, bf16[8,3,4,128]{3,2,1,0:T(4,128)(2,1)S(1)} %copy-done.1, bf16[8,3,4,128]{3,2,1,0:T(4,128)(2,1)S(1)} %collective-permute-done.3.rest_1_, bf16[8,3,4,128]{3,2,1,0:T(4,128)(2,1)S(1)} %collective-permute-done.4.rest_2_, ...), custom_call_target="tpu_custom_call" | custom-call | tf_op jit(solution)/shard_map/stack/pallas_call | solution.py:348
  77.8 20.0 %all_to_all.15 = bf16[32,18,4,128]{3,2,1,0:T(4,128)(2,1)S(1)} all-to-all(bf16[32,18,4,128]{3,2,1,0:T(4,128)(2,1)} %bitcast.51), channel_id=1, replica_groups={{0,64,128,192,1,65,129,193,16,80,144,208,17,81,145,209,32,96,160,224,33..., dimensions={0} | all-to-all | bytes 1179648 | tf_op jit(solution)/shard_map/all_to_all | solution.py:368
  97.8 10.6 %merge.1 = f32[64,4,128]{2,1,0:T(4,128)} custom-call(bf16[4096,256]{1,0:T(8,128)(2,1)} %bitcast.49, bf16[8,4,18,4,128]{4,3,2,1,0:T(4,128)(2,1)S(1)} %bitcast.50, bf16[128,256]{1,0:T(8,128)(2,1)} %constant.123.clone.double_ref), custom_call_target="tpu_custom_call" | custom-call | tf_op jit(solution)/shard_map/merge/pallas_call | solution.py:377
  108.4 6.5 %all-to-all-start.2 = ((f32[64,4,128]{2,1,0:T(4,128)}), f32[64,4,128]{2,1,0:T(4,128)S(1)}, u32[]{:S(2)}, u32[]{:S(2)}) async-start(f32[64,4,128]{2,1,0:T(4,128)} %merge.1), calls=%async_computation.2 | async-start | bytes 262144 | tf_op jit(solution)/shard_map/all_to_all | solution.py:390
  115.5 9.8 %all-to-all-done.2.g_ref = f32[64,4,128]{2,1,0:T(4,128)S(1)} async-done(((f32[64,4,128]{2,1,0:T(4,128)}), f32[64,4,128]{2,1,0:T(4,128)S(1)}, u32[]{:S(2)}, u32[]{:S(2)}) %all-to-all-start.2) | async-done | bytes 131104 | tf_op jit(solution)/shard_map/all_to_all | solution.py:390
  125.3 1.8 %smooth.1 = f32[32,4,128]{2,1,0:T(4,128)} custom-call(s32[2]{0:T(128)} %pad_add_fusion.tile_ref, f32[64,4,128]{2,1,0:T(4,128)S(1)} %all-to-all-done.2.g_ref), custom_call_target="tpu_custom_call" | custom-call | tf_op jit(solution)/shard_map/smooth/pallas_call | solution.py:393
  (42 shorter events, 6.7 us)
Async XLA Ops:
  6.7 13.4 %copy-start.2 = (bf16[16,4,4096]{2,1,0:T(4,128)(2,1)S(1)}, bf16[16,4,4096]{2,1,0:T(4,128)(2,1)}, u32[]{:S(2)}) copy-start(bf16[16,4,4096]{2,1,0:T(4,128)(2,1)} %param.12) | copy-start | bytes 1572868
  6.7 18.6 %copy-start.4 = (bf16[16,256]{1,0:T(8,128)(2,1)S(1)}, bf16[16,256]{1,0:T(8,128)(2,1)}, u32[]{:S(2)}) copy-start(bf16[16,256]{1,0:T(8,128)(2,1)} %param.18) | copy-start | bytes 24580
  6.7 18.6 %copy-start.3 = (bf16[2,256,256]{2,1,0:T(8,128)(2,1)S(1)}, bf16[2,256,256]{2,1,0:T(8,128)(2,1)}, u32[]{:S(2)}) copy-start(bf16[2,256,256]{2,1,0:T(8,128)(2,1)} %param.19) | copy-start | bytes 786436
  6.7 18.7 %copy-start.5 = (s32[16,4]{0,1:T(4,128)S(1)}, s32[16,4]{0,1:T(4,128)}, u32[]{:S(2)}) copy-start(s32[16,4]{0,1:T(4,128)} %param.15) | copy-start | bytes 772
  6.7 71.1 %all-to-all-start = ((bf16[64,64,256]{2,1,0:T(8,128)(2,1)}), bf16[64,64,256]{2,1,0:T(8,128)(2,1)S(1)}, u32[]{:S(2)}, u32[]{:S(2)}) async-start(bf16[64,64,256]{2,1,0:T(8,128)(2,1)} %reproject.1), calls=%async_computation | async-start | bytes 4194304 | tf_op jit(solution)/shard_map/all_to_all | solution.py:277
  20.0 10.1 %copy-start.6 = (bf16[256]{0:T(256)(128)(2,1)S(1)}, bf16[256]{0:T(256)(128)(2,1)}, u32[]{:S(2)}) copy-start(bf16[256]{0:T(256)(128)(2,1)} %param.20) | copy-start | bytes 1540
  20.3 9.8 %collective-permute-start = (bf16[4,4,4096]{2,1,0:T(4,128)(2,1)S(1)}, bf16[4,4,4096]{2,1,0:T(4,128)(2,1)S(1)}, u32[]{:S(2)}, u32[]{:S(2)}) collective-permute-start(bf16[4,4,4096]{2,1,0:T(4,128)(2,1)S(1)} %get-tuple-element.27), channel_id=1, source_target_pairs={{0,64},{64,128},{128,192},{192,0},{1,65},{65,129},{129,193},{193,1... | collective-permute-start | bytes 393224 | tf_op jit(solution)/shard_map/ppermute | solution.py:286
  21.6 8.5 %collective-permute-start.1 = (bf16[4,4,4096]{2,1,0:T(4,128)(2,1)S(1)}, bf16[4,4,4096]{2,1,0:T(4,128)(2,1)S(1)}, u32[]{:S(2)}, u32[]{:S(2)}) collective-permute-start(bf16[4,4,4096]{2,1,0:T(4,128)(2,1)S(1)} %get-tuple-element.26), channel_id=1, source_target_pairs={{0,128},{64,192},{128,0},{192,64},{1,129},{65,193},{129,1},{193,65... | collective-permute-start | bytes 393224 | tf_op jit(solution)/shard_map/ppermute | solution.py:286
  24.1 6.0 %collective-permute-start.2 = (bf16[4,4,4096]{2,1,0:T(4,128)(2,1)S(1)}, bf16[4,4,4096]{2,1,0:T(4,128)(2,1)S(1)}, u32[]{:S(2)}, u32[]{:S(2)}) collective-permute-start(bf16[4,4,4096]{2,1,0:T(4,128)(2,1)S(1)} %get-tuple-element.25), channel_id=1, source_target_pairs={{0,192},{64,0},{128,64},{192,128},{1,193},{65,1},{129,65},{193,129... | collective-permute-start | bytes 393224 | tf_op jit(solution)/shard_map/ppermute | solution.py:286
  45.4 22.2 %collective-permute-start.3 = (bf16[8,3,4,128]{3,2,1,0:T(4,128)(2,1)}, bf16[8,3,4,128]{3,2,1,0:T(4,128)(2,1)S(1)}, u32[]{:S(2)}, u32[]{:S(2)}) collective-permute-start(bf16[8,3,4,128]{3,2,1,0:T(4,128)(2,1)} %get-tuple-element.18), channel_id=1, source_target_pairs={{0,2},{1,3},{2,4},{3,5},{4,6},{5,7},{6,8},{7,9},{8,10},{9,11},{10,... | collective-permute-start | bytes 73736 | tf_op jit(solution)/shard_map/ppermute | solution.py:347
  46.9 23.2 %collective-permute-start.4 = (bf16[8,3,4,128]{3,2,1,0:T(4,128)(2,1)}, bf16[8,3,4,128]{3,2,1,0:T(4,128)(2,1)S(1)}, u32[]{:S(2)}, u32[]{:S(2)}) collective-permute-start(bf16[8,3,4,128]{3,2,1,0:T(4,128)(2,1)} %get-tuple-element.19), channel_id=1, source_target_pairs={{0,4},{1,5},{2,6},{3,7},{4,8},{5,9},{6,10},{7,11},{8,12},{9,13},{1... | collective-permute-start | bytes 73736 | tf_op jit(solution)/shard_map/ppermute | solution.py:347
  49.0 23.4 %collective-permute-start.5 = (bf16[8,3,4,128]{3,2,1,0:T(4,128)(2,1)}, bf16[8,3,4,128]{3,2,1,0:T(4,128)(2,1)S(1)}, u32[]{:S(2)}, u32[]{:S(2)}) collective-permute-start(bf16[8,3,4,128]{3,2,1,0:T(4,128)(2,1)} %get-tuple-element.20), channel_id=1, source_target_pairs={{0,6},{1,7},{2,8},{3,9},{4,10},{5,11},{6,12},{7,13},{8,14},{9,15},... | collective-permute-start | bytes 73736 | tf_op jit(solution)/shard_map/ppermute | solution.py:347
  51.4 24.0 %collective-permute-start.6 = (bf16[8,3,4,128]{3,2,1,0:T(4,128)(2,1)}, bf16[8,3,4,128]{3,2,1,0:T(4,128)(2,1)S(1)}, u32[]{:S(2)}, u32[]{:S(2)}) collective-permute-start(bf16[8,3,4,128]{3,2,1,0:T(4,128)(2,1)} %get-tuple-element.21), channel_id=1, source_target_pairs={{0,8},{1,9},{2,10},{3,11},{4,12},{5,13},{6,14},{7,15},{8,0},{9,1},... | collective-permute-start | bytes 73736 | tf_op jit(solution)/shard_map/ppermute | solution.py:347
  53.5 21.9 %collective-permute-start.7 = (bf16[8,3,4,128]{3,2,1,0:T(4,128)(2,1)}, bf16[8,3,4,128]{3,2,1,0:T(4,128)(2,1)S(1)}, u32[]{:S(2)}, u32[]{:S(2)}) collective-permute-start(bf16[8,3,4,128]{3,2,1,0:T(4,128)(2,1)} %get-tuple-element.22), channel_id=1, source_target_pairs={{0,10},{1,11},{2,12},{3,13},{4,14},{5,15},{6,0},{7,1},{8,2},{9,3},... | collective-permute-start | bytes 73736 | tf_op jit(solution)/shard_map/ppermute | solution.py:347
  67.7 7.7 %collective-permute-start.8 = (bf16[8,3,4,128]{3,2,1,0:T(4,128)(2,1)}, bf16[8,3,4,128]{3,2,1,0:T(4,128)(2,1)S(1)}, u32[]{:S(2)}, u32[]{:S(2)}) collective-permute-start(bf16[8,3,4,128]{3,2,1,0:T(4,128)(2,1)} %get-tuple-element.23), channel_id=1, source_target_pairs={{0,12},{1,13},{2,14},{3,15},{4,0},{5,1},{6,2},{7,3},{8,4},{9,5},{1... | collective-permute-start | bytes 73736 | tf_op jit(solution)/shard_map/ppermute | solution.py:347
  70.1 5.3 %collective-permute-start.9 = (bf16[8,3,4,128]{3,2,1,0:T(4,128)(2,1)}, bf16[8,3,4,128]{3,2,1,0:T(4,128)(2,1)S(1)}, u32[]{:S(2)}, u32[]{:S(2)}) collective-permute-start(bf16[8,3,4,128]{3,2,1,0:T(4,128)(2,1)} %get-tuple-element.24), channel_id=1, source_target_pairs={{0,14},{1,15},{2,0},{3,1},{4,2},{5,3},{6,4},{7,5},{8,6},{9,7},{10,... | collective-permute-start | bytes 73736 | tf_op jit(solution)/shard_map/ppermute | solution.py:347
  75.4 0.7 copy-start.1
  77.8 20.0 %copy-start = (bf16[64,64,256]{2,1,0:T(8,128)(2,1)}, bf16[64,64,256]{2,1,0:T(8,128)(2,1)S(1)}, u32[]{:S(2)}) copy-start(bf16[64,64,256]{2,1,0:T(8,128)(2,1)S(1)} %all-to-all-done.first_ref) | copy-start | bytes 6291460
  108.4 16.9 %all-to-all-start.2 = ((f32[64,4,128]{2,1,0:T(4,128)}), f32[64,4,128]{2,1,0:T(4,128)S(1)}, u32[]{:S(2)}, u32[]{:S(2)}) async-start(f32[64,4,128]{2,1,0:T(4,128)} %merge.1), calls=%async_computation.2 | async-start | bytes 262144 | tf_op jit(solution)/shard_map/all_to_all | solution.py:390

commit v6 on v5

--- a/solution.py
+++ b/solution.py
@@ -90,32 +90,31 @@
         for v in range(2):
             pair = jnp.concatenate(parts[2 * v : 2 * v + 2], 1)
             scratch[v, pl.ds(s, SIDE, stride=4), :] = pair
-    ids = jnp.broadcast_to(id_ref[...].astype(BF16)[None], (8, 4, 128))
+    ids = jnp.broadcast_to(id_ref[...].astype(BF16)[None], (16, 4, 128))
     for turn, out_ref in enumerate(outs):
-        z = (place_ref[1] + turn) % 8
+        pair = (place_ref[1] + turn) % 4
         for y in range(4):
             for v in range(2):
-                line = scratch[v, pl.ds(pl.multiple_of(64 * y + 8 * z, 8), 8), :]
-                out_ref[2 * y : 2 * y + 2, v] = line.reshape(2, 4, 128).astype(BF16)
+                line = scratch[v, pl.ds(pl.multiple_of(64 * y + 16 * pair, 16), 16), :]
+                out_ref[4 * y : 4 * y + 4, v] = line.reshape(4, 4, 128).astype(BF16)
         out_ref[:, 2] = ids
 
 
-def stack_kernel(place_ref, *rest):
-    parts, out_ref, ids = rest[:8], rest[8], rest[9]
-    for turn, part in enumerate(parts):
-        z = (place_ref[1] + 8 - turn) % 8
+def after_kernel(x_ref, first_ref, out_ref):
+    pass
+
+
+def stack_kernel(place_ref, p0, p1, p2, p3, out_ref, ids):
+    for turn, part in enumerate((p0, p1, p2, p3)):
+        pair = (place_ref[1] + 4 - turn) % 4
         for b in range(4):
             for v in range(2):
-                out_ref[:, b, pl.ds(8 * v + z, 1)] = part[:, v : v + 1]
-        ids[pl.ds(z, 1)] = jnp.broadcast_to(part[0, 2].astype(F32)[:1][None], (1, 8, 128))
-    lines = jnp.concatenate([ids[z, :1] for z in range(8)], 0)
-    lines = jnp.broadcast_to(lines.reshape(1, 2, 4, 128), (8, 2, 4, 128)).astype(BF16)
+                out_ref[:, b, pl.ds(4 * v + pair, 1)] = part[:, v : v + 1]
+        ids[pl.ds(pair, 1)] = jnp.broadcast_to(part[0, 2].astype(F32)[:1][None], (1, 8, 128))
+    lines = jnp.concatenate([ids[z, :1] for z in range(4)], 0)
+    lines = jnp.broadcast_to(lines[None], (16, 4, 128)).astype(BF16)
     for b in range(4):
-        out_ref[:, b, 16:18] = lines
-
-
-def after_kernel(x_ref, first_ref, out_ref):
-    pass
+        out_ref[:, b, 8] = lines
 
 
 def cloud_kernel(x0, x1, x2, x3, factor_ref, w_in_ref, w_hidden_ref, w_out_ref, out_ref):
@@ -141,25 +140,25 @@
     chunk = 512
     lane = lax.broadcasted_iota(jnp.int32, (1, 128), 1)
     tile = (lax.broadcasted_iota(jnp.int32, (128, 128), 0) & 63).astype(F32)
-    ids = w_ref[:, 0, 16:18].astype(F32).reshape(8, 8, 128)
+    ids = w_ref[:, 0, 8].astype(F32)
     turned = pltpu.roll(ids, 64, 2)
     for i in range(entries // 128):
         span = slice(i * 128, (i + 1) * 128)
-        y, z = i // 8, i % 8
-        pair = jnp.where(lane < 64, ids[2 * y, z : z + 1], turned[2 * y + 1, z : z + 1])
+        at, z = i // 8 * 4 + i % 2 * 2, i % 8 // 2
+        pair = jnp.where(lane < 64, ids[at, z : z + 1], turned[at + 1, z : z + 1])
         hit = jnp.where(pair == tile, 1.0, 0.0)
         pick[:, span] = hit[:SIDE].astype(BF16)
         pick_t[span, :] = hit.T.astype(BF16)
     for b in range(4):
         for v in range(2):
-            w = w_ref[:, b, 8 * v : 8 * v + 8].reshape(entries // 16, 128)
+            w = w_ref[:, b, 4 * v : 4 * v + 4].reshape(entries // 16, 128)
             w = dot(w, double_ref[...])
             for half in range(2):
                 first = 16 * b + 8 * v + 4 * half
-                part = w[:, half * 128 : (half + 1) * 128].reshape(4, 2, 8, 4, 128)
+                part = w[:, half * 128 : (half + 1) * 128].reshape(4, 4, 4, 4, 128)
                 for y in range(4):
-                    for c in range(2):
-                        weight[y, :, c, first : first + 4, :] = part[y, c]
+                    for low in range(4):
+                        weight[y, :, low, first : first + 4, :] = part[y, low]
     fetch.wait()
 
     def totals(estimate):
@@ -176,7 +175,7 @@
         ahead = expected(spans[0])
         for i, span in enumerate(spans):
             here, ahead = ahead, expected(spans[i + 1]) if i + 1 < len(spans) else None
-            w = weight[i // 2, 4 * (i % 2) : 4 * (i % 2) + 4].reshape(chunk, 128)
+            w = weight[i // 2, 2 * (i % 2) : 2 * (i % 2) + 2].reshape(chunk, 128)
             y = y_ref[span, :]
             h = jnp.concatenate([w, w], 1)
             if estimate is not None:
@@ -319,7 +318,7 @@
     ids = intersections.reshape(groups, share, 4).transpose(0, 2, 1).reshape(1, scenes * 4)
     ids = jnp.broadcast_to(jnp.pad(ids, ((0, 0), (0, 128 - scenes * 4))).astype(F32), (4, 128))
     tile = lax.axis_index("tile")
-    place = jnp.stack([band, (tile // 2) % 8]).astype(jnp.int32)
+    place = jnp.stack([band, (tile // 4) % 4]).astype(jnp.int32)
     mine = pl.BlockSpec((4, 128, 128), lambda i, place: (place[0], 0, 0))
     pieces = pl.pallas_call(
         weight_kernel,
@@ -334,25 +333,25 @@
                 whole((256, 128)),
                 whole((SIDE, SIDE // 2)),
             ],
-            out_specs=[whole((8, 3, share, 128))] * 8,
+            out_specs=[whole((16, 3, share, 128))] * 4,
             scratch_shapes=[pltpu.VMEM((2, SIDE * share, 128), F32)],
         ),
-        out_shape=[jax.ShapeDtypeStruct((8, 3, share, 128), BF16)] * 8,
+        out_shape=[jax.ShapeDtypeStruct((16, 3, share, 128), BF16)] * 4,
         cost_estimate=pl.CostEstimate(flops=3 * 10**9, transcendentals=0, bytes_accessed=10**6),
         name="reproject_weights",
     )(place, weights, ids, cols, rows, spread, spread1)
     along_z = [
-        [(t, t // 16 * 16 + (t // 2 + turn) % 8 * 2 + t % 2) for t in range(tiles)] for turn in range(8)
+        [(t, t // 16 * 16 + (t // 4 + turn) % 4 * 4 + t % 4) for t in range(tiles)] for turn in range(4)
     ]
-    pieces = [pieces[0]] + [lax.ppermute(pieces[t], "tile", along_z[t]) for t in range(1, 8)]
+    pieces = [pieces[0]] + [keep(lax.ppermute(pieces[t], "tile", along_z[t])) for t in range(1, 4)]
+    anywhere = pl.BlockSpec(memory_space=pl.ANY)
     moved_weights = pl.pallas_call(
         stack_kernel,
-        in_specs=[pl.BlockSpec(memory_space=pltpu.SMEM)] + [in_vmem] * 8,
-        out_shape=jax.ShapeDtypeStruct((8, groups, 18, share, 128), BF16),
-        scratch_shapes=[pltpu.VMEM((8, 8, 128), F32)],
+        in_specs=[pl.BlockSpec(memory_space=pltpu.SMEM)] + [in_vmem] * 4,
+        out_shape=jax.ShapeDtypeStruct((16, groups, 9, share, 128), BF16),
+        scratch_shapes=[pltpu.VMEM((4, 8, 128), F32)],
         name="stack",
-    )(place, *map(keep, pieces))
-    anywhere = pl.BlockSpec(memory_space=pl.ANY)
+    )(place, *pieces)
     moved_weights = pl.pallas_call(
         after_kernel,
         in_specs=[anywhere, anywhere],
@@ -361,17 +360,17 @@
         input_output_aliases={0: 0},
         name="after",
     )(moved_weights, keep(values))
-    same_z = [
-        [(16 * y + 2 * z + c) * groups + b for y in range(4) for c in range(2) for b in range(groups)]
-        for z in range(8)
+    same_pair = [
+        [(16 * y + 4 * z + low) * groups + b for y in range(4) for low in range(4) for b in range(groups)]
+        for z in range(4)
     ]
     moved_weights = lax.all_to_all(
-        moved_weights.reshape(8 * groups, 18, share, 128),
+        moved_weights.reshape(16 * groups, 9, share, 128),
         ("tile", "band"),
         split_axis=0,
         concat_axis=0,
-        axis_index_groups=same_z,
-    ).reshape(8, groups, 18, share, 128)
+        axis_index_groups=same_pair,
+    ).reshape(16, groups, 9, share, 128)
 
     entries = tiles * scenes * 4
     estimate = pl.pallas_call(
@@ -382,7 +381,7 @@
             pltpu.VMEM((entries, 256), BF16),
             pltpu.VMEM((SIDE, entries), BF16),
             pltpu.VMEM((entries, 128), BF16),
-            pltpu.VMEM((4, 8, 2, SIDE, 128), F32),
+            pltpu.VMEM((4, 4, 4, SIDE, 128), F32),
             pltpu.SemaphoreType.DMA,
         ],
         name="merge",

time: 128 us -> 126 us (0.984)
  starting transfers between devices: 39.3 us -> 32.4 us
  waiting for transfers between devices: 25.2 us -> 30.9 us
    ppermute x7 -> x3, waiting for transfers between devices: 15.4 us -> 21.1 us  [per_device(): lax.ppermute(pieces[t], 'tile', along_z[t])]
    ppermute x7 -> x3, starting transfers between devices: 14.6 us -> 8.9 us  [per_device(): lax.ppermute(pieces[t], 'tile', along_z[t])]
  transfers between devices with their start and end apart: 12 -> 8, of which waited for: 4 -> 3; matrix products, arithmetic and copies ran while one was open for 5% -> 5% of each run, Pallas kernels for 12% -> 13%
where the time goes in v6:
time: 126 us
  Pallas kernels  34.9 us (28%)
  starting transfers between devices  32.4 us (26%)
  waiting for transfers between devices  30.9 us (25%)
  blocking collectives  20.5 us (16%)
  other arithmetic  3.43 us (3%)
  local copies, waits for them, and re-layouts  3.42 us (3%)
    ppermute x3, waiting for transfers between devices, per_device(): lax.ppermute(pieces[t], 'tile', along_z[t])  21.1 us
    all_to_all x1, blocking collectives, per_device(): lax.all_to_all(moved_weights.reshape(16 * groups, 9, share, 128), ('tile'...  20.5 us
    all_to_all x1, starting transfers between devices, per_device(): values = lax.all_to_all(moved, 'tile', split_axis=0, concat_axis=0)  13.3 us
    pallas_call x1, Pallas kernels, per_device(): pl.pallas_call(cloud_kernel, grid=(share, pixels // width), in_specs=[in_...  11 us
    pallas_call x1, Pallas kernels, per_device(): pl.pallas_call(merge_kernel, in_specs=[anywhere, in_vmem, in_vmem], out_s...  10.6 us
    all_to_all x1, waiting for transfers between devices, per_device(): field = lax.all_to_all(estimate, 'tile', split_axis=0, concat_axis=0)  9.86 us
    ppermute x3, starting transfers between devices, per_device(): lax.ppermute(pieces[t], 'tile', along_z[t])  8.9 us
    pallas_call x1, Pallas kernels, per_device(): pl.pallas_call(reproject_kernel, grid=(4,), in_specs=[scene_block, scene_...  6.64 us
  transfers between devices with their start and end apart: 8, of which 3 were waited for; matrix products, arithmetic and copies ran while one was open for 5% of the time, Pallas kernels for 13%

profile of v6, /device:TPU:1, one launch (start us, length us, event | category | flops | bytes accessed | tf_op | source)
XLA Modules:
  0.0 125.8 jit_solution(10185528428843079691)
XLA Ops:
  0.0 6.6 %reproject.1 = bf16[64,64,256]{2,1,0:T(8,128)(2,1)} custom-call(bf16[16,128,128]{2,1,0:T(8,128)(2,1)} %bitcast.52, bf16[16,128,128]{2,1,0:T(8,128)(2,1)} %bitcast.54, bf16[16,128,128]{2,1,0:T(8,128)(2,1)} %bitcast.56, bf16[256,128]{1,0:T(8,128)(2,1)} %constant.115.clone.spread_ref), custom_call_target="tpu_custom_call" | custom-call | tf_op jit(solution)/shard_map/reproject/pallas_call | solution.py:266
  6.7 13.3 %all-to-all-start = ((bf16[64,64,256]{2,1,0:T(8,128)(2,1)}), bf16[64,64,256]{2,1,0:T(8,128)(2,1)S(1)}, u32[]{:S(2)}, u32[]{:S(2)}) async-start(bf16[64,64,256]{2,1,0:T(8,128)(2,1)} %reproject.1), calls=%async_computation | async-start | bytes 4194304 | tf_op jit(solution)/shard_map/all_to_all | solution.py:276
  20.3 1.3 %collective-permute-start = (bf16[4,4,4096]{2,1,0:T(4,128)(2,1)S(1)}, bf16[4,4,4096]{2,1,0:T(4,128)(2,1)S(1)}, u32[]{:S(2)}, u32[]{:S(2)}) collective-permute-start(bf16[4,4,4096]{2,1,0:T(4,128)(2,1)S(1)} %get-tuple-element.19), channel_id=1, source_target_pairs={{0,64},{64,128},{128,192},{192,0},{1,65},{65,129},{129,193},{193,1... | collective-permute-start | bytes 393224 | tf_op jit(solution)/shard_map/ppermute | solution.py:285
  21.6 2.5 %collective-permute-start.1 = (bf16[4,4,4096]{2,1,0:T(4,128)(2,1)S(1)}, bf16[4,4,4096]{2,1,0:T(4,128)(2,1)S(1)}, u32[]{:S(2)}, u32[]{:S(2)}) collective-permute-start(bf16[4,4,4096]{2,1,0:T(4,128)(2,1)S(1)} %get-tuple-element.18), channel_id=1, source_target_pairs={{0,128},{64,192},{128,0},{192,64},{1,129},{65,193},{129,1},{193,65... | collective-permute-start | bytes 393224 | tf_op jit(solution)/shard_map/ppermute | solution.py:285
  24.0 1.2 collective-permute-start.2
  25.6 0.7 add_exponential_fusion
  26.3 0.8 fusion.1
  27.1 0.7 multiply_bitcast_fusion.w_hidden_ref
  27.9 0.8 reshape.56.factor_ref
  28.7 0.7 copy.33
  29.4 0.6 pad_add_fusion.1.place_ref
  30.7 11.0 %cloud.1.w_ref = bf16[4,32,128]{2,1,0:T(8,128)(2,1)} custom-call(bf16[4,4,4096]{2,1,0:T(4,128)(2,1)S(1)} %get-tuple-element.20.x0, bf16[4,4,4096]{2,1,0:T(4,128)(2,1)S(1)} %collective-permute-done.x1, bf16[4,4,4096]{2,1,0:T(4,128)(2,1)S(1)} %collective-permute-done.1.x2, bf16[4,4,4096]{2,1,0:T(4,128)(2,1)S(1)} %collective-permute-done.2.x3, ...), custom_call_target="tpu_custom_call" | custom-call | flops 12000000000 | bytes 1000000 | tf_op jit(solution)/shard_map/cloud/pallas_call | solution.py:297
  42.2 3.2 %reproject_weights.1 = (bf16[16,3,4,128]{3,2,1,0:T(4,128)(2,1)}, bf16[16,3,4,128]{3,2,1,0:T(4,128)(2,1)}, bf16[16,3,4,128]{3,2,1,0:T(4,128)(2,1)}, bf16[16,3,4,128]{3,2,1,0:T(4,128)(2,1)}) custom-call(s32[2]{0:T(128)} %pad_add_fusion.1.place_ref, bf16[4,32,128]{2,1,0:T(8,128)(2,1)} %cloud.1.w_ref, f32[4,128]{1,0:T(4,128)} %broadcast_in_dim.11.id_ref, ...), custom_call_target="tpu_custom_call" | custom-call | flops 3000000000 | bytes 1000000 | tf_op jit(solution)/shard_map/reproject_weights/pallas_call | solution.py:323
  45.4 2.3 %collective-permute-start.3 = (bf16[16,3,4,128]{3,2,1,0:T(4,128)(2,1)}, bf16[16,3,4,128]{3,2,1,0:T(4,128)(2,1)S(1)}, u32[]{:S(2)}, u32[]{:S(2)}) collective-permute-start(bf16[16,3,4,128]{3,2,1,0:T(4,128)(2,1)} %get-tuple-element.14), channel_id=1, source_target_pairs={{0,4},{1,5},{2,6},{3,7},{4,8},{5,9},{6,10},{7,11},{8,12},{9,13},{1... | collective-permute-start | bytes 147464 | tf_op jit(solution)/shard_map/ppermute | solution.py:346
  47.7 3.3 %collective-permute-start.4 = (bf16[16,3,4,128]{3,2,1,0:T(4,128)(2,1)}, bf16[16,3,4,128]{3,2,1,0:T(4,128)(2,1)S(1)}, u32[]{:S(2)}, u32[]{:S(2)}) collective-permute-start(bf16[16,3,4,128]{3,2,1,0:T(4,128)(2,1)} %get-tuple-element.15), channel_id=1, source_target_pairs={{0,8},{1,9},{2,10},{3,11},{4,12},{5,13},{6,14},{7,15},{8,0},{9,1},... | collective-permute-start | bytes 147464 | tf_op jit(solution)/shard_map/ppermute | solution.py:346
  51.0 3.3 %collective-permute-start.5 = (bf16[16,3,4,128]{3,2,1,0:T(4,128)(2,1)}, bf16[16,3,4,128]{3,2,1,0:T(4,128)(2,1)S(1)}, u32[]{:S(2)}, u32[]{:S(2)}) collective-permute-start(bf16[16,3,4,128]{3,2,1,0:T(4,128)(2,1)} %get-tuple-element.16), channel_id=1, source_target_pairs={{0,12},{1,13},{2,14},{3,15},{4,0},{5,1},{6,2},{7,3},{8,4},{9,5},{1... | collective-permute-start | bytes 147464 | tf_op jit(solution)/shard_map/ppermute | solution.py:346
  54.3 16.4 %collective-permute-done.3.p1 = bf16[16,3,4,128]{3,2,1,0:T(4,128)(2,1)S(1)} collective-permute-done((bf16[16,3,4,128]{3,2,1,0:T(4,128)(2,1)}, bf16[16,3,4,128]{3,2,1,0:T(4,128)(2,1)S(1)}, u32[]{:S(2)}, u32[]{:S(2)}) %collective-permute-start.3) | collective-permute-done | bytes 49184 | tf_op jit(solution)/shard_map/ppermute | solution.py:346
  70.7 4.7 %collective-permute-done.4.p2 = bf16[16,3,4,128]{3,2,1,0:T(4,128)(2,1)S(1)} collective-permute-done((bf16[16,3,4,128]{3,2,1,0:T(4,128)(2,1)}, bf16[16,3,4,128]{3,2,1,0:T(4,128)(2,1)S(1)}, u32[]{:S(2)}, u32[]{:S(2)}) %collective-permute-start.4) | collective-permute-done | bytes 49184 | tf_op jit(solution)/shard_map/ppermute | solution.py:346
  75.4 1.8 %stack.21.x_ref = bf16[16,4,9,4,128]{4,3,2,1,0:T(4,128)(2,1)} custom-call(s32[2]{0:T(128)} %pad_add_fusion.1.place_ref, bf16[16,3,4,128]{3,2,1,0:T(4,128)(2,1)} %get-tuple-element.13.p0, bf16[16,3,4,128]{3,2,1,0:T(4,128)(2,1)S(1)} %collective-permute-done.3.p1, bf16[16,3,4,128]{3,2,1,0:T(4,128)(2,1)S(1)} %collective-permute-done.4.p2, ...), custom_call_target="tpu_custom_call" | custom-call | tf_op jit(solution)/shard_map/stack/pallas_call | solution.py:348
  77.2 20.5 %all_to_all.15 = bf16[64,9,4,128]{3,2,1,0:T(4,128)(2,1)S(1)} all-to-all(bf16[64,9,4,128]{3,2,1,0:T(4,128)(2,1)} %bitcast.51), channel_id=1, replica_groups={{0,64,128,192,1,65,129,193,2,66,130,194,3,67,131,195,16,80,144,208,17,8..., dimensions={0} | all-to-all | bytes 1179648 | tf_op jit(solution)/shard_map/all_to_all | solution.py:367
  97.6 10.6 %merge.1 = f32[64,4,128]{2,1,0:T(4,128)} custom-call(bf16[4096,256]{1,0:T(8,128)(2,1)} %bitcast.49, bf16[16,4,9,4,128]{4,3,2,1,0:T(4,128)(2,1)S(1)} %bitcast.50, bf16[128,256]{1,0:T(8,128)(2,1)} %constant.117.clone.double_ref), custom_call_target="tpu_custom_call" | custom-call | tf_op jit(solution)/shard_map/merge/pallas_call | solution.py:376
  108.2 5.3 %all-to-all-start.2 = ((f32[64,4,128]{2,1,0:T(4,128)}), f32[64,4,128]{2,1,0:T(4,128)S(1)}, u32[]{:S(2)}, u32[]{:S(2)}) async-start(f32[64,4,128]{2,1,0:T(4,128)} %merge.1), calls=%async_computation.2 | async-start | bytes 262144 | tf_op jit(solution)/shard_map/all_to_all | solution.py:389
  114.2 9.9 %all-to-all-done.2.g_ref = f32[64,4,128]{2,1,0:T(4,128)S(1)} async-done(((f32[64,4,128]{2,1,0:T(4,128)}), f32[64,4,128]{2,1,0:T(4,128)S(1)}, u32[]{:S(2)}, u32[]{:S(2)}) %all-to-all-start.2) | async-done | bytes 131104 | tf_op jit(solution)/shard_map/all_to_all | solution.py:389
  124.0 1.8 %smooth.1 = f32[32,4,128]{2,1,0:T(4,128)} custom-call(s32[2]{0:T(128)} %pad_add_fusion.tile_ref, f32[64,4,128]{2,1,0:T(4,128)S(1)} %all-to-all-done.2.g_ref), custom_call_target="tpu_custom_call" | custom-call | tf_op jit(solution)/shard_map/smooth/pallas_call | solution.py:392
  (32 shorter events, 2.6 us)
Async XLA Ops:
  6.6 13.4 %copy-start.1 = (bf16[16,4,4096]{2,1,0:T(4,128)(2,1)S(1)}, bf16[16,4,4096]{2,1,0:T(4,128)(2,1)}, u32[]{:S(2)}) copy-start(bf16[16,4,4096]{2,1,0:T(4,128)(2,1)} %param.12) | copy-start | bytes 1572868
  6.6 18.6 %copy-start.3 = (bf16[16,256]{1,0:T(8,128)(2,1)S(1)}, bf16[16,256]{1,0:T(8,128)(2,1)}, u32[]{:S(2)}) copy-start(bf16[16,256]{1,0:T(8,128)(2,1)} %param.18) | copy-start | bytes 24580
  6.6 18.6 %copy-start.2 = (bf16[2,256,256]{2,1,0:T(8,128)(2,1)S(1)}, bf16[2,256,256]{2,1,0:T(8,128)(2,1)}, u32[]{:S(2)}) copy-start(bf16[2,256,256]{2,1,0:T(8,128)(2,1)} %param.19) | copy-start | bytes 786436
  6.7 18.7 %copy-start.4 = (s32[16,4]{0,1:T(4,128)S(1)}, s32[16,4]{0,1:T(4,128)}, u32[]{:S(2)}) copy-start(s32[16,4]{0,1:T(4,128)} %param.15) | copy-start | bytes 772
  6.7 70.5 %all-to-all-start = ((bf16[64,64,256]{2,1,0:T(8,128)(2,1)}), bf16[64,64,256]{2,1,0:T(8,128)(2,1)S(1)}, u32[]{:S(2)}, u32[]{:S(2)}) async-start(bf16[64,64,256]{2,1,0:T(8,128)(2,1)} %reproject.1), calls=%async_computation | async-start | bytes 4194304 | tf_op jit(solution)/shard_map/all_to_all | solution.py:276
  20.0 10.1 %copy-start.5 = (bf16[256]{0:T(256)(128)(2,1)S(1)}, bf16[256]{0:T(256)(128)(2,1)}, u32[]{:S(2)}) copy-start(bf16[256]{0:T(256)(128)(2,1)} %param.20) | copy-start | bytes 1540
  20.3 9.8 %collective-permute-start = (bf16[4,4,4096]{2,1,0:T(4,128)(2,1)S(1)}, bf16[4,4,4096]{2,1,0:T(4,128)(2,1)S(1)}, u32[]{:S(2)}, u32[]{:S(2)}) collective-permute-start(bf16[4,4,4096]{2,1,0:T(4,128)(2,1)S(1)} %get-tuple-element.19), channel_id=1, source_target_pairs={{0,64},{64,128},{128,192},{192,0},{1,65},{65,129},{129,193},{193,1... | collective-permute-start | bytes 393224 | tf_op jit(solution)/shard_map/ppermute | solution.py:285
  21.6 8.5 %collective-permute-start.1 = (bf16[4,4,4096]{2,1,0:T(4,128)(2,1)S(1)}, bf16[4,4,4096]{2,1,0:T(4,128)(2,1)S(1)}, u32[]{:S(2)}, u32[]{:S(2)}) collective-permute-start(bf16[4,4,4096]{2,1,0:T(4,128)(2,1)S(1)} %get-tuple-element.18), channel_id=1, source_target_pairs={{0,128},{64,192},{128,0},{192,64},{1,129},{65,193},{129,1},{193,65... | collective-permute-start | bytes 393224 | tf_op jit(solution)/shard_map/ppermute | solution.py:285
  24.0 6.0 %collective-permute-start.2 = (bf16[4,4,4096]{2,1,0:T(4,128)(2,1)S(1)}, bf16[4,4,4096]{2,1,0:T(4,128)(2,1)S(1)}, u32[]{:S(2)}, u32[]{:S(2)}) collective-permute-start(bf16[4,4,4096]{2,1,0:T(4,128)(2,1)S(1)} %get-tuple-element.17), channel_id=1, source_target_pairs={{0,192},{64,0},{128,64},{192,128},{1,193},{65,1},{129,65},{193,129... | collective-permute-start | bytes 393224 | tf_op jit(solution)/shard_map/ppermute | solution.py:285
  45.4 25.3 %collective-permute-start.3 = (bf16[16,3,4,128]{3,2,1,0:T(4,128)(2,1)}, bf16[16,3,4,128]{3,2,1,0:T(4,128)(2,1)S(1)}, u32[]{:S(2)}, u32[]{:S(2)}) collective-permute-start(bf16[16,3,4,128]{3,2,1,0:T(4,128)(2,1)} %get-tuple-element.14), channel_id=1, source_target_pairs={{0,4},{1,5},{2,6},{3,7},{4,8},{5,9},{6,10},{7,11},{8,12},{9,13},{1... | collective-permute-start | bytes 147464 | tf_op jit(solution)/shard_map/ppermute | solution.py:346
  47.7 27.6 %collective-permute-start.4 = (bf16[16,3,4,128]{3,2,1,0:T(4,128)(2,1)}, bf16[16,3,4,128]{3,2,1,0:T(4,128)(2,1)S(1)}, u32[]{:S(2)}, u32[]{:S(2)}) collective-permute-start(bf16[16,3,4,128]{3,2,1,0:T(4,128)(2,1)} %get-tuple-element.15), channel_id=1, source_target_pairs={{0,8},{1,9},{2,10},{3,11},{4,12},{5,13},{6,14},{7,15},{8,0},{9,1},... | collective-permute-start | bytes 147464 | tf_op jit(solution)/shard_map/ppermute | solution.py:346
  51.0 24.4 %collective-permute-start.5 = (bf16[16,3,4,128]{3,2,1,0:T(4,128)(2,1)}, bf16[16,3,4,128]{3,2,1,0:T(4,128)(2,1)S(1)}, u32[]{:S(2)}, u32[]{:S(2)}) collective-permute-start(bf16[16,3,4,128]{3,2,1,0:T(4,128)(2,1)} %get-tuple-element.16), channel_id=1, source_target_pairs={{0,12},{1,13},{2,14},{3,15},{4,0},{5,1},{6,2},{7,3},{8,4},{9,5},{1... | collective-permute-start | bytes 147464 | tf_op jit(solution)/shard_map/ppermute | solution.py:346
  77.1 20.5 %copy-start = (bf16[64,64,256]{2,1,0:T(8,128)(2,1)}, bf16[64,64,256]{2,1,0:T(8,128)(2,1)S(1)}, u32[]{:S(2)}) copy-start(bf16[64,64,256]{2,1,0:T(8,128)(2,1)S(1)} %all-to-all-done.first_ref) | copy-start | bytes 6291460
  108.2 15.8 %all-to-all-start.2 = ((f32[64,4,128]{2,1,0:T(4,128)}), f32[64,4,128]{2,1,0:T(4,128)S(1)}, u32[]{:S(2)}, u32[]{:S(2)}) async-start(f32[64,4,128]{2,1,0:T(4,128)} %merge.1), calls=%async_computation.2 | async-start | bytes 262144 | tf_op jit(solution)/shard_map/all_to_all | solution.py:389

commit v7 on v4

--- a/solution.py
+++ b/solution.py
@@ -51,7 +51,7 @@
 def reproject_kernel(x_ref, col_ref, row_ref, spread_ref, out_ref, scratch):
     mask = parity_mask(256)
     spread = spread_ref[...]
-    group = range(4)
+    group = range(8)
     wide = [jnp.concatenate([x_ref[s], col_ref[s], row_ref[s]], 1) for s in group]
     wide = [dot(spread, w) for w in wide]
     planes = [jnp.where(mask, w[:, :128], 0.0).astype(BF16) for w in wide]
@@ -65,9 +65,26 @@
             part = jnp.concatenate([part, part], 0)
             moved = dot(pairs[s][1][k * SIDE : (k + 1) * SIDE], part)
             for v in range(2):
-                scratch[v, pl.ds(4 * k + s, SIDE, stride=16), :] = moved[:, v * 128 : (v + 1) * 128]
-    for v in range(2):
-        out_ref[:, :, v * 128 : (v + 1) * 128] = scratch[v].reshape(SIDE, 16, 128).astype(BF16)
+                at = pl.ds(4 * k + s % 4, SIDE, stride=16)
+                scratch[s // 4, v, at, :] = moved[:, v * 128 : (v + 1) * 128]
+    for g in range(2):
+        for v in range(2):
+            lines = scratch[g, v].reshape(SIDE, 16, 128).astype(BF16)
+            out_ref[:, 16 * g : 16 * g + 16, v * 128 : (v + 1) * 128] = lines
+
+
+def reproject_call(x, cols, rows, name):
+    steps = x.shape[0] // 8
+    scene_block = pl.BlockSpec((8, 128, 128), lambda i: (i, 0, 0))
+    return pl.pallas_call(
+        reproject_kernel,
+        grid=(steps,),
+        in_specs=[scene_block, scene_block, scene_block, whole((256, 128))],
+        out_specs=pl.BlockSpec((SIDE, 32, 256), lambda i: (0, i, 0)),
+        out_shape=jax.ShapeDtypeStruct((SIDE, 32 * steps, 256), BF16),
+        scratch_shapes=[pltpu.VMEM((2, 2, SIDE * 16, 128), F32)],
+        name=name,
+    )(x, cols, rows, jnp.asarray(spread_matrix(4), BF16))
 
 
 def weight_kernel(
@@ -126,7 +143,7 @@
     fetch = pltpu.make_async_copy(y_in, y_ref, arrival)
     fetch.start()
     entries = y_ref.shape[0]
-    chunk = 512
+    chunk = 1024
     lane = lax.broadcasted_iota(jnp.int32, (1, 128), 1)
     tile = (lax.broadcasted_iota(jnp.int32, (128, 128), 0) & 63).astype(F32)
     ids = w_ref[:, 8].astype(F32)[:, 0, :]
@@ -247,16 +264,7 @@
     in_vmem = pl.BlockSpec(memory_space=pltpu.VMEM)
     cols = two_rows_per_line(col_resample)
     rows = two_rows_per_line(row_resample)
-    scene_block = pl.BlockSpec((4, 128, 128), lambda i: (i, 0, 0))
-    moved = pl.pallas_call(
-        reproject_kernel,
-        grid=(4,),
-        in_specs=[scene_block, scene_block, scene_block, whole((256, 128))],
-        out_specs=pl.BlockSpec((SIDE, 16, 256), lambda i: (0, i, 0)),
-        out_shape=jax.ShapeDtypeStruct((SIDE, 64, 256), BF16),
-        scratch_shapes=[pltpu.VMEM((2, SIDE * 16, 128), F32)],
-        name="reproject",
-    )(two_rows_per_line(granules), cols, rows, spread)
+    moved = reproject_call(two_rows_per_line(granules), cols, rows, "reproject")
     moved, granules = lax.optimization_barrier((moved, granules))
     values = lax.all_to_all(moved, "tile", split_axis=0, concat_axis=0)
 

time: 125 us -> 124 us (level)
  no operation moved by 1% of the time
where the time goes in v7:
time: 124 us
  Pallas kernels  34.4 us (28%)
  waiting for transfers between devices  30.4 us (25%)
  starting transfers between devices  28.6 us (23%)
  blocking collectives  24.5 us (20%)
  local copies, waits for them, and re-layouts  3.46 us (3%)
  other arithmetic  2.11 us (2%)
    all_to_all x1, blocking collectives, per_device(): lax.all_to_all(moved_weights, 'tile', split_axis=0, concat_axis=0)  24.5 us
    all_to_all x1, waiting for transfers between devices, per_device(): values = lax.all_to_all(moved, 'tile', split_axis=0, concat_axis=0)  17 us
    all_to_all x1, starting transfers between devices, per_device(): values = lax.all_to_all(moved, 'tile', split_axis=0, concat_axis=0)  13.3 us
    pallas_call x1, Pallas kernels, per_device(): pl.pallas_call(cloud_kernel, grid=(share, pixels // width), in_specs=[in_...  11 us
    pallas_call x1, Pallas kernels, per_device(): pl.pallas_call(merge_kernel, in_specs=[anywhere, in_vmem, in_vmem], out_s...  10.4 us
    all_to_all x1, waiting for transfers between devices, per_device(): field = lax.all_to_all(estimate, 'tile', split_axis=0, concat_axis=0)  9.76 us
    all_to_all x1, starting transfers between devices, per_device(): field = lax.all_to_all(estimate, 'tile', split_axis=0, concat_axis=0)  6.28 us
    pallas_call x1, Pallas kernels, reproject_call(): pl.pallas_call(reproject_kernel, grid=(steps,), in_specs=[scene_block, sc...  5.73 us
  transfers between devices with their start and end apart: 8, of which 6 were waited for; matrix products, arithmetic and copies ran while one was open for 4% of the time, Pallas kernels for 13%

profile of v7, /device:TPU:1, one launch (start us, length us, event | category | flops | bytes accessed | tf_op | source)
XLA Modules:
  0.0 123.7 jit_solution(1600275526839148201)
XLA Ops:
  0.0 5.7 %reproject.1 = bf16[64,64,256]{2,1,0:T(8,128)(2,1)} custom-call(bf16[16,128,128]{2,1,0:T(8,128)(2,1)} %bitcast.47, bf16[16,128,128]{2,1,0:T(8,128)(2,1)} %bitcast.49, bf16[16,128,128]{2,1,0:T(8,128)(2,1)} %bitcast.51, bf16[256,128]{1,0:T(8,128)(2,1)} %constant.101.clone.spread_ref), custom_call_target="tpu_custom_call" | custom-call | tf_op jit(solution)/shard_map/reproject/pallas_call | solution.py:79
  5.8 13.3 %all-to-all-start = ((bf16[64,64,256]{2,1,0:T(8,128)(2,1)}), bf16[64,64,256]{2,1,0:T(8,128)(2,1)S(1)}, u32[]{:S(2)}, u32[]{:S(2)}) async-start(bf16[64,64,256]{2,1,0:T(8,128)(2,1)} %reproject.1), calls=%async_computation | async-start | bytes 4194304 | tf_op jit(solution)/shard_map/all_to_all | solution.py:269
  19.4 1.3 %collective-permute-start = (bf16[4,4,4096]{2,1,0:T(4,128)(2,1)S(1)}, bf16[4,4,4096]{2,1,0:T(4,128)(2,1)S(1)}, u32[]{:S(2)}, u32[]{:S(2)}) collective-permute-start(bf16[4,4,4096]{2,1,0:T(4,128)(2,1)S(1)} %get-tuple-element.11), channel_id=1, source_target_pairs={{0,64},{64,128},{128,192},{192,0},{1,65},{65,129},{129,193},{193,1... | collective-permute-start | bytes 393224 | tf_op jit(solution)/shard_map/ppermute | solution.py:278
  20.7 2.5 %collective-permute-start.1 = (bf16[4,4,4096]{2,1,0:T(4,128)(2,1)S(1)}, bf16[4,4,4096]{2,1,0:T(4,128)(2,1)S(1)}, u32[]{:S(2)}, u32[]{:S(2)}) collective-permute-start(bf16[4,4,4096]{2,1,0:T(4,128)(2,1)S(1)} %get-tuple-element.10), channel_id=1, source_target_pairs={{0,128},{64,192},{128,0},{192,64},{1,129},{65,193},{129,1},{193,65... | collective-permute-start | bytes 393224 | tf_op jit(solution)/shard_map/ppermute | solution.py:278
  23.1 1.2 collective-permute-start.2
  24.4 0.8 fusion.1
  25.2 0.8 reshape.54.factor_ref
  26.1 0.7 copy.34
  27.1 0.7 multiply_bitcast_fusion.w_hidden_ref
  27.9 1.2 collective-permute-done.1.x2
  29.7 11.0 %cloud.1.w0 = bf16[4,32,128]{2,1,0:T(8,128)(2,1)} custom-call(bf16[4,4,4096]{2,1,0:T(4,128)(2,1)S(1)} %get-tuple-element.12.x0, bf16[4,4,4096]{2,1,0:T(4,128)(2,1)S(1)} %collective-permute-done.x1, bf16[4,4,4096]{2,1,0:T(4,128)(2,1)S(1)} %collective-permute-done.1.x2, bf16[4,4,4096]{2,1,0:T(4,128)(2,1)S(1)} %collective-permute-done.2.x3, ...), custom_call_target="tpu_custom_call" | custom-call | flops 12000000000 | bytes 1000000 | tf_op jit(solution)/shard_map/cloud/pallas_call | solution.py:290
  40.7 1.1 collective-permute-start.3
  41.8 2.1 %collective-permute-start.4 = (bf16[4,32,128]{2,1,0:T(8,128)(2,1)}, bf16[4,32,128]{2,1,0:T(8,128)(2,1)S(1)}, u32[]{:S(2)}, u32[]{:S(2)}) collective-permute-start(bf16[4,32,128]{2,1,0:T(8,128)(2,1)} %cloud.1.w0), channel_id=1, source_target_pairs={{0,128},{64,192},{128,0},{192,64},{1,129},{65,193},{129,1},{193,65... | collective-permute-start | bytes 98312 | tf_op jit(solution)/shard_map/ppermute | solution.py:314
  43.9 0.9 collective-permute-start.5
  45.1 1.4 %collective-permute-done.4.w2 = bf16[4,32,128]{2,1,0:T(8,128)(2,1)S(1)} collective-permute-done((bf16[4,32,128]{2,1,0:T(8,128)(2,1)}, bf16[4,32,128]{2,1,0:T(8,128)(2,1)S(1)}, u32[]{:S(2)}, u32[]{:S(2)}) %collective-permute-start.4) | collective-permute-done | bytes 32800 | tf_op jit(solution)/shard_map/ppermute | solution.py:314
  46.6 0.6 collective-permute-done.5.w3
  47.8 5.5 %reproject_weights.1.x_ref = bf16[64,9,4,128]{3,2,1,0:T(4,128)(2,1)} custom-call(s32[1]{0:T(128)} %bitcast.11.band_ref, bf16[4,32,128]{2,1,0:T(8,128)(2,1)} %cloud.1.w0, bf16[4,32,128]{2,1,0:T(8,128)(2,1)} %copy-done.6, bf16[4,32,128]{2,1,0:T(8,128)(2,1)} %copy-done.7, bf16[4,32,128]{2,1,0:T(8,128)(2,1)} %copy-done.8, f32[4,128]{1,0:T(4,128)} %broadcast_in_dim.11.id_ref, ...), custom_call_target="tpu_custom_call" | custom-call | flops 8000000000 | bytes 1000000 | tf_op jit(solution)/shard_map/reproject_weights/pallas_call | solution.py:318
  53.3 17.0 %all-to-all-done.first_ref = bf16[64,64,256]{2,1,0:T(8,128)(2,1)S(1)} async-done(((bf16[64,64,256]{2,1,0:T(8,128)(2,1)}), bf16[64,64,256]{2,1,0:T(8,128)(2,1)S(1)}, u32[]{:S(2)}, u32[]{:S(2)}) %all-to-all-start) | async-done | bytes 2097184 | tf_op jit(solution)/shard_map/all_to_all | solution.py:269
  70.3 24.5 %all_to_all.15.w_ref = bf16[64,9,4,128]{3,2,1,0:T(4,128)(2,1)S(1)} all-to-all(bf16[64,9,4,128]{3,2,1,0:T(4,128)(2,1)} %after.1), channel_id=1, replica_groups=mesh['band'=4,'tile'=64] {'tile'}, dimensions={0} | all-to-all | bytes 1179648 | tf_op jit(solution)/shard_map/all_to_all | solution.py:341
  94.9 10.4 %merge.1 = f32[64,4,128]{2,1,0:T(4,128)} custom-call(bf16[4096,256]{1,0:T(8,128)(2,1)} %bitcast.46, bf16[64,9,4,128]{3,2,1,0:T(4,128)(2,1)S(1)} %all_to_all.15.w_ref, bf16[128,256]{1,0:T(8,128)(2,1)} %constant.103.clone.double_ref), custom_call_target="tpu_custom_call" | custom-call | tf_op jit(solution)/shard_map/merge/pallas_call | solution.py:344
  105.3 6.3 %all-to-all-start.2 = ((f32[64,4,128]{2,1,0:T(4,128)}), f32[64,4,128]{2,1,0:T(4,128)S(1)}, u32[]{:S(2)}, u32[]{:S(2)}) async-start(f32[64,4,128]{2,1,0:T(4,128)} %merge.1), calls=%async_computation.2 | async-start | bytes 262144 | tf_op jit(solution)/shard_map/all_to_all | solution.py:357
  111.6 0.6 pad_add_fusion.tile_ref
  112.2 9.8 %all-to-all-done.2.g_ref = f32[64,4,128]{2,1,0:T(4,128)S(1)} async-done(((f32[64,4,128]{2,1,0:T(4,128)}), f32[64,4,128]{2,1,0:T(4,128)S(1)}, u32[]{:S(2)}, u32[]{:S(2)}) %all-to-all-start.2) | async-done | bytes 131104 | tf_op jit(solution)/shard_map/all_to_all | solution.py:357
  122.0 1.8 %smooth.1 = f32[32,4,128]{2,1,0:T(4,128)} custom-call(s32[2]{0:T(128)} %pad_add_fusion.tile_ref, f32[64,4,128]{2,1,0:T(4,128)S(1)} %all-to-all-done.2.g_ref), custom_call_target="tpu_custom_call" | custom-call | tf_op jit(solution)/shard_map/smooth/pallas_call | solution.py:360
  (38 shorter events, 2.3 us)
Async XLA Ops:
  5.7 13.4 %copy-start.1 = (bf16[16,4,4096]{2,1,0:T(4,128)(2,1)S(1)}, bf16[16,4,4096]{2,1,0:T(4,128)(2,1)}, u32[]{:S(2)}) copy-start(bf16[16,4,4096]{2,1,0:T(4,128)(2,1)} %param.13) | copy-start | bytes 1572868
  5.7 18.6 %copy-start.9 = (s32[16]{0:T(128)S(1)}, s32[16]{0:T(128)}, u32[]{:S(2)}) copy-start(s32[16]{0:T(128)} %param.15) | copy-start | bytes 196
  5.7 20.3 %copy-start.3 = (bf16[16,256]{1,0:T(8,128)(2,1)S(1)}, bf16[16,256]{1,0:T(8,128)(2,1)}, u32[]{:S(2)}) copy-start(bf16[16,256]{1,0:T(8,128)(2,1)} %param.19) | copy-start | bytes 24580
  5.7 21.1 %copy-start.2 = (bf16[2,256,256]{2,1,0:T(8,128)(2,1)S(1)}, bf16[2,256,256]{2,1,0:T(8,128)(2,1)}, u32[]{:S(2)}) copy-start(bf16[2,256,256]{2,1,0:T(8,128)(2,1)} %param.20) | copy-start | bytes 786436
  5.8 64.6 %all-to-all-start = ((bf16[64,64,256]{2,1,0:T(8,128)(2,1)}), bf16[64,64,256]{2,1,0:T(8,128)(2,1)S(1)}, u32[]{:S(2)}, u32[]{:S(2)}) async-start(bf16[64,64,256]{2,1,0:T(8,128)(2,1)} %reproject.1), calls=%async_computation | async-start | bytes 4194304 | tf_op jit(solution)/shard_map/all_to_all | solution.py:269
  19.1 7.9 %copy-start.4 = (s32[16,4]{0,1:T(4,128)S(1)}, s32[16,4]{0,1:T(4,128)}, u32[]{:S(2)}) copy-start(s32[16,4]{0,1:T(4,128)} %param.16) | copy-start | bytes 772
  19.1 10.0 %copy-start.5 = (bf16[256]{0:T(256)(128)(2,1)S(1)}, bf16[256]{0:T(256)(128)(2,1)}, u32[]{:S(2)}) copy-start(bf16[256]{0:T(256)(128)(2,1)} %param.21) | copy-start | bytes 1540
  19.4 8.5 %collective-permute-start = (bf16[4,4,4096]{2,1,0:T(4,128)(2,1)S(1)}, bf16[4,4,4096]{2,1,0:T(4,128)(2,1)S(1)}, u32[]{:S(2)}, u32[]{:S(2)}) collective-permute-start(bf16[4,4,4096]{2,1,0:T(4,128)(2,1)S(1)} %get-tuple-element.11), channel_id=1, source_target_pairs={{0,64},{64,128},{128,192},{192,0},{1,65},{65,129},{129,193},{193,1... | collective-permute-start | bytes 393224 | tf_op jit(solution)/shard_map/ppermute | solution.py:278
  20.7 8.4 %collective-permute-start.1 = (bf16[4,4,4096]{2,1,0:T(4,128)(2,1)S(1)}, bf16[4,4,4096]{2,1,0:T(4,128)(2,1)S(1)}, u32[]{:S(2)}, u32[]{:S(2)}) collective-permute-start(bf16[4,4,4096]{2,1,0:T(4,128)(2,1)S(1)} %get-tuple-element.10), channel_id=1, source_target_pairs={{0,128},{64,192},{128,0},{192,64},{1,129},{65,193},{129,1},{193,65... | collective-permute-start | bytes 393224 | tf_op jit(solution)/shard_map/ppermute | solution.py:278
  23.1 6.0 %collective-permute-start.2 = (bf16[4,4,4096]{2,1,0:T(4,128)(2,1)S(1)}, bf16[4,4,4096]{2,1,0:T(4,128)(2,1)S(1)}, u32[]{:S(2)}, u32[]{:S(2)}) collective-permute-start(bf16[4,4,4096]{2,1,0:T(4,128)(2,1)S(1)} %get-tuple-element.9), channel_id=1, source_target_pairs={{0,192},{64,0},{128,64},{192,128},{1,193},{65,1},{129,65},{193,129... | collective-permute-start | bytes 393224 | tf_op jit(solution)/shard_map/ppermute | solution.py:278
  40.7 4.5 %collective-permute-start.3 = (bf16[4,32,128]{2,1,0:T(8,128)(2,1)}, bf16[4,32,128]{2,1,0:T(8,128)(2,1)S(1)}, u32[]{:S(2)}, u32[]{:S(2)}) collective-permute-start(bf16[4,32,128]{2,1,0:T(8,128)(2,1)} %cloud.1.w0), channel_id=1, source_target_pairs={{0,64},{64,128},{128,192},{192,0},{1,65},{65,129},{129,193},{193,1... | collective-permute-start | bytes 98312 | tf_op jit(solution)/shard_map/ppermute | solution.py:314
  41.8 4.8 %collective-permute-start.4 = (bf16[4,32,128]{2,1,0:T(8,128)(2,1)}, bf16[4,32,128]{2,1,0:T(8,128)(2,1)S(1)}, u32[]{:S(2)}, u32[]{:S(2)}) collective-permute-start(bf16[4,32,128]{2,1,0:T(8,128)(2,1)} %cloud.1.w0), channel_id=1, source_target_pairs={{0,128},{64,192},{128,0},{192,64},{1,129},{65,193},{129,1},{193,65... | collective-permute-start | bytes 98312 | tf_op jit(solution)/shard_map/ppermute | solution.py:314
  43.9 3.3 %collective-permute-start.5 = (bf16[4,32,128]{2,1,0:T(8,128)(2,1)}, bf16[4,32,128]{2,1,0:T(8,128)(2,1)S(1)}, u32[]{:S(2)}, u32[]{:S(2)}) collective-permute-start(bf16[4,32,128]{2,1,0:T(8,128)(2,1)} %cloud.1.w0), channel_id=1, source_target_pairs={{0,192},{64,0},{128,64},{192,128},{1,193},{65,1},{129,65},{193,129... | collective-permute-start | bytes 98312 | tf_op jit(solution)/shard_map/ppermute | solution.py:314
  45.1 2.6 %copy-start.6 = (bf16[4,32,128]{2,1,0:T(8,128)(2,1)}, bf16[4,32,128]{2,1,0:T(8,128)(2,1)S(1)}, u32[]{:S(2)}) copy-start(bf16[4,32,128]{2,1,0:T(8,128)(2,1)S(1)} %collective-permute-done.3.w1) | copy-start | bytes 98308
  46.6 1.2 %copy-start.7 = (bf16[4,32,128]{2,1,0:T(8,128)(2,1)}, bf16[4,32,128]{2,1,0:T(8,128)(2,1)S(1)}, u32[]{:S(2)}) copy-start(bf16[4,32,128]{2,1,0:T(8,128)(2,1)S(1)} %collective-permute-done.4.w2) | copy-start | bytes 98308
  47.2 0.6 copy-start.8
  70.3 24.5 %copy-start = (bf16[64,64,256]{2,1,0:T(8,128)(2,1)}, bf16[64,64,256]{2,1,0:T(8,128)(2,1)S(1)}, u32[]{:S(2)}) copy-start(bf16[64,64,256]{2,1,0:T(8,128)(2,1)S(1)} %all-to-all-done.first_ref) | copy-start | bytes 6291460
  105.3 16.6 %all-to-all-start.2 = ((f32[64,4,128]{2,1,0:T(4,128)}), f32[64,4,128]{2,1,0:T(4,128)S(1)}, u32[]{:S(2)}, u32[]{:S(2)}) async-start(f32[64,4,128]{2,1,0:T(4,128)} %merge.1), calls=%async_computation.2 | async-start | bytes 262144 | tf_op jit(solution)/shard_map/all_to_all | solution.py:357

commit v8 on v7

--- a/solution.py
+++ b/solution.py
@@ -145,15 +145,16 @@
     entries = y_ref.shape[0]
     chunk = 1024
     lane = lax.broadcasted_iota(jnp.int32, (1, 128), 1)
-    tile = (lax.broadcasted_iota(jnp.int32, (128, 128), 0) & 63).astype(F32)
+    tile = (lax.broadcasted_iota(jnp.int32, (128, 128), 0) & 63).astype(F32).astype(BF16)
+    one, none = jnp.ones((128, 128), BF16), jnp.zeros((128, 128), BF16)
     ids = w_ref[:, 8].astype(F32)[:, 0, :]
     turned = pltpu.roll(ids, 64, 1)
     for i in range(entries // 128):
         span = slice(i * 128, (i + 1) * 128)
         pair = jnp.where(lane < 64, ids[2 * i : 2 * i + 1], turned[2 * i + 1 : 2 * i + 2])
-        hit = jnp.where(pair == tile, 1.0, 0.0)
-        pick[:, span] = hit[:SIDE].astype(BF16)
-        pick_t[span, :] = hit.T.astype(BF16)
+        hit = jnp.where(jnp.broadcast_to(pair, (128, 128)).astype(BF16) == tile, one, none)
+        pick[:, span] = hit[:SIDE]
+        pick_t[span, :] = hit.T
     for i in range(8):
         w = dot(w_ref[:, i].reshape(entries // 16, 128), double_ref[...])
         for half in range(2):
@@ -185,7 +186,9 @@
             h = h.astype(BF16)
             picked = pick[:, span]
             top = top + dot(picked, h * y)
-            bottom = bottom + dot(picked, h)
+            bottom = bottom + dot(picked, h[:, :128] if estimate is None else h)
+        if estimate is None:
+            bottom = jnp.concatenate([bottom, bottom], 1)
         prior = prior_weight if estimate is not None else prior_weight * huber_delta
         return top / (bottom + prior)
 

time: 124 us -> 124 us (level)
  no operation moved by 1% of the time
where the time goes in v8:
time: 124 us
  Pallas kernels  34.3 us (28%)
  waiting for transfers between devices  30.4 us (25%)
  starting transfers between devices  28.6 us (23%)
  blocking collectives  24.5 us (20%)
  local copies, waits for them, and re-layouts  3.46 us (3%)
  other arithmetic  2.11 us (2%)
    all_to_all x1, blocking collectives, per_device(): lax.all_to_all(moved_weights, 'tile', split_axis=0, concat_axis=0)  24.5 us
    all_to_all x1, waiting for transfers between devices, per_device(): values = lax.all_to_all(moved, 'tile', split_axis=0, concat_axis=0)  17 us
    all_to_all x1, starting transfers between devices, per_device(): values = lax.all_to_all(moved, 'tile', split_axis=0, concat_axis=0)  13.3 us
    pallas_call x1, Pallas kernels, per_device(): pl.pallas_call(cloud_kernel, grid=(share, pixels // width), in_specs=[in_...  11 us
    pallas_call x1, Pallas kernels, per_device(): pl.pallas_call(merge_kernel, in_specs=[anywhere, in_vmem, in_vmem], out_s...  10.4 us
    all_to_all x1, waiting for transfers between devices, per_device(): field = lax.all_to_all(estimate, 'tile', split_axis=0, concat_axis=0)  9.76 us
    all_to_all x1, starting transfers between devices, per_device(): field = lax.all_to_all(estimate, 'tile', split_axis=0, concat_axis=0)  6.27 us
    pallas_call x1, Pallas kernels, reproject_call(): pl.pallas_call(reproject_kernel, grid=(steps,), in_specs=[scene_block, sc...  5.73 us
  transfers between devices with their start and end apart: 8, of which 6 were waited for; matrix products, arithmetic and copies ran while one was open for 4% of the time, Pallas kernels for 13%

profile of v8, /device:TPU:1, one launch (start us, length us, event | category | flops | bytes accessed | tf_op | source)
XLA Modules:
  0.0 123.7 jit_solution(1701588354426399863)
XLA Ops:
  0.0 5.7 %reproject.1 = bf16[64,64,256]{2,1,0:T(8,128)(2,1)} custom-call(bf16[16,128,128]{2,1,0:T(8,128)(2,1)} %bitcast.47, bf16[16,128,128]{2,1,0:T(8,128)(2,1)} %bitcast.49, bf16[16,128,128]{2,1,0:T(8,128)(2,1)} %bitcast.51, bf16[256,128]{1,0:T(8,128)(2,1)} %constant.101.clone.spread_ref), custom_call_target="tpu_custom_call" | custom-call | tf_op jit(solution)/shard_map/reproject/pallas_call | solution.py:79
  5.8 13.3 %all-to-all-start = ((bf16[64,64,256]{2,1,0:T(8,128)(2,1)}), bf16[64,64,256]{2,1,0:T(8,128)(2,1)S(1)}, u32[]{:S(2)}, u32[]{:S(2)}) async-start(bf16[64,64,256]{2,1,0:T(8,128)(2,1)} %reproject.1), calls=%async_computation | async-start | bytes 4194304 | tf_op jit(solution)/shard_map/all_to_all | solution.py:272
  19.4 1.3 %collective-permute-start = (bf16[4,4,4096]{2,1,0:T(4,128)(2,1)S(1)}, bf16[4,4,4096]{2,1,0:T(4,128)(2,1)S(1)}, u32[]{:S(2)}, u32[]{:S(2)}) collective-permute-start(bf16[4,4,4096]{2,1,0:T(4,128)(2,1)S(1)} %get-tuple-element.11), channel_id=1, source_target_pairs={{0,64},{64,128},{128,192},{192,0},{1,65},{65,129},{129,193},{193,1... | collective-permute-start | bytes 393224 | tf_op jit(solution)/shard_map/ppermute | solution.py:281
  20.7 2.5 %collective-permute-start.1 = (bf16[4,4,4096]{2,1,0:T(4,128)(2,1)S(1)}, bf16[4,4,4096]{2,1,0:T(4,128)(2,1)S(1)}, u32[]{:S(2)}, u32[]{:S(2)}) collective-permute-start(bf16[4,4,4096]{2,1,0:T(4,128)(2,1)S(1)} %get-tuple-element.10), channel_id=1, source_target_pairs={{0,128},{64,192},{128,0},{192,64},{1,129},{65,193},{129,1},{193,65... | collective-permute-start | bytes 393224 | tf_op jit(solution)/shard_map/ppermute | solution.py:281
  23.1 1.2 collective-permute-start.2
  24.4 0.8 fusion.1
  25.2 0.8 reshape.54.factor_ref
  26.1 0.7 copy.34
  27.1 0.7 multiply_bitcast_fusion.w_hidden_ref
  27.9 1.2 collective-permute-done.1.x2
  29.7 11.0 %cloud.1.w0 = bf16[4,32,128]{2,1,0:T(8,128)(2,1)} custom-call(bf16[4,4,4096]{2,1,0:T(4,128)(2,1)S(1)} %get-tuple-element.12.x0, bf16[4,4,4096]{2,1,0:T(4,128)(2,1)S(1)} %collective-permute-done.x1, bf16[4,4,4096]{2,1,0:T(4,128)(2,1)S(1)} %collective-permute-done.1.x2, bf16[4,4,4096]{2,1,0:T(4,128)(2,1)S(1)} %collective-permute-done.2.x3, ...), custom_call_target="tpu_custom_call" | custom-call | flops 12000000000 | bytes 1000000 | tf_op jit(solution)/shard_map/cloud/pallas_call | solution.py:293
  40.7 1.1 collective-permute-start.3
  41.8 2.1 %collective-permute-start.4 = (bf16[4,32,128]{2,1,0:T(8,128)(2,1)}, bf16[4,32,128]{2,1,0:T(8,128)(2,1)S(1)}, u32[]{:S(2)}, u32[]{:S(2)}) collective-permute-start(bf16[4,32,128]{2,1,0:T(8,128)(2,1)} %cloud.1.w0), channel_id=1, source_target_pairs={{0,128},{64,192},{128,0},{192,64},{1,129},{65,193},{129,1},{193,65... | collective-permute-start | bytes 98312 | tf_op jit(solution)/shard_map/ppermute | solution.py:317
  43.9 0.9 collective-permute-start.5
  45.1 1.4 %collective-permute-done.4.w2 = bf16[4,32,128]{2,1,0:T(8,128)(2,1)S(1)} collective-permute-done((bf16[4,32,128]{2,1,0:T(8,128)(2,1)}, bf16[4,32,128]{2,1,0:T(8,128)(2,1)S(1)}, u32[]{:S(2)}, u32[]{:S(2)}) %collective-permute-start.4) | collective-permute-done | bytes 32800 | tf_op jit(solution)/shard_map/ppermute | solution.py:317
  46.6 0.6 collective-permute-done.5.w3
  47.8 5.5 %reproject_weights.1.x_ref = bf16[64,9,4,128]{3,2,1,0:T(4,128)(2,1)} custom-call(s32[1]{0:T(128)} %bitcast.11.band_ref, bf16[4,32,128]{2,1,0:T(8,128)(2,1)} %cloud.1.w0, bf16[4,32,128]{2,1,0:T(8,128)(2,1)} %copy-done.6, bf16[4,32,128]{2,1,0:T(8,128)(2,1)} %copy-done.7, bf16[4,32,128]{2,1,0:T(8,128)(2,1)} %copy-done.8, f32[4,128]{1,0:T(4,128)} %broadcast_in_dim.11.id_ref, ...), custom_call_target="tpu_custom_call" | custom-call | flops 8000000000 | bytes 1000000 | tf_op jit(solution)/shard_map/reproject_weights/pallas_call | solution.py:321
  53.3 17.0 %all-to-all-done.first_ref = bf16[64,64,256]{2,1,0:T(8,128)(2,1)S(1)} async-done(((bf16[64,64,256]{2,1,0:T(8,128)(2,1)}), bf16[64,64,256]{2,1,0:T(8,128)(2,1)S(1)}, u32[]{:S(2)}, u32[]{:S(2)}) %all-to-all-start) | async-done | bytes 2097184 | tf_op jit(solution)/shard_map/all_to_all | solution.py:272
  70.3 24.5 %all_to_all.15.w_ref = bf16[64,9,4,128]{3,2,1,0:T(4,128)(2,1)S(1)} all-to-all(bf16[64,9,4,128]{3,2,1,0:T(4,128)(2,1)} %after.1), channel_id=1, replica_groups=mesh['band'=4,'tile'=64] {'tile'}, dimensions={0} | all-to-all | bytes 1179648 | tf_op jit(solution)/shard_map/all_to_all | solution.py:344
  94.9 10.4 %merge.1 = f32[64,4,128]{2,1,0:T(4,128)} custom-call(bf16[4096,256]{1,0:T(8,128)(2,1)} %bitcast.46, bf16[64,9,4,128]{3,2,1,0:T(4,128)(2,1)S(1)} %all_to_all.15.w_ref, bf16[128,256]{1,0:T(8,128)(2,1)} %constant.103.clone.double_ref), custom_call_target="tpu_custom_call" | custom-call | tf_op jit(solution)/shard_map/merge/pallas_call | solution.py:347
  105.3 6.3 %all-to-all-start.2 = ((f32[64,4,128]{2,1,0:T(4,128)}), f32[64,4,128]{2,1,0:T(4,128)S(1)}, u32[]{:S(2)}, u32[]{:S(2)}) async-start(f32[64,4,128]{2,1,0:T(4,128)} %merge.1), calls=%async_computation.2 | async-start | bytes 262144 | tf_op jit(solution)/shard_map/all_to_all | solution.py:360
  111.5 0.6 pad_add_fusion.tile_ref
  112.1 9.8 %all-to-all-done.2.g_ref = f32[64,4,128]{2,1,0:T(4,128)S(1)} async-done(((f32[64,4,128]{2,1,0:T(4,128)}), f32[64,4,128]{2,1,0:T(4,128)S(1)}, u32[]{:S(2)}, u32[]{:S(2)}) %all-to-all-start.2) | async-done | bytes 131104 | tf_op jit(solution)/shard_map/all_to_all | solution.py:360
  121.9 1.8 %smooth.1 = f32[32,4,128]{2,1,0:T(4,128)} custom-call(s32[2]{0:T(128)} %pad_add_fusion.tile_ref, f32[64,4,128]{2,1,0:T(4,128)S(1)} %all-to-all-done.2.g_ref), custom_call_target="tpu_custom_call" | custom-call | tf_op jit(solution)/shard_map/smooth/pallas_call | solution.py:363
  (38 shorter events, 2.3 us)
Async XLA Ops:
  5.7 13.4 %copy-start.1 = (bf16[16,4,4096]{2,1,0:T(4,128)(2,1)S(1)}, bf16[16,4,4096]{2,1,0:T(4,128)(2,1)}, u32[]{:S(2)}) copy-start(bf16[16,4,4096]{2,1,0:T(4,128)(2,1)} %param.13) | copy-start | bytes 1572868
  5.7 18.6 %copy-start.9 = (s32[16]{0:T(128)S(1)}, s32[16]{0:T(128)}, u32[]{:S(2)}) copy-start(s32[16]{0:T(128)} %param.15) | copy-start | bytes 196
  5.7 20.3 %copy-start.3 = (bf16[16,256]{1,0:T(8,128)(2,1)S(1)}, bf16[16,256]{1,0:T(8,128)(2,1)}, u32[]{:S(2)}) copy-start(bf16[16,256]{1,0:T(8,128)(2,1)} %param.19) | copy-start | bytes 24580
  5.7 21.1 %copy-start.2 = (bf16[2,256,256]{2,1,0:T(8,128)(2,1)S(1)}, bf16[2,256,256]{2,1,0:T(8,128)(2,1)}, u32[]{:S(2)}) copy-start(bf16[2,256,256]{2,1,0:T(8,128)(2,1)} %param.20) | copy-start | bytes 786436
  5.8 64.6 %all-to-all-start = ((bf16[64,64,256]{2,1,0:T(8,128)(2,1)}), bf16[64,64,256]{2,1,0:T(8,128)(2,1)S(1)}, u32[]{:S(2)}, u32[]{:S(2)}) async-start(bf16[64,64,256]{2,1,0:T(8,128)(2,1)} %reproject.1), calls=%async_computation | async-start | bytes 4194304 | tf_op jit(solution)/shard_map/all_to_all | solution.py:272
  19.1 7.9 %copy-start.4 = (s32[16,4]{0,1:T(4,128)S(1)}, s32[16,4]{0,1:T(4,128)}, u32[]{:S(2)}) copy-start(s32[16,4]{0,1:T(4,128)} %param.16) | copy-start | bytes 772
  19.1 10.0 %copy-start.5 = (bf16[256]{0:T(256)(128)(2,1)S(1)}, bf16[256]{0:T(256)(128)(2,1)}, u32[]{:S(2)}) copy-start(bf16[256]{0:T(256)(128)(2,1)} %param.21) | copy-start | bytes 1540
  19.4 8.5 %collective-permute-start = (bf16[4,4,4096]{2,1,0:T(4,128)(2,1)S(1)}, bf16[4,4,4096]{2,1,0:T(4,128)(2,1)S(1)}, u32[]{:S(2)}, u32[]{:S(2)}) collective-permute-start(bf16[4,4,4096]{2,1,0:T(4,128)(2,1)S(1)} %get-tuple-element.11), channel_id=1, source_target_pairs={{0,64},{64,128},{128,192},{192,0},{1,65},{65,129},{129,193},{193,1... | collective-permute-start | bytes 393224 | tf_op jit(solution)/shard_map/ppermute | solution.py:281
  20.7 8.4 %collective-permute-start.1 = (bf16[4,4,4096]{2,1,0:T(4,128)(2,1)S(1)}, bf16[4,4,4096]{2,1,0:T(4,128)(2,1)S(1)}, u32[]{:S(2)}, u32[]{:S(2)}) collective-permute-start(bf16[4,4,4096]{2,1,0:T(4,128)(2,1)S(1)} %get-tuple-element.10), channel_id=1, source_target_pairs={{0,128},{64,192},{128,0},{192,64},{1,129},{65,193},{129,1},{193,65... | collective-permute-start | bytes 393224 | tf_op jit(solution)/shard_map/ppermute | solution.py:281
  23.1 6.0 %collective-permute-start.2 = (bf16[4,4,4096]{2,1,0:T(4,128)(2,1)S(1)}, bf16[4,4,4096]{2,1,0:T(4,128)(2,1)S(1)}, u32[]{:S(2)}, u32[]{:S(2)}) collective-permute-start(bf16[4,4,4096]{2,1,0:T(4,128)(2,1)S(1)} %get-tuple-element.9), channel_id=1, source_target_pairs={{0,192},{64,0},{128,64},{192,128},{1,193},{65,1},{129,65},{193,129... | collective-permute-start | bytes 393224 | tf_op jit(solution)/shard_map/ppermute | solution.py:281
  40.7 4.5 %collective-permute-start.3 = (bf16[4,32,128]{2,1,0:T(8,128)(2,1)}, bf16[4,32,128]{2,1,0:T(8,128)(2,1)S(1)}, u32[]{:S(2)}, u32[]{:S(2)}) collective-permute-start(bf16[4,32,128]{2,1,0:T(8,128)(2,1)} %cloud.1.w0), channel_id=1, source_target_pairs={{0,64},{64,128},{128,192},{192,0},{1,65},{65,129},{129,193},{193,1... | collective-permute-start | bytes 98312 | tf_op jit(solution)/shard_map/ppermute | solution.py:317
  41.8 4.8 %collective-permute-start.4 = (bf16[4,32,128]{2,1,0:T(8,128)(2,1)}, bf16[4,32,128]{2,1,0:T(8,128)(2,1)S(1)}, u32[]{:S(2)}, u32[]{:S(2)}) collective-permute-start(bf16[4,32,128]{2,1,0:T(8,128)(2,1)} %cloud.1.w0), channel_id=1, source_target_pairs={{0,128},{64,192},{128,0},{192,64},{1,129},{65,193},{129,1},{193,65... | collective-permute-start | bytes 98312 | tf_op jit(solution)/shard_map/ppermute | solution.py:317
  43.9 3.3 %collective-permute-start.5 = (bf16[4,32,128]{2,1,0:T(8,128)(2,1)}, bf16[4,32,128]{2,1,0:T(8,128)(2,1)S(1)}, u32[]{:S(2)}, u32[]{:S(2)}) collective-permute-start(bf16[4,32,128]{2,1,0:T(8,128)(2,1)} %cloud.1.w0), channel_id=1, source_target_pairs={{0,192},{64,0},{128,64},{192,128},{1,193},{65,1},{129,65},{193,129... | collective-permute-start | bytes 98312 | tf_op jit(solution)/shard_map/ppermute | solution.py:317
  45.1 2.6 %copy-start.6 = (bf16[4,32,128]{2,1,0:T(8,128)(2,1)}, bf16[4,32,128]{2,1,0:T(8,128)(2,1)S(1)}, u32[]{:S(2)}) copy-start(bf16[4,32,128]{2,1,0:T(8,128)(2,1)S(1)} %collective-permute-done.3.w1) | copy-start | bytes 98308
  46.6 1.2 %copy-start.7 = (bf16[4,32,128]{2,1,0:T(8,128)(2,1)}, bf16[4,32,128]{2,1,0:T(8,128)(2,1)S(1)}, u32[]{:S(2)}) copy-start(bf16[4,32,128]{2,1,0:T(8,128)(2,1)S(1)} %collective-permute-done.4.w2) | copy-start | bytes 98308
  47.2 0.6 copy-start.8
  70.3 24.5 %copy-start = (bf16[64,64,256]{2,1,0:T(8,128)(2,1)}, bf16[64,64,256]{2,1,0:T(8,128)(2,1)S(1)}, u32[]{:S(2)}) copy-start(bf16[64,64,256]{2,1,0:T(8,128)(2,1)S(1)} %all-to-all-done.first_ref) | copy-start | bytes 6291460
  105.3 16.6 %all-to-all-start.2 = ((f32[64,4,128]{2,1,0:T(4,128)}), f32[64,4,128]{2,1,0:T(4,128)S(1)}, u32[]{:S(2)}, u32[]{:S(2)}) async-start(f32[64,4,128]{2,1,0:T(4,128)} %merge.1), calls=%async_computation.2 | async-start | bytes 262144 | tf_op jit(solution)/shard_map/all_to_all | solution.py:360

commit v9 on v7

--- a/solution.py
+++ b/solution.py
@@ -215,15 +215,16 @@
     def flux(d):
         return d / (1.0 + d * d)
 
+    bands = [g_ref[:, c, :] for c in range(4)]
+    for repeat in range(SMOOTH):
+        across = [jnp.where(closed, 0.0, flux(pltpu.roll(g, 127, 1) - g)) for g in bands]
+        down = [jnp.where(bottom, 0.0, flux(pltpu.roll(g, SIDE - 1, 0) - g)) for g in bands]
+        across = [a - pltpu.roll(a, 1, 1) for a in across]
+        down = [d - pltpu.roll(d, 1, 0) for d in down]
+        bands = [g + smooth_rate * (a + d) for g, a, d in zip(bands, across, down)]
     for c in range(4):
-        g = g_ref[:, c, :]
-        for repeat in range(SMOOTH):
-            across = jnp.where(closed, 0.0, flux(pltpu.roll(g, 127, 1) - g))
-            down = jnp.where(bottom, 0.0, flux(pltpu.roll(g, SIDE - 1, 0) - g))
-            g = g + smooth_rate * (
-                across - pltpu.roll(across, 1, 1) + (down - pltpu.roll(down, 1, 0))
-            )
-        scratch[c] = g
+        scratch[c] = bands[c]
+    for c in range(4):
         even = scratch[c, pl.ds(0, SIDE // 2, stride=2), :]
         odd = scratch[c, pl.ds(1, SIDE // 2, stride=2), :]
         out_ref[:, c, :] = jnp.where(lane[: SIDE // 2] < SIDE, even, pltpu.roll(odd, SIDE, 1))

time: 124 us -> 124 us (level)
  no operation moved by 1% of the time
where the time goes in v9:
time: 124 us
  Pallas kernels  34.4 us (28%)
  waiting for transfers between devices  30.4 us (25%)
  starting transfers between devices  28.6 us (23%)
  blocking collectives  24.5 us (20%)
  local copies, waits for them, and re-layouts  3.46 us (3%)
  other arithmetic  2.11 us (2%)
    all_to_all x1, blocking collectives, per_device(): lax.all_to_all(moved_weights, 'tile', split_axis=0, concat_axis=0)  24.5 us
    all_to_all x1, waiting for transfers between devices, per_device(): values = lax.all_to_all(moved, 'tile', split_axis=0, concat_axis=0)  17 us
    all_to_all x1, starting transfers between devices, per_device(): values = lax.all_to_all(moved, 'tile', split_axis=0, concat_axis=0)  13.3 us
    pallas_call x1, Pallas kernels, per_device(): pl.pallas_call(cloud_kernel, grid=(share, pixels // width), in_specs=[in_...  11 us
    pallas_call x1, Pallas kernels, per_device(): pl.pallas_call(merge_kernel, in_specs=[anywhere, in_vmem, in_vmem], out_s...  10.4 us
    all_to_all x1, waiting for transfers between devices, per_device(): field = lax.all_to_all(estimate, 'tile', split_axis=0, concat_axis=0)  9.76 us
    all_to_all x1, starting transfers between devices, per_device(): field = lax.all_to_all(estimate, 'tile', split_axis=0, concat_axis=0)  6.28 us
    pallas_call x1, Pallas kernels, reproject_call(): pl.pallas_call(reproject_kernel, grid=(steps,), in_specs=[scene_block, sc...  5.73 us
  transfers between devices with their start and end apart: 8, of which 6 were waited for; matrix products, arithmetic and copies ran while one was open for 4% of the time, Pallas kernels for 13%

profile of v9, /device:TPU:1, one launch (start us, length us, event | category | flops | bytes accessed | tf_op | source)
XLA Modules:
  0.0 123.7 jit_solution(1600275526839148201)
XLA Ops:
  0.0 5.7 %reproject.1 = bf16[64,64,256]{2,1,0:T(8,128)(2,1)} custom-call(bf16[16,128,128]{2,1,0:T(8,128)(2,1)} %bitcast.47, bf16[16,128,128]{2,1,0:T(8,128)(2,1)} %bitcast.49, bf16[16,128,128]{2,1,0:T(8,128)(2,1)} %bitcast.51, bf16[256,128]{1,0:T(8,128)(2,1)} %constant.101.clone.spread_ref), custom_call_target="tpu_custom_call" | custom-call | tf_op jit(solution)/shard_map/reproject/pallas_call | solution.py:79
  5.8 13.3 %all-to-all-start = ((bf16[64,64,256]{2,1,0:T(8,128)(2,1)}), bf16[64,64,256]{2,1,0:T(8,128)(2,1)S(1)}, u32[]{:S(2)}, u32[]{:S(2)}) async-start(bf16[64,64,256]{2,1,0:T(8,128)(2,1)} %reproject.1), calls=%async_computation | async-start | bytes 4194304 | tf_op jit(solution)/shard_map/all_to_all | solution.py:270
  19.4 1.3 %collective-permute-start = (bf16[4,4,4096]{2,1,0:T(4,128)(2,1)S(1)}, bf16[4,4,4096]{2,1,0:T(4,128)(2,1)S(1)}, u32[]{:S(2)}, u32[]{:S(2)}) collective-permute-start(bf16[4,4,4096]{2,1,0:T(4,128)(2,1)S(1)} %get-tuple-element.11), channel_id=1, source_target_pairs={{0,64},{64,128},{128,192},{192,0},{1,65},{65,129},{129,193},{193,1... | collective-permute-start | bytes 393224 | tf_op jit(solution)/shard_map/ppermute | solution.py:279
  20.7 2.5 %collective-permute-start.1 = (bf16[4,4,4096]{2,1,0:T(4,128)(2,1)S(1)}, bf16[4,4,4096]{2,1,0:T(4,128)(2,1)S(1)}, u32[]{:S(2)}, u32[]{:S(2)}) collective-permute-start(bf16[4,4,4096]{2,1,0:T(4,128)(2,1)S(1)} %get-tuple-element.10), channel_id=1, source_target_pairs={{0,128},{64,192},{128,0},{192,64},{1,129},{65,193},{129,1},{193,65... | collective-permute-start | bytes 393224 | tf_op jit(solution)/shard_map/ppermute | solution.py:279
  23.1 1.2 collective-permute-start.2
  24.4 0.8 fusion.1
  25.2 0.8 reshape.54.factor_ref
  26.1 0.7 copy.34
  27.1 0.7 multiply_bitcast_fusion.w_hidden_ref
  27.9 1.2 collective-permute-done.1.x2
  29.7 11.0 %cloud.1.w0 = bf16[4,32,128]{2,1,0:T(8,128)(2,1)} custom-call(bf16[4,4,4096]{2,1,0:T(4,128)(2,1)S(1)} %get-tuple-element.12.x0, bf16[4,4,4096]{2,1,0:T(4,128)(2,1)S(1)} %collective-permute-done.x1, bf16[4,4,4096]{2,1,0:T(4,128)(2,1)S(1)} %collective-permute-done.1.x2, bf16[4,4,4096]{2,1,0:T(4,128)(2,1)S(1)} %collective-permute-done.2.x3, ...), custom_call_target="tpu_custom_call" | custom-call | flops 12000000000 | bytes 1000000 | tf_op jit(solution)/shard_map/cloud/pallas_call | solution.py:291
  40.7 1.1 collective-permute-start.3
  41.8 2.1 %collective-permute-start.4 = (bf16[4,32,128]{2,1,0:T(8,128)(2,1)}, bf16[4,32,128]{2,1,0:T(8,128)(2,1)S(1)}, u32[]{:S(2)}, u32[]{:S(2)}) collective-permute-start(bf16[4,32,128]{2,1,0:T(8,128)(2,1)} %cloud.1.w0), channel_id=1, source_target_pairs={{0,128},{64,192},{128,0},{192,64},{1,129},{65,193},{129,1},{193,65... | collective-permute-start | bytes 98312 | tf_op jit(solution)/shard_map/ppermute | solution.py:315
  43.9 0.9 collective-permute-start.5
  45.1 1.4 %collective-permute-done.4.w2 = bf16[4,32,128]{2,1,0:T(8,128)(2,1)S(1)} collective-permute-done((bf16[4,32,128]{2,1,0:T(8,128)(2,1)}, bf16[4,32,128]{2,1,0:T(8,128)(2,1)S(1)}, u32[]{:S(2)}, u32[]{:S(2)}) %collective-permute-start.4) | collective-permute-done | bytes 32800 | tf_op jit(solution)/shard_map/ppermute | solution.py:315
  46.6 0.6 collective-permute-done.5.w3
  47.8 5.5 %reproject_weights.1.x_ref = bf16[64,9,4,128]{3,2,1,0:T(4,128)(2,1)} custom-call(s32[1]{0:T(128)} %bitcast.11.band_ref, bf16[4,32,128]{2,1,0:T(8,128)(2,1)} %cloud.1.w0, bf16[4,32,128]{2,1,0:T(8,128)(2,1)} %copy-done.6, bf16[4,32,128]{2,1,0:T(8,128)(2,1)} %copy-done.7, bf16[4,32,128]{2,1,0:T(8,128)(2,1)} %copy-done.8, f32[4,128]{1,0:T(4,128)} %broadcast_in_dim.11.id_ref, ...), custom_call_target="tpu_custom_call" | custom-call | flops 8000000000 | bytes 1000000 | tf_op jit(solution)/shard_map/reproject_weights/pallas_call | solution.py:319
  53.3 17.0 %all-to-all-done.first_ref = bf16[64,64,256]{2,1,0:T(8,128)(2,1)S(1)} async-done(((bf16[64,64,256]{2,1,0:T(8,128)(2,1)}), bf16[64,64,256]{2,1,0:T(8,128)(2,1)S(1)}, u32[]{:S(2)}, u32[]{:S(2)}) %all-to-all-start) | async-done | bytes 2097184 | tf_op jit(solution)/shard_map/all_to_all | solution.py:270
  70.3 24.5 %all_to_all.15.w_ref = bf16[64,9,4,128]{3,2,1,0:T(4,128)(2,1)S(1)} all-to-all(bf16[64,9,4,128]{3,2,1,0:T(4,128)(2,1)} %after.1), channel_id=1, replica_groups=mesh['band'=4,'tile'=64] {'tile'}, dimensions={0} | all-to-all | bytes 1179648 | tf_op jit(solution)/shard_map/all_to_all | solution.py:342
  94.9 10.4 %merge.1 = f32[64,4,128]{2,1,0:T(4,128)} custom-call(bf16[4096,256]{1,0:T(8,128)(2,1)} %bitcast.46, bf16[64,9,4,128]{3,2,1,0:T(4,128)(2,1)S(1)} %all_to_all.15.w_ref, bf16[128,256]{1,0:T(8,128)(2,1)} %constant.103.clone.double_ref), custom_call_target="tpu_custom_call" | custom-call | tf_op jit(solution)/shard_map/merge/pallas_call | solution.py:345
  105.3 6.3 %all-to-all-start.2 = ((f32[64,4,128]{2,1,0:T(4,128)}), f32[64,4,128]{2,1,0:T(4,128)S(1)}, u32[]{:S(2)}, u32[]{:S(2)}) async-start(f32[64,4,128]{2,1,0:T(4,128)} %merge.1), calls=%async_computation.2 | async-start | bytes 262144 | tf_op jit(solution)/shard_map/all_to_all | solution.py:358
  111.6 0.6 pad_add_fusion.tile_ref
  112.2 9.8 %all-to-all-done.2.g_ref = f32[64,4,128]{2,1,0:T(4,128)S(1)} async-done(((f32[64,4,128]{2,1,0:T(4,128)}), f32[64,4,128]{2,1,0:T(4,128)S(1)}, u32[]{:S(2)}, u32[]{:S(2)}) %all-to-all-start.2) | async-done | bytes 131104 | tf_op jit(solution)/shard_map/all_to_all | solution.py:358
  122.0 1.8 %smooth.1 = f32[32,4,128]{2,1,0:T(4,128)} custom-call(s32[2]{0:T(128)} %pad_add_fusion.tile_ref, f32[64,4,128]{2,1,0:T(4,128)S(1)} %all-to-all-done.2.g_ref), custom_call_target="tpu_custom_call" | custom-call | tf_op jit(solution)/shard_map/smooth/pallas_call | solution.py:361
  (38 shorter events, 2.3 us)
Async XLA Ops:
  5.7 13.4 %copy-start.1 = (bf16[16,4,4096]{2,1,0:T(4,128)(2,1)S(1)}, bf16[16,4,4096]{2,1,0:T(4,128)(2,1)}, u32[]{:S(2)}) copy-start(bf16[16,4,4096]{2,1,0:T(4,128)(2,1)} %param.13) | copy-start | bytes 1572868
  5.7 18.6 %copy-start.9 = (s32[16]{0:T(128)S(1)}, s32[16]{0:T(128)}, u32[]{:S(2)}) copy-start(s32[16]{0:T(128)} %param.15) | copy-start | bytes 196
  5.7 20.3 %copy-start.3 = (bf16[16,256]{1,0:T(8,128)(2,1)S(1)}, bf16[16,256]{1,0:T(8,128)(2,1)}, u32[]{:S(2)}) copy-start(bf16[16,256]{1,0:T(8,128)(2,1)} %param.19) | copy-start | bytes 24580
  5.7 21.1 %copy-start.2 = (bf16[2,256,256]{2,1,0:T(8,128)(2,1)S(1)}, bf16[2,256,256]{2,1,0:T(8,128)(2,1)}, u32[]{:S(2)}) copy-start(bf16[2,256,256]{2,1,0:T(8,128)(2,1)} %param.20) | copy-start | bytes 786436
  5.8 64.6 %all-to-all-start = ((bf16[64,64,256]{2,1,0:T(8,128)(2,1)}), bf16[64,64,256]{2,1,0:T(8,128)(2,1)S(1)}, u32[]{:S(2)}, u32[]{:S(2)}) async-start(bf16[64,64,256]{2,1,0:T(8,128)(2,1)} %reproject.1), calls=%async_computation | async-start | bytes 4194304 | tf_op jit(solution)/shard_map/all_to_all | solution.py:270
  19.1 7.9 %copy-start.4 = (s32[16,4]{0,1:T(4,128)S(1)}, s32[16,4]{0,1:T(4,128)}, u32[]{:S(2)}) copy-start(s32[16,4]{0,1:T(4,128)} %param.16) | copy-start | bytes 772
  19.1 10.0 %copy-start.5 = (bf16[256]{0:T(256)(128)(2,1)S(1)}, bf16[256]{0:T(256)(128)(2,1)}, u32[]{:S(2)}) copy-start(bf16[256]{0:T(256)(128)(2,1)} %param.21) | copy-start | bytes 1540
  19.4 8.5 %collective-permute-start = (bf16[4,4,4096]{2,1,0:T(4,128)(2,1)S(1)}, bf16[4,4,4096]{2,1,0:T(4,128)(2,1)S(1)}, u32[]{:S(2)}, u32[]{:S(2)}) collective-permute-start(bf16[4,4,4096]{2,1,0:T(4,128)(2,1)S(1)} %get-tuple-element.11), channel_id=1, source_target_pairs={{0,64},{64,128},{128,192},{192,0},{1,65},{65,129},{129,193},{193,1... | collective-permute-start | bytes 393224 | tf_op jit(solution)/shard_map/ppermute | solution.py:279
  20.7 8.4 %collective-permute-start.1 = (bf16[4,4,4096]{2,1,0:T(4,128)(2,1)S(1)}, bf16[4,4,4096]{2,1,0:T(4,128)(2,1)S(1)}, u32[]{:S(2)}, u32[]{:S(2)}) collective-permute-start(bf16[4,4,4096]{2,1,0:T(4,128)(2,1)S(1)} %get-tuple-element.10), channel_id=1, source_target_pairs={{0,128},{64,192},{128,0},{192,64},{1,129},{65,193},{129,1},{193,65... | collective-permute-start | bytes 393224 | tf_op jit(solution)/shard_map/ppermute | solution.py:279
  23.1 6.0 %collective-permute-start.2 = (bf16[4,4,4096]{2,1,0:T(4,128)(2,1)S(1)}, bf16[4,4,4096]{2,1,0:T(4,128)(2,1)S(1)}, u32[]{:S(2)}, u32[]{:S(2)}) collective-permute-start(bf16[4,4,4096]{2,1,0:T(4,128)(2,1)S(1)} %get-tuple-element.9), channel_id=1, source_target_pairs={{0,192},{64,0},{128,64},{192,128},{1,193},{65,1},{129,65},{193,129... | collective-permute-start | bytes 393224 | tf_op jit(solution)/shard_map/ppermute | solution.py:279
  40.7 4.5 %collective-permute-start.3 = (bf16[4,32,128]{2,1,0:T(8,128)(2,1)}, bf16[4,32,128]{2,1,0:T(8,128)(2,1)S(1)}, u32[]{:S(2)}, u32[]{:S(2)}) collective-permute-start(bf16[4,32,128]{2,1,0:T(8,128)(2,1)} %cloud.1.w0), channel_id=1, source_target_pairs={{0,64},{64,128},{128,192},{192,0},{1,65},{65,129},{129,193},{193,1... | collective-permute-start | bytes 98312 | tf_op jit(solution)/shard_map/ppermute | solution.py:315
  41.8 4.8 %collective-permute-start.4 = (bf16[4,32,128]{2,1,0:T(8,128)(2,1)}, bf16[4,32,128]{2,1,0:T(8,128)(2,1)S(1)}, u32[]{:S(2)}, u32[]{:S(2)}) collective-permute-start(bf16[4,32,128]{2,1,0:T(8,128)(2,1)} %cloud.1.w0), channel_id=1, source_target_pairs={{0,128},{64,192},{128,0},{192,64},{1,129},{65,193},{129,1},{193,65... | collective-permute-start | bytes 98312 | tf_op jit(solution)/shard_map/ppermute | solution.py:315
  43.9 3.3 %collective-permute-start.5 = (bf16[4,32,128]{2,1,0:T(8,128)(2,1)}, bf16[4,32,128]{2,1,0:T(8,128)(2,1)S(1)}, u32[]{:S(2)}, u32[]{:S(2)}) collective-permute-start(bf16[4,32,128]{2,1,0:T(8,128)(2,1)} %cloud.1.w0), channel_id=1, source_target_pairs={{0,192},{64,0},{128,64},{192,128},{1,193},{65,1},{129,65},{193,129... | collective-permute-start | bytes 98312 | tf_op jit(solution)/shard_map/ppermute | solution.py:315
  45.1 2.6 %copy-start.6 = (bf16[4,32,128]{2,1,0:T(8,128)(2,1)}, bf16[4,32,128]{2,1,0:T(8,128)(2,1)S(1)}, u32[]{:S(2)}) copy-start(bf16[4,32,128]{2,1,0:T(8,128)(2,1)S(1)} %collective-permute-done.3.w1) | copy-start | bytes 98308
  46.6 1.2 %copy-start.7 = (bf16[4,32,128]{2,1,0:T(8,128)(2,1)}, bf16[4,32,128]{2,1,0:T(8,128)(2,1)S(1)}, u32[]{:S(2)}) copy-start(bf16[4,32,128]{2,1,0:T(8,128)(2,1)S(1)} %collective-permute-done.4.w2) | copy-start | bytes 98308
  47.2 0.6 copy-start.8
  70.3 24.5 %copy-start = (bf16[64,64,256]{2,1,0:T(8,128)(2,1)}, bf16[64,64,256]{2,1,0:T(8,128)(2,1)S(1)}, u32[]{:S(2)}) copy-start(bf16[64,64,256]{2,1,0:T(8,128)(2,1)S(1)} %all-to-all-done.first_ref) | copy-start | bytes 6291460
  105.3 16.6 %all-to-all-start.2 = ((f32[64,4,128]{2,1,0:T(4,128)}), f32[64,4,128]{2,1,0:T(4,128)S(1)}, u32[]{:S(2)}, u32[]{:S(2)}) async-start(f32[64,4,128]{2,1,0:T(4,128)} %merge.1), calls=%async_computation.2 | async-start | bytes 262144 | tf_op jit(solution)/shard_map/all_to_all | solution.py:358
